TPU v7x, 128 devices: a whole 4x4x4 slice. The times are simulated.
128 devices in a mesh: nodes: 128 (over x, y, z, core).
Axes of the slice: x: 4, y: 4, z: 4, core: 2. Of those that a mesh axis runs over, the one named last changes fastest.
Arguments:
- features: bfloat16 [2097152, 128], P('nodes'), may hold values from -6 to 6
- nbr_owner: int32 [4096, 32], P('nodes'), may hold values from 0 to 127, all different within a row; in each aligned block of 32 rows (0 to 31, 32 to 63, ...) at most 16 rows name the same one
- nbr_local: int32 [4096, 32], P('nodes'), may hold values from 0 to 16383
- ppr_weight: float32 [4096, 32], P('nodes'), may hold values from 0.01 to 0.1
- labels: int32 [4096], P('nodes'), may hold values from 0 to 171
- w_first: bfloat16 [128, 512], replicated, may hold values from -0.5 to 0.5
- w_second: bfloat16 [512, 512], replicated, may hold values from -0.25 to 0.25
- w_third: bfloat16 [512, 172], replicated, may hold values from -0.25 to 0.25
Outputs:
- loss: float32 [], replicated
- seed_logits: float32 [4096, 172], P('nodes')
- grad_first: float32 [128, 512], replicated
- grad_second: float32 [512, 512], replicated
- grad_third: float32 [512, 172], replicated
Inputs may be any that keep to these rules, and one draw needn't show every extreme that they name: `nbr_owner`: each row names 32 different devices; among the rows of one device no device is named by more than 16 rows.
All inputs are finite; a program needn't handle non-finite values.
Results may differ from a plain program's by a relative error of at most 0.01.
The roundings to bfloat16 on the way count: a program that leaves them out, or rounds other values in their place, can miss the bound.
Values may be sent and summed in bfloat16 or wider, within the bound.
No kernel may reach another device: no remote copies, remote signals or barrier semaphores. Data moves between devices by JAX's collectives and lax.ppermute only.
A program may use at most 64 MiB of HBM per device.

v0:
```python
import jax
import jax.numpy as jnp
from jax import lax
from jax.sharding import Mesh
from jax.sharding import PartitionSpec as P

NODES = ("nodes_0", "nodes_1", "nodes_2", "nodes_3")


def split_up(shard, dim, count):
    lengths = shard.shape
    parts = shard.reshape(*lengths[:dim], count, lengths[dim] // count, *lengths[dim + 1 :])
    return jnp.moveaxis(parts, dim, 0)


def summed_on_arrival(shard, axis, dim):
    count = lax.axis_size(axis)
    parts = lax.all_to_all(split_up(shard, dim, count), axis, 0, 0, tiled=True)
    return jnp.sum(parts, axis=0)


def sum_in_two_steps(shard, axes, dim):
    far, near = axes
    parts = split_up(shard, dim, lax.axis_size(far))
    nearer = summed_on_arrival(parts, near, dim + 1)
    arrived = lax.all_to_all(nearer, far, split_axis=0, concat_axis=0, tiled=True)
    return arrived.sum(axis=0)


def padded_to(lines, count):
    spare = -len(lines) % count
    return jnp.pad(lines, [(0, spare)] + [(0, 0)] * (lines.ndim - 1))


def copy_for_each(shard, axis):
    count = lax.axis_size(axis)
    return lax.all_to_all(
        jnp.broadcast_to(shard[None], (count, *shard.shape)), axis, 0, 0, tiled=True
    )


def joined_along(parts, dim):
    parts = jnp.moveaxis(parts, 0, dim)
    lengths = parts.shape
    return parts.reshape(*lengths[:dim], lengths[dim] * lengths[dim + 1], *lengths[dim + 2 :])


def gather_axes(shard, axes, dim):
    far, near = axes
    first = copy_for_each(shard, far)
    parts = jnp.swapaxes(copy_for_each(first, near), 0, 1)
    return joined_along(parts.reshape(-1, *shard.shape), dim)


def nested_sum(shard, axes):
    own = sum_in_two_steps(
        padded_to(shard, lax.axis_size(axes[0]) * lax.axis_size(axes[1])), axes, 0
    )
    whole = gather_axes(own, axes, 0)
    return whole[: len(shard)].reshape(shard.shape)


def in_one(arrays, axis):
    ends = [0]
    for a in arrays:
        ends.append(ends[-1] + a.size)
    running = nested_sum(jnp.concatenate([a.ravel() for a in arrays]), axis)
    return tuple((running[b:e].reshape(a.shape) for a, b, e in zip(arrays, ends, ends[1:])))


def forward_rows(row_block, w_first, w_second, w_third):
    first_pre = jnp.dot(row_block, w_first, preferred_element_type=jnp.float32)
    first_act = jnp.maximum(first_pre, 0.0).astype(jnp.bfloat16)
    second_pre = jnp.dot(first_act, w_second, preferred_element_type=jnp.float32)
    second_act = jnp.maximum(second_pre, 0.0).astype(jnp.bfloat16)
    row_logits = jnp.dot(second_act, w_third, preferred_element_type=jnp.float32)
    return ((first_pre > 0, first_act, second_pre > 0, second_act), row_logits)


def backward_rows(row_block, cached, logit_grads, w_second, w_third):
    first_mask, first_act, second_mask, second_act = cached
    grad_third = jnp.dot(second_act.T, logit_grads, preferred_element_type=jnp.float32)
    second_grad = jnp.where(
        second_mask, jnp.dot(logit_grads, w_third.T, preferred_element_type=jnp.float32), 0.0
    ).astype(jnp.bfloat16)
    grad_second = jnp.dot(first_act.T, second_grad, preferred_element_type=jnp.float32)
    first_grad = jnp.where(
        first_mask, jnp.dot(second_grad, w_second.T, preferred_element_type=jnp.float32), 0.0
    ).astype(jnp.bfloat16)
    grad_first = jnp.dot(row_block.T, first_grad, preferred_element_type=jnp.float32)
    return (grad_first, grad_second, grad_third)


def seed_loss(seed_logits, labels, total_seeds):
    classes = seed_logits.shape[1]
    highest = jnp.max(seed_logits, axis=1, keepdims=True)
    log_total = jnp.log(jnp.sum(jnp.exp(seed_logits - highest), axis=1, keepdims=True)) + highest
    onehot = (labels[:, None] == jnp.arange(classes, dtype=jnp.int32)[None, :]).astype(jnp.float32)
    loss_terms = jnp.sum(log_total[:, 0] - jnp.sum(onehot * seed_logits, axis=1))
    logit_grad = (jnp.exp(seed_logits - log_total) - onehot) / total_seeds
    return (loss_terms, logit_grad)


def on_device(features, nbr_owner, nbr_local, ppr_weight, labels, w_first, w_second, w_third):
    groups = lax.axis_size(NODES)
    seed_count, neighbours = nbr_owner.shape
    capacity = min(seed_count, 2 * seed_count * neighbours // groups)
    classes = w_third.shape[1]
    total_seeds = float(seed_count * groups)
    owner_table = jnp.arange(groups, dtype=jnp.int32)
    per_seed = jnp.sum(
        (nbr_owner[:, :, None] == owner_table[None, None, :]).astype(jnp.int32), axis=1
    )
    earlier = jnp.cumsum(per_seed, axis=0) - per_seed
    position = jnp.take_along_axis(earlier, nbr_owner, axis=1)
    slot_index = (nbr_owner * capacity + position).reshape(-1)
    outgoing = jnp.zeros((groups * capacity,), jnp.int32).at[slot_index].set(nbr_local.reshape(-1))
    requested = lax.all_to_all(
        outgoing.reshape(groups, capacity), NODES, split_axis=0, concat_axis=0, tiled=True
    )
    local_rows = jnp.take(features, requested.reshape(-1), axis=0)
    arrived = lax.all_to_all(
        local_rows.reshape(groups, capacity, local_rows.shape[1]),
        NODES,
        split_axis=0,
        concat_axis=0,
        tiled=True,
    )
    row_block = jnp.take(
        arrived.reshape(groups * capacity, local_rows.shape[1]), slot_index, axis=0
    )
    cached, row_logits = forward_rows(row_block, w_first, w_second, w_third)
    seed_logits = jnp.sum(
        ppr_weight[:, :, None] * row_logits.reshape(seed_count, neighbours, classes), axis=1
    )
    loss_terms, logit_grad = seed_loss(seed_logits, labels, total_seeds)
    weighted = (
        (ppr_weight[:, :, None] * logit_grad[:, None, :]).astype(jnp.bfloat16).reshape(-1, classes)
    )
    gradients = backward_rows(row_block, cached, weighted, w_second, w_third)
    loss_sum, grad_first, grad_second, grad_third = in_one(
        (loss_terms, gradients[0], gradients[1], gradients[2]),
        (("nodes_0", "nodes_1", "nodes_2"), "nodes_3"),
    )
    return (loss_sum / total_seeds, seed_logits, grad_first, grad_second, grad_third)


def solution(mesh):
    finer = Mesh(mesh.devices.reshape(4, 4, 4, 2), ("nodes_0", "nodes_1", "nodes_2", "nodes_3"))
    placed = (
        P(NODES, None),
        P(NODES, None),
        P(NODES, None),
        P(NODES, None),
        P(NODES),
        P(),
        P(),
        P(),
    )
    return jax.shard_map(
        on_device,
        mesh=finer,
        in_specs=placed,
        out_specs=(P(), P(NODES, None), P(), P(), P()),
        check_vma=False,
    )
```

profile of v0, /device:TPU:1, one launch (start us, length us, event | category | flops | bytes accessed | tf_op | source)
XLA Modules:
  0.0 164.7 jit_solution(17635588731153683011)
XLA Ops:
  0.6 1.0 convert_reduce_fusion
  1.6 0.7 bitcast_or_fusion
  2.5 6.8 %gather_fusion.2 = s32[1024]{0:T(1024)S(1)} fusion(s32[32,128]{1,0:T(8,128)S(1)} %sub.33, s32[1024]{0:T(1024)S(1)} %reshape.232), kind=kCustom, calls=%fused_computation.2 | custom fusion | bytes 16384 | tf_op jit(solution)/shard_map/jit(take_along_axis)/gather | solution.py:115
  9.6 4.3 %scatter_custom_fusion = s32[2048]{0:T(1024)S(1)} fusion(s32[1024]{0:T(1024)S(1)} %bitcast.48, s32[1024]{0:T(1024)S(1)} %reshape.242, s32[]{:T(128)} %constant.39.clone.1), kind=kCustom, calls=%fused_computation.37 | custom fusion | bytes 8196 | tf_op jit(solution)/shard_map/scatter | solution.py:117
  14.0 20.7 %all_to_all.39 = s32[128,1,16]{2,1,0:T(1,128)S(1)} all-to-all(s32[128,1,16]{2,1,0:T(1,128)S(1)} %bitcast.46), channel_id=1, replica_groups=mesh['nodes_0'=4,'nodes_1'=4,'nodes_2'=4,'nodes_3'=2] {'nodes_0','nodes_..., dimensions={0} | all-to-all | bytes 16384 | tf_op jit(solution)/shard_map/all_to_all | solution.py:118
  34.6 0.5 broadcast.143
  35.2 0.8 reduce.4
  36.1 8.3 %gather_fusion = bf16[2048,128]{1,0:T(8,128)(2,1)S(1)} fusion(bf16[16384,128]{1,0:T(8,128)(2,1)} %param.8, s32[2048]{0:T(1024)S(1)} %broadcast_clamp_fusion), kind=kCustom, calls=%fused_computation | custom fusion | bytes 1056768 | tf_op jit(solution)/shard_map/jit(_take)/gather | solution.py:121
  44.5 1.1 broadcast_select_fusion
  45.6 4.7 %all-to-all-start.1 = ((bf16[128,16,128]{2,1,0:T(8,128)(2,1)}), bf16[128,16,128]{2,1,0:T(8,128)(2,1)S(1)}, u32[]{:S(2)}, u32[]{:S(2)}) async-start(bf16[128,16,128]{2,1,0:T(8,128)(2,1)} %broadcast_select_fusion), calls=%async_computation.1 | async-start | bytes 1048576 | tf_op jit(solution)/shard_map/all_to_all | solution.py:122
  50.5 13.5 %all-to-all-done.1 = bf16[128,16,128]{2,1,0:T(8,128)(2,1)S(1)} async-done(((bf16[128,16,128]{2,1,0:T(8,128)(2,1)}), bf16[128,16,128]{2,1,0:T(8,128)(2,1)S(1)}, u32[]{:S(2)}, u32[]{:S(2)}) %all-to-all-start.1) | async-done | bytes 524320 | tf_op jit(solution)/shard_map/all_to_all | solution.py:122
  64.1 3.2 %gather_fusion.1 = bf16[1024,128]{1,0:T(8,128)(2,1)S(1)} fusion(bf16[2048,128]{1,0:T(8,128)(2,1)S(1)} %bitcast.38, s32[1024]{0:T(1024)S(1)} %broadcast_clamp_fusion.1), kind=kCustom, calls=%fused_computation.1 | custom fusion | bytes 528384 | tf_op jit(solution)/shard_map/jit(_take)/gather | solution.py:129
  67.3 0.5 fusion.7
  67.8 0.7 fusion.4
  68.5 0.6 copy-done.1
  69.1 0.5 multiply_reduce_fusion
  69.8 0.2 select_reduce_fusion
  70.0 0.6 subtract_reduce_fusion
  70.7 0.2 fusion.2
  70.9 0.5 fusion.5
  71.4 0.4 select_convert_fusion.1
  71.8 1.0 copy-done.4
  72.8 0.6 copy-done.2
  73.3 1.7 %convolution_bitcast_fusion = f32[64,4,8,128]{3,2,1,0:T(8,128)} fusion(bf16[1024,512]{1,0:T(8,128)(2,1)S(1)} %select_convert_fusion.1, f32[1024,512]{1,0:T(8,128)S(1)} %copy-done.2), kind=kOutput, calls=%fused_computation.9 | convolution fusion | flops 537919488 | bytes 4194304 | tf_op jit(solution)/shard_map/dot_general | solution.py:86
  75.1 2.8 %fusion.1 = f32[16,4,8,128]{3,2,1,0:T(8,128)} fusion(f32[1024,512]{1,0:T(8,128)S(1)} %copy-done.3, bf16[1024,512]{1,0:T(8,128)(2,1)} %copy-done.4, bf16[512,512]{1,0:T(8,128)(2,1)S(1)} %copy-done, bf16[1024,128]{1,0:T(8,128)(2,1)S(1)} %gather_fusion.1, pred[1024]{0:T(1024)(128)(4,1)S(1)} %compare_and_fusion.1), kind=kOutput, calls=%fused_computation.10 | convolution fusion | flops 672792576 | bytes 4195328 | tf_op jit(solution)/shard_map/dot_general | solution.py:90
  77.9 1.2 reshape.212
  79.1 1.5 copy.37
  80.7 10.8 %concatenate.3 = f32[415745]{0:T(1024)S(1)} concatenate(f32[1]{0:T(128)} %bitcast.8, f32[65536]{0:T(1024)S(1)} %bitcast.44, f32[262144]{0:T(1024)S(1)} %bitcast.41, f32[88064]{0:T(1024)} %reshape.212), dimensions={0} | concatenate | bytes 3325960 | tf_op jit(solution)/shard_map/concatenate | solution.py:67
  91.5 1.3 pad.4
  92.8 3.1 %reshape_reshape.6 = f32[64,2,3249]{2,1,0:T(2,128)S(1)} reshape(f32[415872]{0:T(1024)} %pad.4) | data formatting | bytes 3326976 | tf_op jit(solution)/shard_map/reshape;reshape | solution.py:12
  96.1 6.1 %all_to_all.40 = f32[2,64,3249]{2,1,0:T(8,128)S(1)} all-to-all(f32[2,64,3249]{2,1,0:T(8,128)S(1)} %copy.30), channel_id=1, replica_groups=mesh['nodes_0'=4,'nodes_1'=4,'nodes_2'=4,'nodes_3'=2] {'nodes_3'}, dimensions={0} | all-to-all | bytes 3326976 | tf_op jit(solution)/shard_map/all_to_all | solution.py:18
  102.1 0.2 reduce_sum.68
  102.3 0.6 all_to_all.29
  102.9 19.5 %all_to_all.41 = f32[64,1,3249]{2,1,0:T(1,128)S(1)} all-to-all(f32[64,1,3249]{2,1,0:T(1,128)S(1)} %all_to_all.29), channel_id=1, replica_groups=mesh['nodes_0'=4,'nodes_1'=4,'nodes_2'=4,'nodes_3'=2] {'nodes_0','nodes_..., dimensions={0} | all-to-all | bytes 1663488 | tf_op jit(solution)/shard_map/all_to_all | solution.py:26
  122.3 0.5 reduce_sum.69
  122.9 0.4 broadcast_in_dim.66
  123.3 19.1 %all_to_all.42 = f32[64,1,3249]{2,1,0:T(1,128)S(1)} all-to-all(f32[64,1,3249]{2,1,0:T(1,128)S(1)} %broadcast_in_dim.66), channel_id=1, replica_groups=mesh['nodes_0'=4,'nodes_1'=4,'nodes_2'=4,'nodes_3'=2] {'nodes_0','nodes_..., dimensions={0} | all-to-all | bytes 1663488 | tf_op jit(solution)/shard_map/all_to_all | solution.py:37
  142.6 8.1 %all_to_all.43 = f32[2,64,3249]{2,1,0:T(8,128)S(1)} all-to-all(f32[2,64,3249]{2,1,0:T(8,128)S(1)} %broadcast_in_dim.68), channel_id=1, replica_groups=mesh['nodes_0'=4,'nodes_1'=4,'nodes_2'=4,'nodes_3'=2] {'nodes_3'}, dimensions={0} | all-to-all | bytes 3326976 | tf_op jit(solution)/shard_map/all_to_all | solution.py:37
  150.6 1.3 copy.31
  151.9 2.5 %reshape_reshape.7 = f32[415872]{0:T(1024)} reshape(f32[64,2,3249]{2,1,0:T(2,128)S(1)} %copy.31) | data formatting | bytes 3326976 | tf_op jit(solution)/shard_map/reshape;reshape | solution.py:45
  154.5 1.6 slice.29
  156.0 1.1 slice.30
  157.2 1.1 slice.28
  158.3 1.2 slice.27
  159.5 1.1 reshape.214
  160.6 0.7 reshape.215
  161.3 0.9 copy.32
  162.2 0.7 reshape.213
  (48 shorter events, 1.4 us)
Async XLA Ops:
  0.6 67.1 %copy-start = (bf16[512,512]{1,0:T(8,128)(2,1)S(1)}, bf16[512,512]{1,0:T(8,128)(2,1)}, u32[]{:S(2)}) copy-start(bf16[512,512]{1,0:T(8,128)(2,1)} %param.14) | copy-start | bytes 1572868
  2.5 6.9 %copy-start.9 = (s32[32,32]{1,0:T(8,128)S(1)}, s32[32,32]{1,0:T(8,128)}, u32[]{:S(2)}) copy-start(s32[32,32]{1,0:T(8,128)} %param.9) | copy-start | bytes 12292
  2.5 7.0 %copy-start.12 = (s32[32,32]{1,0:T(8,128)S(1)}, s32[32,32]{1,0:T(8,128)}, u32[]{:S(2)}) copy-start(s32[32,32]{1,0:T(8,128)} %param.10) | copy-start | bytes 12292
  44.5 6.0 %copy-start.11 = (f32[32,32]{1,0:T(8,128)S(1)}, f32[32,32]{1,0:T(8,128)}, u32[]{:S(2)}) copy-start(f32[32,32]{1,0:T(8,128)} %param.11) | copy-start | bytes 12292
  44.5 22.8 %copy-start.10 = (bf16[128,512]{1,0:T(8,128)(2,1)S(1)}, bf16[128,512]{1,0:T(8,128)(2,1)}, u32[]{:S(2)}) copy-start(bf16[128,512]{1,0:T(8,128)(2,1)} %param.13) | copy-start | bytes 393220
  45.6 18.4 %all-to-all-start.1 = ((bf16[128,16,128]{2,1,0:T(8,128)(2,1)}), bf16[128,16,128]{2,1,0:T(8,128)(2,1)S(1)}, u32[]{:S(2)}, u32[]{:S(2)}) async-start(bf16[128,16,128]{2,1,0:T(8,128)(2,1)} %broadcast_select_fusion), calls=%async_computation.1 | async-start | bytes 1048576 | tf_op jit(solution)/shard_map/all_to_all | solution.py:122
  67.8 1.4 copy-start.1
  67.8 1.3 copy-start.5
  69.1 0.7 copy-start.13
  69.6 2.2 %copy-start.7 = (f32[32,172]{1,0:T(8,128)}, f32[32,172]{1,0:T(8,128)S(1)}, u32[]{:S(2)}) copy-start(f32[32,172]{1,0:T(8,128)S(1)} %multiply_reduce_fusion) | copy-start | bytes 66052
  69.8 1.6 copy-start.6
  71.4 2.0 %copy-start.2 = (f32[1024,512]{1,0:T(8,128)S(1)}, f32[1024,512]{1,0:T(8,128)}, u32[]{:S(2)}) copy-start(f32[1024,512]{1,0:T(8,128)} %copy-done.1) | copy-start | bytes 6291460
  71.8 1.0 copy-start.4
  73.3 1.7 %copy-start.3 = (f32[1024,512]{1,0:T(8,128)S(1)}, f32[1024,512]{1,0:T(8,128)}, u32[]{:S(2)}) copy-start(f32[1024,512]{1,0:T(8,128)} %copy-done.1) | copy-start | bytes 6291460
  77.9 2.7 %copy-start.8 = (f32[16,4,8,128]{3,2,1,0:T(8,128)S(1)}, f32[16,4,8,128]{3,2,1,0:T(8,128)}, u32[]{:S(2)}) copy-start(f32[16,4,8,128]{3,2,1,0:T(8,128)} %fusion.1) | copy-start | bytes 786436
where the time goes:
time: 166 us; the launch traced here: 165 us
  blocking collectives  73.3 us (44%)
  local copies, waits for them, and re-layouts  57.6 us (35%)
  waiting for transfers between devices  13.5 us (8%)
  matrix products  7.11 us (4%)
  other arithmetic  5.7 us (3%)
  starting transfers between devices  4.74 us (3%)
  between operations  2.76 us (2%)
    all_to_all x2, blocking collectives, copy_for_each(): lax.all_to_all(jnp.broadcast_to(shard[None], (count, *shard.shape)), axis...  27.1 us
    all_to_all x1, blocking collectives, on_device(): lax.all_to_all(outgoing.reshape(groups, capacity), NODES, split_axis=0, c...  20.7 us
    all_to_all x1, blocking collectives, sum_in_two_steps(): lax.all_to_all(nearer, far, split_axis=0, concat_axis=0, tiled=True)  19.5 us
    all_to_all x1, waiting for transfers between devices, on_device(): lax.all_to_all(local_rows.reshape(groups, capacity, local_rows.shape[1]),...  13.5 us
    concatenate x1, local copies, waits for them, and re-layouts, in_one(): running = nested_sum(jnp.concatenate([a.ravel() for a in arrays]), axis)  10.8 us
    gather x1, local copies, waits for them, and re-layouts, on_device(): local_rows = jnp.take(features, requested.reshape(-1), axis=0)  8.32 us
    gather x3, local copies, waits for them, and re-layouts, on_device(): position = jnp.take_along_axis(earlier, nbr_owner, axis=1)  6.93 us
    all_to_all x1, blocking collectives, summed_on_arrival(): parts = lax.all_to_all(split_up(shard, dim, count), axis, 0, 0, tiled=True)  6.06 us
  transfers between devices with their start and end apart: 1, of which 1 were waited for; matrix products, arithmetic and copies ran while one was open for 0% of the time, Pallas kernels for 0%

commit v1 on v0

v1 whole, which is shorter than its diff:
```python
import functools

import jax
import jax.numpy as jnp
from jax import lax
from jax.experimental import pallas as pl
from jax.experimental.pallas import tpu as pltpu
from jax.sharding import Mesh
from jax.sharding import PartitionSpec as P

CHIPS = ("nodes_0", "nodes_1", "nodes_2")
CORE = "nodes_3"
NODES = (*CHIPS, CORE)
LANES = 128
VMEM_BYTES = 48 << 20

bf16 = jnp.bfloat16
f32 = jnp.float32
i32 = jnp.int32


def iota(shape, dim):
    return lax.broadcasted_iota(i32, shape, dim)


def dot(a, b, over=((1,), (0,))):
    return lax.dot_general(a, b, (over, ((), ())), preferred_element_type=f32)


def whole(shape=None):
    return pl.BlockSpec(memory_space=pltpu.VMEM)


def call(body, outs, ins, scratch=()):
    return pl.pallas_call(
        body,
        out_shape=outs,
        in_specs=ins,
        out_specs=jax.tree.map(lambda _: whole(), outs),
        scratch_shapes=scratch,
        compiler_params=pltpu.CompilerParams(vmem_limit_bytes=VMEM_BYTES),
    )


def request_body(capacity, owner_ref, local_ref, table_ref, earlier_ref):
    owner, local = owner_ref[...], local_ref[...]
    seeds, neighbours = owner.shape
    groups = table_ref.shape[0]
    lane = iota((seeds, groups), 1)
    named = jnp.zeros((seeds, groups), f32)
    wanted = jnp.zeros((seeds, groups), i32)
    for k in range(neighbours):
        hit = owner[:, k : k + 1] == lane
        named = jnp.where(hit, 1.0, named)
        wanted = jnp.where(hit, local[:, k : k + 1], wanted)
    before = (iota((seeds, seeds), 1) < iota((seeds, seeds), 0)).astype(f32)
    earlier = dot(before.astype(bf16), named.astype(bf16))
    earlier_ref[...] = earlier
    place = jnp.where(named > 0, earlier.astype(i32), -1)
    slot = iota((capacity, groups), 0)
    table = jnp.zeros((capacity, groups), i32)
    for s in range(seeds):
        table = jnp.where(place[s : s + 1, :] == slot, wanted[s : s + 1, :], table)
    spare = jnp.zeros((LANES - capacity, groups), i32)
    table_ref[...] = jnp.concatenate([table, spare], axis=0).T


def widen_body(rows_ref, wide_ref):
    wide_ref[...] = rows_ref[...].astype(f32)


def widen(features):
    rows, width = features.shape
    block = 2048
    return pl.pallas_call(
        widen_body,
        grid=(rows // block,),
        out_shape=jax.ShapeDtypeStruct((rows, width), f32),
        in_specs=[pl.BlockSpec((block, width), lambda i: (i, 0))],
        out_specs=pl.BlockSpec((block, width), lambda i: (i, 0)),
        compiler_params=pltpu.CompilerParams(vmem_limit_bytes=VMEM_BYTES),
    )(features)


def pick_body(capacity, owner_t_ref, earlier_ref, pick_ref):
    neighbours, seeds = owner_t_ref.shape
    groups = earlier_ref.shape[1]
    owner_t = owner_t_ref[...]
    lane = iota((neighbours, groups), 1)
    slots = iota((neighbours, groups * capacity), 1)
    for s in range(seeds):
        owner = owner_t[:, s : s + 1]
        place = jnp.sum(jnp.where(owner == lane, earlier_ref[s : s + 1, :], 0.0), axis=1, keepdims=True)
        slot = owner * capacity + place.astype(i32)
        pick_ref[s * neighbours : (s + 1) * neighbours, :] = jnp.where(slots == slot, 1.0, 0.0).astype(bf16)


def serve_body(capacity, asked_ref, wide_ref, rows_ref, stage_ref):
    def one(source, carry):
        base = pl.multiple_of(source * capacity, capacity)
        for p in range(capacity):
            stage_ref[pl.ds(base + p, 1), :] = wide_ref[pl.ds(asked_ref[source, p], 1), :]
        rows_ref[pl.ds(base, capacity), :] = stage_ref[pl.ds(base, capacity), :].astype(bf16)
        return carry

    lax.fori_loop(0, asked_ref.shape[0], one, 0)


def step_body(
    total_seeds,
    core_ref,
    pick_ref,
    arrived_ref,
    weight_ref,
    labels_ref,
    first_ref,
    second_ref,
    third_t_ref,
    logits_ref,
    keep_ref,
    send_ref,
    grads_ref,
):
    seeds, classes = logits_ref.shape
    rows = pick_ref.shape[0]
    neighbours = rows // seeds
    features, hidden = first_ref.shape
    half = keep_ref.shape[0]
    x = dot(pick_ref[...], arrived_ref[...]).astype(bf16)
    first_pre = dot(x, first_ref[...])
    first_act = jnp.maximum(first_pre, 0.0).astype(bf16)
    second_pre = dot(first_act, second_ref[...])
    second_act = jnp.maximum(second_pre, 0.0).astype(bf16)
    row_logits = dot(second_act, third_t_ref[...], ((1,), (1,)))
    weight = weight_ref[...]
    scaled = (weight * row_logits).reshape(seeds, neighbours, classes)
    logits = jnp.sum(scaled, axis=1)
    logits_ref[...] = logits
    highest = jnp.max(logits, axis=1, keepdims=True)
    log_total = jnp.log(jnp.sum(jnp.exp(logits - highest), axis=1, keepdims=True)) + highest
    onehot = jnp.where(labels_ref[...] == iota((seeds, classes), 1), 1.0, 0.0)
    terms = log_total - jnp.sum(onehot * logits, axis=1, keepdims=True)
    logit_grad = (jnp.exp(logits - log_total) - onehot) / total_seeds
    spread = jnp.broadcast_to(logit_grad[:, None, :], (seeds, neighbours, classes)).reshape(rows, classes)
    weighted = (weight * spread).astype(bf16)
    end_first = features
    end_second = end_first + hidden
    end_third = end_second + classes
    grads_ref[end_second:end_third, :] = dot(weighted, second_act, ((0,), (0,)))
    second_grad = jnp.where(second_pre > 0, dot(weighted, third_t_ref[...]), 0.0).astype(bf16)
    grads_ref[end_first:end_second, :] = dot(first_act, second_grad, ((0,), (0,)))
    first_grad = jnp.where(first_pre > 0, dot(second_grad, second_ref[...], ((1,), (1,))), 0.0).astype(bf16)
    grads_ref[:end_first, :] = dot(x, first_grad, ((0,), (0,)))
    grads_ref[end_third:, :] = jnp.zeros((2 * half - end_third, hidden), f32)
    diagonal = iota((seeds, LANES), 0) == iota((seeds, LANES), 1)
    grads_ref[end_third : end_third + 1, :LANES] = jnp.sum(jnp.where(diagonal, terms, 0.0), axis=0, keepdims=True)
    core = core_ref[0]
    keep_ref[...] = grads_ref[pl.ds(pl.multiple_of(core * half, half), half), :]
    send_ref[...] = grads_ref[pl.ds(pl.multiple_of((1 - core) * half, half), half), :].astype(bf16)


def finish_body(total_seeds, core_ref, own_ref, other_ref, loss_ref, first_ref, second_ref, third_t_ref):
    half = own_ref.shape[0]
    end_first = first_ref.shape[0]
    end_second = end_first + second_ref.shape[0]
    end_third = end_second + third_t_ref.shape[0]

    def write(low_ref, high_ref):
        first_ref[...] = low_ref[:end_first, :].astype(f32)
        second_ref[: half - end_first, :] = low_ref[end_first:, :].astype(f32)
        second_ref[half - end_first :, :] = high_ref[: end_second - half, :].astype(f32)
        third_t_ref[...] = high_ref[end_second - half : end_third - half, :].astype(f32)
        terms = high_ref[end_third - half : end_third - half + 1, :LANES].astype(f32)
        loss_ref[...] = jnp.sum(terms, axis=1, keepdims=True) / total_seeds

    @pl.when(core_ref[0] == 0)
    def _():
        write(own_ref, other_ref)

    @pl.when(core_ref[0] != 0)
    def _():
        write(other_ref, own_ref)


def everywhere(parts, axis):
    return lax.all_to_all(parts, axis, 0, 0, tiled=True)


def on_device(features, nbr_owner, nbr_local, ppr_weight, labels, w_first, w_second, w_third):
    groups = lax.axis_size(NODES)
    chips = lax.axis_size(CHIPS)
    seeds, neighbours = nbr_owner.shape
    capacity = min(seeds, 2 * seeds * neighbours // groups)
    width, hidden = w_first.shape
    classes = w_third.shape[1]
    total_seeds = float(seeds * groups)
    vmem = whole()
    smem = pl.BlockSpec(memory_space=pltpu.SMEM)
    shape = jax.ShapeDtypeStruct
    core = lax.axis_index(CORE).astype(i32).reshape(1)
    swap = [(0, 1), (1, 0)]

    table, earlier = call(
        functools.partial(request_body, capacity),
        (shape((groups, LANES), i32), shape((seeds, groups), f32)),
        [vmem, vmem],
    )(nbr_owner, nbr_local)
    asked = everywhere(table.reshape(groups, 1, LANES), NODES).reshape(groups, LANES)
    wide = widen(features)
    (pick,) = call(
        functools.partial(pick_body, capacity),
        (shape((seeds * neighbours, groups * capacity), bf16),),
        [vmem, vmem],
    )(nbr_owner.T, earlier)
    (served,) = call(
        functools.partial(serve_body, capacity),
        (shape((groups * capacity, width), bf16),),
        [smem, vmem],
        [pltpu.VMEM((groups * capacity, width), f32)],
    )(asked, wide)
    arrived = everywhere(served.reshape(groups, capacity, width), NODES).reshape(groups * capacity, width)

    tile = 8
    half = chips * tile * -(-(width + hidden + classes + 1) // (2 * chips * tile))
    seed_logits, keep, send = call(
        functools.partial(step_body, total_seeds),
        (shape((seeds, classes), f32), shape((half, hidden), f32), shape((half, hidden), bf16)),
        [smem] + [vmem] * 7,
        [pltpu.VMEM((2 * half, hidden), f32)],
    )(
        core,
        pick,
        arrived,
        ppr_weight.reshape(-1, 1),
        labels.reshape(-1, 1),
        w_first,
        w_second,
        w_third.T,
    )
    near = lax.ppermute(send, CORE, swap)
    parts = (keep + near.astype(f32)).astype(bf16).reshape(chips, half // chips, hidden)
    mine = jnp.sum(everywhere(parts, CHIPS).astype(f32), axis=0).astype(bf16)
    own = everywhere(jnp.broadcast_to(mine[None], parts.shape), CHIPS).reshape(half, hidden)
    other = lax.ppermute(own, CORE, swap)
    loss, grad_first, grad_second, grad_third_t = call(
        functools.partial(finish_body, total_seeds),
        (
            shape((1, 1), f32),
            shape((width, hidden), f32),
            shape((hidden, hidden), f32),
            shape((classes, hidden), f32),
        ),
        [smem, vmem, vmem],
    )(core, own, other)
    return (loss.reshape(()), seed_logits, grad_first, grad_second, grad_third_t.T)


def solution(mesh):
    finer = Mesh(mesh.devices.reshape(4, 4, 4, 2), NODES)
    placed = (
        P(NODES, None),
        P(NODES, None),
        P(NODES, None),
        P(NODES, None),
        P(NODES),
        P(),
        P(),
        P(),
    )
    return jax.shard_map(
        on_device,
        mesh=finer,
        in_specs=placed,
        out_specs=(P(), P(NODES, None), P(), P(), P()),
        check_vma=False,
    )
```

time: 166 us -> 103 us (0.62)
  local copies, waits for them, and re-layouts: 57.6 us -> 6.33 us
  blocking collectives: 73.3 us -> 32.5 us
  Pallas kernels: 0 us -> 29.8 us
  starting transfers between devices: 4.74 us -> 23.2 us
  matrix products: 7.11 us -> 0 us
  other arithmetic: 5.7 us -> 0.3 us
  waiting for transfers between devices: 13.5 us -> 10.1 us
  between operations: 2.76 us -> 0.73 us
    all_to_all x5 -> x2, blocking collectives: 73.3 us -> 32.5 us  [everywhere(): return lax.all_to_all(parts, axis, 0, 0, tiled=True)]
    pallas_call x0 -> x6, Pallas kernels: none -> 29.8 us  [the longest x1 9.29 us: on_device(): call(functools.partial(step_body, total_seeds), (shape((seeds, classes),...]
    gather x5 -> x0, local copies, waits for them, and re-layouts: 18.5 us -> none  [the longest x1 8.32 us: on_device(): local_rows = jnp.take(features, requested.reshape(-1), axis=0)]
    all_to_all x1 -> x2, starting transfers between devices: 4.74 us -> 18.8 us  [everywhere(): return lax.all_to_all(parts, axis, 0, 0, tiled=True)]
    concatenate x1 -> x0, local copies, waits for them, and re-layouts: 10.8 us -> none  [in_one(): running = nested_sum(jnp.concatenate([a.ravel() for a in arrays]), axis)]
    dot_general x7 -> x0, matrix products: 7.11 us -> none  [the longest x1 2.85 us: backward_rows(): jnp.dot(row_block.T, first_grad, preferred_element_type=jnp.float32)]
    all_to_all x1 -> x2, waiting for transfers between devices: 13.5 us -> 7.01 us  [everywhere(): return lax.all_to_all(parts, axis, 0, 0, tiled=True)]
    another operation x2 -> x0, local copies, waits for them, and re-layouts: 5.63 us -> none  [the longest x1 3.1 us: split_up(): shard.reshape(*lengths[:dim], count, lengths[dim] // count, *lengths[dim...]
  transfers between devices with their start and end apart: 1 -> 4, of which waited for: 1 -> 4; matrix products, arithmetic and copies ran while one was open for 0% -> 1% of each run, Pallas kernels for 0% -> 11%
where the time goes in v1:
time: 103 us
  blocking collectives  32.5 us (32%)
  Pallas kernels  29.8 us (29%)
  starting transfers between devices  23.2 us (23%)
  waiting for transfers between devices  10.1 us (10%)
  local copies, waits for them, and re-layouts  6.33 us (6%)
    all_to_all x2, blocking collectives, everywhere(): return lax.all_to_all(parts, axis, 0, 0, tiled=True)  32.5 us
    all_to_all x2, starting transfers between devices, everywhere(): return lax.all_to_all(parts, axis, 0, 0, tiled=True)  18.8 us
    pallas_call x1, Pallas kernels, on_device(): call(functools.partial(step_body, total_seeds), (shape((seeds, classes),...  9.29 us
    all_to_all x2, waiting for transfers between devices, everywhere(): return lax.all_to_all(parts, axis, 0, 0, tiled=True)  7.01 us
    pallas_call x1, Pallas kernels, on_device(): call(functools.partial(serve_body, capacity), (shape((groups * capacity,...  6.85 us
    pallas_call x1, Pallas kernels, on_device(): call(functools.partial(pick_body, capacity), (shape((seeds * neighbours,...  6.39 us
    unnamed x21, local copies, waits for them, and re-layouts  5.67 us
    pallas_call x1, Pallas kernels, widen(): pl.pallas_call(widen_body, grid=(rows // block,), out_shape=jax.ShapeDtyp...  4.67 us
  transfers between devices with their start and end apart: 4, of which 4 were waited for; matrix products, arithmetic and copies ran while one was open for 1% of the time, Pallas kernels for 11%

profile of v1, /device:TPU:1, one launch (start us, length us, event | category | flops | bytes accessed | tf_op | source)
XLA Modules:
  0.0 102.9 jit_solution(7686543480480458577)
XLA Ops:
  0.6 0.0 copy-start.5
  0.6 0.7 copy-done.5
  1.4 0.0 copy-start.7
  1.4 0.7 copy-done.7
  2.1 1.2 %shard_map.119 = (s32[128,128]{1,0:T(8,128)}, f32[32,128]{1,0:T(8,128)S(1)}) custom-call(s32[32,32]{1,0:T(8,128)S(1)} %copy-done.5, s32[32,32]{1,0:T(8,128)S(1)} %copy-done.7), custom_call_target="tpu_custom_call" | custom-call | tf_op jit(solution)/shard_map/pallas_call | solution.py:203
  3.3 11.5 %all-to-all-start = ((s32[128,1,128]{2,1,0:T(1,128)}), s32[128,1,128]{2,1,0:T(1,128)S(1)}, u32[]{:S(2)}, u32[]{:S(2)}) async-start(s32[128,1,128]{2,1,0:T(1,128)} %bitcast.3), calls=%async_computation | async-start | bytes 131072 | tf_op jit(solution)/shard_map/all_to_all | solution.py:186
  14.8 0.0 copy-start.1
  14.8 2.2 %copy-done.1 = bf16[16384,128]{1,0:T(8,128)(2,1)S(1)} copy-done((bf16[16384,128]{1,0:T(8,128)(2,1)S(1)}, bf16[16384,128]{1,0:T(8,128)(2,1)}, u32[]{:S(2)}) %copy-start.1) | copy-done | bytes 4194328
  17.0 4.7 %shard_map.121.wide_ref = f32[16384,128]{1,0:T(8,128)} custom-call(bf16[16384,128]{1,0:T(8,128)(2,1)S(1)} %copy-done.1), custom_call_target="tpu_custom_call" | custom-call | tf_op jit(solution)/shard_map/pallas_call | solution.py:75
  21.6 2.4 %all-to-all-done = s32[128,1,128]{2,1,0:T(1,128)S(1)} async-done(((s32[128,1,128]{2,1,0:T(1,128)}), s32[128,1,128]{2,1,0:T(1,128)S(1)}, u32[]{:S(2)}, u32[]{:S(2)}) %all-to-all-start) | async-done | bytes 65568 | tf_op jit(solution)/shard_map/all_to_all | solution.py:186
  24.1 0.0 copy-start.6
  24.1 0.0 copy-start.8
  24.1 0.0 copy-start.9
  24.1 6.9 %shard_map.122 = bf16[2048,128]{1,0:T(8,128)(2,1)} custom-call(s32[128,128]{1,0:T(8,128)S(1)} %bitcast.18, f32[16384,128]{1,0:T(8,128)} %shard_map.121.wide_ref), custom_call_target="tpu_custom_call" | custom-call | tf_op jit(solution)/shard_map/pallas_call | solution.py:215
  30.9 0.0 copy-start.2
  30.9 0.0 copy-start.3
  30.9 0.0 copy-start.4
  30.9 7.3 %all-to-all-start.1 = ((bf16[128,16,128]{2,1,0:T(8,128)(2,1)}), bf16[128,16,128]{2,1,0:T(8,128)(2,1)S(1)}, u32[]{:S(2)}, u32[]{:S(2)}) async-start(bf16[128,16,128]{2,1,0:T(8,128)(2,1)} %bitcast.5), calls=%async_computation.1 | async-start | bytes 1048576 | tf_op jit(solution)/shard_map/all_to_all | solution.py:186
  38.3 0.0 copy-done.6
  38.3 0.1 copy.18
  38.4 0.0 copy-done.8
  38.4 0.5 reshape.51.weight_ref
  38.9 0.0 copy-done.9
  38.9 0.1 copy.21.labels_ref
  39.0 6.4 %shard_map.120.pick_ref = bf16[1024,2048]{1,0:T(8,128)(2,1)S(1)} custom-call(s32[32,32]{1,0:T(8,128)S(1)} %bitcast.20, f32[32,128]{1,0:T(8,128)S(1)} %get-tuple-element.14.earlier_ref), custom_call_target="tpu_custom_call" | custom-call | tf_op jit(solution)/shard_map/pallas_call | solution.py:210
  45.4 0.0 copy-start
  45.4 2.0 %copy-done = bf16[1024,2048]{1,0:T(8,128)(2,1)} copy-done((bf16[1024,2048]{1,0:T(8,128)(2,1)}, bf16[1024,2048]{1,0:T(8,128)(2,1)S(1)}, u32[]{:S(2)}) %copy-start) | copy-done | bytes 4194328
  47.4 4.6 %all-to-all-done.1 = bf16[128,16,128]{2,1,0:T(8,128)(2,1)S(1)} async-done(((bf16[128,16,128]{2,1,0:T(8,128)(2,1)}), bf16[128,16,128]{2,1,0:T(8,128)(2,1)S(1)}, u32[]{:S(2)}, u32[]{:S(2)}) %all-to-all-start.1) | async-done | bytes 524320 | tf_op jit(solution)/shard_map/all_to_all | solution.py:186
  52.0 0.0 copy-done.2
  52.0 0.0 copy-done.3
  52.0 0.0 copy-done.4
  52.0 9.3 %shard_map.123 = (f32[32,172]{1,0:T(8,128)}, f32[512,512]{1,0:T(8,128)S(1)}, bf16[512,512]{1,0:T(8,128)(2,1)S(1)}) custom-call(s32[1]{0:T(128)} %bitcast.core_ref, bf16[1024,2048]{1,0:T(8,128)(2,1)} %copy-done, bf16[2048,128]{1,0:T(8,128)(2,1)S(1)} %bitcast.15, f32[1024,1]{1,0:T(8,128)S(1)} %reshape.51.weight_ref, s32[32,1]{1,0:T(8,128)S(1)} %copy.21.labels_ref, ...), custom_call_target="tpu_custom_call" | custom-call | tf_op jit(solution)/shard_map/pallas_call | solution.py:225
  61.3 1.2 %collective-permute-start = (bf16[512,512]{1,0:T(8,128)(2,1)S(1)}, bf16[512,512]{1,0:T(8,128)(2,1)S(1)}, u32[]{:S(2)}, u32[]{:S(2)}) collective-permute-start(bf16[512,512]{1,0:T(8,128)(2,1)S(1)} %get-tuple-element.17), channel_id=1, source_target_pairs={{0,1},{1,0},{2,3},{3,2},{4,5},{5,4},{6,7},{7,6},{8,9},{9,8},{10,11... | collective-permute-start | bytes 1572872 | tf_op jit(solution)/shard_map/ppermute | solution.py:240
  62.4 1.5 %collective-permute-done = bf16[512,512]{1,0:T(8,128)(2,1)S(1)} collective-permute-done((bf16[512,512]{1,0:T(8,128)(2,1)S(1)}, bf16[512,512]{1,0:T(8,128)(2,1)S(1)}, u32[]{:S(2)}, u32[]{:S(2)}) %collective-permute-start) | collective-permute-done | bytes 524320 | tf_op jit(solution)/shard_map/ppermute | solution.py:240
  64.0 0.2 fusion
  64.2 17.0 %all_to_all.20 = bf16[64,8,512]{2,1,0:T(8,128)(2,1)S(1)} all-to-all(bf16[64,8,512]{2,1,0:T(8,128)(2,1)S(1)} %fusion), channel_id=1, replica_groups=mesh['nodes_0'=4,'nodes_1'=4,'nodes_2'=4,'nodes_3'=2] {'nodes_0','nodes_..., dimensions={0} | all-to-all | bytes 1048576 | tf_op jit(solution)/shard_map/all_to_all | solution.py:186
  81.1 0.1 reduce_sum.12
  81.3 15.5 %all_to_all.21 = bf16[64,8,512]{2,1,0:T(8,128)(2,1)S(1)} all-to-all(bf16[64,8,512]{2,1,0:T(8,128)(2,1)S(1)} %broadcast_in_dim.2), channel_id=1, replica_groups=mesh['nodes_0'=4,'nodes_1'=4,'nodes_2'=4,'nodes_3'=2] {'nodes_0','nodes_..., dimensions={0} | all-to-all | bytes 1048576 | tf_op jit(solution)/shard_map/all_to_all | solution.py:186
  96.8 3.2 %collective-permute-start.1 = (bf16[512,512]{1,0:T(8,128)(2,1)S(1)}, bf16[512,512]{1,0:T(8,128)(2,1)S(1)}, u32[]{:S(2)}, u32[]{:S(2)}) collective-permute-start(bf16[512,512]{1,0:T(8,128)(2,1)S(1)} %bitcast.16), channel_id=1, source_target_pairs={{0,1},{1,0},{2,3},{3,2},{4,5},{5,4},{6,7},{7,6},{8,9},{9,8},{10,11... | collective-permute-start | bytes 1572872 | tf_op jit(solution)/shard_map/ppermute | solution.py:244
  100.0 1.5 %collective-permute-done.1.other_ref = bf16[512,512]{1,0:T(8,128)(2,1)S(1)} collective-permute-done((bf16[512,512]{1,0:T(8,128)(2,1)S(1)}, bf16[512,512]{1,0:T(8,128)(2,1)S(1)}, u32[]{:S(2)}, u32[]{:S(2)}) %collective-permute-start.1) | collective-permute-done | bytes 524320 | tf_op jit(solution)/shard_map/ppermute | solution.py:244
  101.5 1.3 %shard_map.124 = (f32[1,1]{1,0:T(1,128)}, f32[128,512]{1,0:T(8,128)}, f32[512,512]{1,0:T(8,128)}, f32[172,512]{1,0:T(8,128)}) custom-call(s32[1]{0:T(128)} %bitcast.core_ref, bf16[512,512]{1,0:T(8,128)(2,1)S(1)} %bitcast.17, bf16[512,512]{1,0:T(8,128)(2,1)S(1)} %collective-permute-done.1.other_ref), custom_call_target="tpu_custom_call" | custom-call | tf_op jit(solution)/shard_map/pallas_call | solution.py:245
  (1 shorter events, 0.0 us)
Async XLA Ops:
  0.6 0.7 copy-start.5
  1.4 0.7 copy-start.7
  3.3 20.8 %all-to-all-start = ((s32[128,1,128]{2,1,0:T(1,128)}), s32[128,1,128]{2,1,0:T(1,128)S(1)}, u32[]{:S(2)}, u32[]{:S(2)}) async-start(s32[128,1,128]{2,1,0:T(1,128)} %bitcast.3), calls=%async_computation | async-start | bytes 131072 | tf_op jit(solution)/shard_map/all_to_all | solution.py:186
  14.8 2.2 %copy-start.1 = (bf16[16384,128]{1,0:T(8,128)(2,1)S(1)}, bf16[16384,128]{1,0:T(8,128)(2,1)}, u32[]{:S(2)}) copy-start(bf16[16384,128]{1,0:T(8,128)(2,1)} %rows_ref.1) | copy-start | bytes 12582916
  24.1 14.2 %copy-start.6 = (s32[32,32]{1,0:T(8,128)S(1)}, s32[32,32]{1,0:T(8,128)}, u32[]{:S(2)}) copy-start(s32[32,32]{1,0:T(8,128)} %owner_ref.1) | copy-start | bytes 12292
  24.1 14.3 %copy-start.8 = (f32[32,32]{1,0:T(8,128)S(1)}, f32[32,32]{1,0:T(8,128)}, u32[]{:S(2)}) copy-start(f32[32,32]{1,0:T(8,128)} %param.11) | copy-start | bytes 12292
  24.1 14.8 %copy-start.9 = (s32[32]{0:T(128)S(1)}, s32[32]{0:T(128)}, u32[]{:S(2)}) copy-start(s32[32]{0:T(128)} %param.12) | copy-start | bytes 388
  30.9 21.0 %copy-start.2 = (bf16[512,512]{1,0:T(8,128)(2,1)S(1)}, bf16[512,512]{1,0:T(8,128)(2,1)}, u32[]{:S(2)}) copy-start(bf16[512,512]{1,0:T(8,128)(2,1)} %second_ref.1) | copy-start | bytes 1572868
  30.9 21.0 %copy-start.3 = (bf16[512,172]{0,1:T(8,128)(2,1)S(1)}, bf16[512,172]{0,1:T(8,128)(2,1)}, u32[]{:S(2)}) copy-start(bf16[512,172]{0,1:T(8,128)(2,1)} %param.15) | copy-start | bytes 528388
  30.9 21.0 %copy-start.4 = (bf16[128,512]{1,0:T(8,128)(2,1)S(1)}, bf16[128,512]{1,0:T(8,128)(2,1)}, u32[]{:S(2)}) copy-start(bf16[128,512]{1,0:T(8,128)(2,1)} %first_ref.1) | copy-start | bytes 393220
  30.9 21.0 %all-to-all-start.1 = ((bf16[128,16,128]{2,1,0:T(8,128)(2,1)}), bf16[128,16,128]{2,1,0:T(8,128)(2,1)S(1)}, u32[]{:S(2)}, u32[]{:S(2)}) async-start(bf16[128,16,128]{2,1,0:T(8,128)(2,1)} %bitcast.5), calls=%async_computation.1 | async-start | bytes 1048576 | tf_op jit(solution)/shard_map/all_to_all | solution.py:186
  45.4 2.0 %copy-start = (bf16[1024,2048]{1,0:T(8,128)(2,1)}, bf16[1024,2048]{1,0:T(8,128)(2,1)S(1)}, u32[]{:S(2)}) copy-start(bf16[1024,2048]{1,0:T(8,128)(2,1)S(1)} %shard_map.120.pick_ref) | copy-start | bytes 12582916
  61.3 2.7 %collective-permute-start = (bf16[512,512]{1,0:T(8,128)(2,1)S(1)}, bf16[512,512]{1,0:T(8,128)(2,1)S(1)}, u32[]{:S(2)}, u32[]{:S(2)}) collective-permute-start(bf16[512,512]{1,0:T(8,128)(2,1)S(1)} %get-tuple-element.17), channel_id=1, source_target_pairs={{0,1},{1,0},{2,3},{3,2},{4,5},{5,4},{6,7},{7,6},{8,9},{9,8},{10,11... | collective-permute-start | bytes 1572872 | tf_op jit(solution)/shard_map/ppermute | solution.py:240
  96.8 4.8 %collective-permute-start.1 = (bf16[512,512]{1,0:T(8,128)(2,1)S(1)}, bf16[512,512]{1,0:T(8,128)(2,1)S(1)}, u32[]{:S(2)}, u32[]{:S(2)}) collective-permute-start(bf16[512,512]{1,0:T(8,128)(2,1)S(1)} %bitcast.16), channel_id=1, source_target_pairs={{0,1},{1,0},{2,3},{3,2},{4,5},{5,4},{6,7},{7,6},{8,9},{9,8},{10,11... | collective-permute-start | bytes 1572872 | tf_op jit(solution)/shard_map/ppermute | solution.py:244

commit v2 on v1

v2 whole, which is shorter than its diff:
```python
import functools

import jax
import jax.numpy as jnp
from jax import lax
from jax.experimental import pallas as pl
from jax.experimental.pallas import tpu as pltpu
from jax.sharding import Mesh
from jax.sharding import PartitionSpec as P

CHIPS = ("nodes_0", "nodes_1", "nodes_2")
CORE = "nodes_3"
NODES = (*CHIPS, CORE)
LANES = 128

bf16 = jnp.bfloat16
f32 = jnp.float32
i32 = jnp.int32


def iota(shape, dim):
    return lax.broadcasted_iota(i32, shape, dim)


def dot(a, b, over=((1,), (0,))):
    return lax.dot_general(a, b, (over, ((), ())), preferred_element_type=f32)


VMEM = pl.BlockSpec(memory_space=pltpu.VMEM)
SMEM = pl.BlockSpec(memory_space=pltpu.SMEM)
FAR = pl.BlockSpec(memory_space=pltpu.HBM)


def call(body, outs, ins, scratch=(), megabytes=8, where=VMEM):
    return pl.pallas_call(
        body,
        out_shape=outs,
        in_specs=ins,
        out_specs=jax.tree.map(lambda _: where, outs),
        scratch_shapes=scratch,
        compiler_params=pltpu.CompilerParams(vmem_limit_bytes=megabytes << 20),
    )


def places(capacity, groups, owner, local=None):
    seeds, neighbours = owner.shape
    lane = iota((seeds, groups), 1)
    named = jnp.zeros((seeds, groups), f32)
    wanted = jnp.zeros((seeds, groups), i32)
    for k in range(neighbours):
        hit = owner[:, k : k + 1] == lane
        named = jnp.where(hit, 1.0, named)
        if local is not None:
            wanted = jnp.where(hit, local[:, k : k + 1], wanted)
    before = (iota((seeds, seeds), 1) < iota((seeds, seeds), 0)).astype(f32)
    earlier = dot(before.astype(bf16), named.astype(bf16)).astype(i32)
    return named > 0, earlier, wanted


def request_body(capacity, owner_hbm, local_hbm, table_ref, owner_ref, local_ref, arrivals):
    copies = [
        pltpu.make_async_copy(owner_hbm, owner_ref, arrivals.at[0]),
        pltpu.make_async_copy(local_hbm, local_ref, arrivals.at[1]),
    ]
    for copy in copies:
        copy.start()
    for copy in copies:
        copy.wait()
    groups = table_ref.shape[0]
    seeds = owner_ref.shape[0]
    named, earlier, wanted = places(capacity, groups, owner_ref[...], local_ref[...])
    place = jnp.where(named, earlier, -1)
    slot = iota((capacity, groups), 0)
    table = jnp.zeros((capacity, groups), i32)
    for s in range(seeds):
        table = jnp.where(place[s : s + 1, :] == slot, wanted[s : s + 1, :], table)
    spare = jnp.zeros((LANES - capacity, groups), i32)
    table_ref[...] = jnp.concatenate([table, spare], axis=0).T


def coded_slots(slot):
    return ((128 + (slot & 127)) * (1 << (slot >> 7))).astype(f32)


def hold_body(pairs_hbm, held_ref, arrival):
    copy = pltpu.make_async_copy(pairs_hbm.at[pl.ds(0, held_ref.shape[0])], held_ref, arrival)
    copy.start()
    copy.wait()


def spread_body(capacity, groups, owner_ref, weight_ref, codes_ref, weights_ref):
    seeds, neighbours = owner_ref.shape
    _, earlier, _ = places(capacity, groups, owner_ref[...])
    code_of = coded_slots(iota((seeds, groups), 1) * capacity + earlier)
    owner_t = owner_ref[...].T
    weight_t = weight_ref[...].T
    lane = iota((neighbours, groups), 1)
    for s in range(seeds):
        rows = pl.ds(s * neighbours, neighbours)
        own = jnp.where(owner_t[:, s : s + 1] == lane, code_of[s : s + 1, :], 0.0)
        code = jnp.sum(own, axis=1, keepdims=True)
        codes_ref[rows, :] = jnp.broadcast_to(code, (neighbours, codes_ref.shape[1])).astype(bf16)
        weights_ref[rows, :] = jnp.broadcast_to(weight_t[:, s : s + 1], (neighbours, weights_ref.shape[1]))


def serve_body(
    capacity, asked_ref, held_ref, pairs_hbm, rows_hbm, rows_ref, pairs_ref, stage_ref, turned_ref, index_ref, arrivals, leaving
):
    held, pairs = held_ref.shape[0], pairs_ref.shape[0]
    rest = pl.ds(held, pairs - held)
    near = pltpu.make_async_copy(held_ref, pairs_ref.at[pl.ds(0, held)], arrivals.at[0])
    far = pltpu.make_async_copy(pairs_hbm.at[rest], pairs_ref.at[rest], arrivals.at[1])
    far.start()
    near.start()
    asked = asked_ref[...].T[:capacity, :]
    turned_ref[...] = asked >> 1
    odd = (asked & 1).astype(f32)
    index = pltpu.make_async_copy(turned_ref, index_ref, arrivals.at[2])
    index.start()
    index.wait()
    near.wait()
    far.wait()
    sources = asked.shape[1]
    together = stage_ref.shape[0] // (2 * capacity)

    def some(step, carry):
        for j in range(together):
            source = step * together + j
            low = 2 * j * capacity
            for p in range(capacity):
                stage_ref[low + 2 * p : low + 2 * p + 2, :] = pairs_ref[index_ref[p, source]].astype(f32)
            later = jnp.broadcast_to(pltpu.roll(odd, sources - source, 1)[:, 0:1], (capacity, stage_ref.shape[1])) > 0
            first = stage_ref[pl.ds(low, capacity, stride=2), :]
            second = stage_ref[pl.ds(low + 1, capacity, stride=2), :]
            base = pl.multiple_of(source * capacity, capacity)
            rows_ref[pl.ds(base, capacity), :] = jnp.where(later, second, first).astype(bf16)
        out(step).start()
        return carry

    def out(step):
        size = together * capacity
        span = pl.ds(pl.multiple_of(step * size, size), size)
        return pltpu.make_async_copy(rows_ref.at[span], rows_hbm.at[span], leaving.at[step])

    def last(step, carry):
        out(step).wait()
        return carry

    lax.fori_loop(0, sources // together, some, 0)
    lax.fori_loop(0, sources // together, last, 0)


def step_body(
    total_seeds,
    blocks,
    core_ref,
    codes_ref,
    arrived_ref,
    weights_ref,
    labels_ref,
    first_hbm,
    second_hbm,
    third_t_hbm,
    logits_ref,
    keep_ref,
    send_ref,
    grads_ref,
    first_ref,
    second_ref,
    third_t_ref,
    arrivals,
):
    sources = (first_hbm, second_hbm, third_t_hbm)
    targets = (first_ref, second_ref, third_t_ref)
    copies = [pltpu.make_async_copy(a, b, arrivals.at[i]) for i, (a, b) in enumerate(zip(sources, targets))]
    for copy in copies:
        copy.start()
    seeds, classes = logits_ref.shape
    rows = codes_ref.shape[0]
    neighbours = rows // seeds
    features, hidden = first_ref.shape
    half = keep_ref.shape[0]
    zero = jnp.zeros((), bf16)
    own_rows = [slice(b * rows // blocks, (b + 1) * rows // blocks) for b in range(blocks)]
    own_seeds = [slice(b * seeds // blocks, (b + 1) * seeds // blocks) for b in range(blocks)]
    size, seed_size = rows // blocks, seeds // blocks

    def rectified(pre):
        return jnp.maximum(pre.astype(bf16), zero)

    def masked(act, grad):
        return jnp.where(act > zero, grad.astype(bf16), zero)

    def joined(parts):
        return jnp.concatenate(parts, axis=0)

    slots = arrived_ref.shape[0]
    every_code = coded_slots(iota((16, slots), 1)).astype(bf16)
    every_code = jnp.concatenate([every_code] * (size // 16), axis=0)
    x = []
    for r in own_rows:
        code = jnp.concatenate([codes_ref[r, :]] * (slots // LANES), axis=1)
        pick = jnp.where(code == every_code, jnp.ones((), bf16), zero)
        x.append(dot(pick, arrived_ref[...]).astype(bf16))
    copies[0].wait()
    first_act = [rectified(dot(part, first_ref[...])) for part in x]
    copies[1].wait()
    copies[2].wait()
    second_act = [rectified(dot(part, second_ref[...])) for part in first_act]
    weighted, terms = [], []
    for act, r, s in zip(second_act, own_rows, own_seeds):
        row_logits = dot(act, third_t_ref[...], ((1,), (1,)))
        weight = weights_ref[r, :]
        weight = jnp.concatenate([weight, weight[:, : classes - LANES]], axis=1)
        logits = jnp.sum((weight * row_logits).reshape(seed_size, neighbours, classes), axis=1)
        logits_ref[s, :] = logits
        highest = jnp.max(logits, axis=1, keepdims=True)
        log_total = jnp.log(jnp.sum(jnp.exp(logits - highest), axis=1, keepdims=True)) + highest
        onehot = jnp.where(labels_ref[s, :] == iota((seed_size, classes), 1), 1.0, 0.0)
        terms.append(log_total - jnp.sum(onehot * logits, axis=1, keepdims=True))
        logit_grad = (jnp.exp(logits - log_total) - onehot) / total_seeds
        every = jnp.broadcast_to(logit_grad[:, None, :], (seed_size, neighbours, classes)).reshape(size, classes)
        weighted.append((weight * every).astype(bf16))
    second_grad = [masked(a, dot(g, third_t_ref[...])) for a, g in zip(second_act, weighted)]
    first_grad = [masked(a, dot(g, second_ref[...], ((1,), (1,)))) for a, g in zip(first_act, second_grad)]
    end_first = features
    end_second = end_first + hidden
    end_third = end_second + classes
    down = ((0,), (0,))
    grads_ref[end_second:end_third, :] = dot(joined(weighted), joined(second_act), down)
    grads_ref[end_first:end_second, :] = dot(joined(first_act), joined(second_grad), down)
    grads_ref[:end_first, :] = dot(joined(x), joined(first_grad), down)
    grads_ref[end_third:, :] = jnp.zeros((2 * half - end_third, hidden), f32)
    diagonal = iota((seeds, LANES), 0) == iota((seeds, LANES), 1)
    grads_ref[end_third : end_third + 1, :LANES] = jnp.sum(jnp.where(diagonal, joined(terms), 0.0), axis=0, keepdims=True)
    core = core_ref[0]
    keep_ref[...] = grads_ref[pl.ds(pl.multiple_of(core * half, half), half), :]
    send_ref[...] = grads_ref[pl.ds(pl.multiple_of((1 - core) * half, half), half), :].astype(bf16)


def finish_body(total_seeds, core_ref, own_ref, other_ref, loss_ref, first_ref, second_ref, third_t_ref):
    half = own_ref.shape[0]
    end_first = first_ref.shape[0]
    end_second = end_first + second_ref.shape[0]
    end_third = end_second + third_t_ref.shape[0]

    def write(low_ref, high_ref):
        first_ref[...] = low_ref[:end_first, :].astype(f32)
        second_ref[: half - end_first, :] = low_ref[end_first:, :].astype(f32)
        second_ref[half - end_first :, :] = high_ref[: end_second - half, :].astype(f32)
        third_t_ref[...] = high_ref[end_second - half : end_third - half, :].astype(f32)
        terms = high_ref[end_third - half : end_third - half + 1, :LANES].astype(f32)
        loss_ref[...] = jnp.sum(terms, axis=1, keepdims=True) / total_seeds

    @pl.when(core_ref[0] == 0)
    def _():
        write(own_ref, other_ref)

    @pl.when(core_ref[0] != 0)
    def _():
        write(other_ref, own_ref)


def everywhere(parts, axis):
    return lax.all_to_all(parts, axis, 0, 0, tiled=True)


def on_device(features, nbr_owner, nbr_local, ppr_weight, labels, w_first, w_second, w_third):
    groups = lax.axis_size(NODES)
    chips = lax.axis_size(CHIPS)
    seeds, neighbours = nbr_owner.shape
    capacity = min(seeds, 2 * seeds * neighbours // groups)
    width, hidden = w_first.shape
    classes = w_third.shape[1]
    total_seeds = float(seeds * groups)
    slots = groups * capacity
    shape = jax.ShapeDtypeStruct
    core = lax.axis_index(CORE).astype(i32).reshape(1)
    swap = [(0, 1), (1, 0)]

    table = call(
        functools.partial(request_body, capacity),
        shape((groups, LANES), i32),
        [FAR, FAR],
        [
            pltpu.VMEM((seeds, neighbours), i32),
            pltpu.VMEM((seeds, neighbours), i32),
            pltpu.SemaphoreType.DMA((2,)),
        ],
    )(*(pltpu.with_memory_space_constraint(a, pltpu.HBM) for a in (nbr_owner, nbr_local)))
    asked = everywhere(table.reshape(groups, 1, LANES), NODES).reshape(groups, LANES)
    pairs = pltpu.with_memory_space_constraint(features.reshape(-1, 2, width), pltpu.HBM)
    held = call(
        hold_body,
        pltpu.VMEM((pairs.shape[0] * 3 // 4, 2, width), bf16),
        [FAR],
        [pltpu.SemaphoreType.DMA],
    )(pairs)
    codes, weights = call(
        functools.partial(spread_body, capacity, groups),
        (shape((seeds * neighbours, LANES), bf16), shape((seeds * neighbours, LANES), f32)),
        [VMEM] * 2,
    )(nbr_owner, ppr_weight)
    served = call(
        functools.partial(serve_body, capacity),
        pltpu.HBM((slots, width), bf16),
        [VMEM, VMEM, FAR],
        [
            pltpu.VMEM((slots, width), bf16),
            pltpu.VMEM(pairs.shape, bf16),
            pltpu.VMEM((8 * 2 * capacity, width), f32),
            pltpu.VMEM((capacity, groups), i32),
            pltpu.SMEM((capacity, groups), i32),
            pltpu.SemaphoreType.DMA((3,)),
            pltpu.SemaphoreType.DMA((groups // 8,)),
        ],
        16,
        FAR,
    )(asked, held, pairs)
    arrived = everywhere(served.reshape(groups, capacity, width), NODES).reshape(slots, width)

    tile = 8
    half = chips * tile * -(-(width + hidden + classes + 1) // (2 * chips * tile))
    params = [pltpu.with_memory_space_constraint(p, pltpu.HBM) for p in (w_first, w_second, w_third.T)]
    seed_logits, keep, send = call(
        functools.partial(step_body, total_seeds, 2),
        (shape((seeds, classes), f32), shape((half, hidden), f32), shape((half, hidden), bf16)),
        [SMEM] + [VMEM] * 4 + [FAR] * 3,
        [
            pltpu.VMEM((2 * half, hidden), f32),
            *(pltpu.VMEM(p.shape, p.dtype) for p in params),
            pltpu.SemaphoreType.DMA((3,)),
        ],
        24,
    )(core, codes, arrived, weights, labels.reshape(-1, 1), *params)
    near = lax.ppermute(send, CORE, swap)
    parts = (keep + near.astype(f32)).astype(bf16).reshape(chips, half // chips, hidden)
    mine = jnp.sum(everywhere(parts, CHIPS).astype(f32), axis=0).astype(bf16)
    own = everywhere(jnp.broadcast_to(mine[None], parts.shape), CHIPS).reshape(half, hidden)
    other = lax.ppermute(own, CORE, swap)
    loss, grad_first, grad_second, grad_third_t = call(
        functools.partial(finish_body, total_seeds),
        (
            shape((1, 1), f32),
            shape((width, hidden), f32),
            shape((hidden, hidden), f32),
            shape((classes, hidden), f32),
        ),
        [SMEM, VMEM, VMEM],
    )(core, own, other)
    return (loss.reshape(()), seed_logits, grad_first, grad_second, grad_third_t.T)


def solution(mesh):
    finer = Mesh(mesh.devices.reshape(4, 4, 4, 2), NODES)
    placed = (
        P(NODES, None),
        P(NODES, None),
        P(NODES, None),
        P(NODES, None),
        P(NODES),
        P(),
        P(),
        P(),
    )
    return jax.shard_map(
        on_device,
        mesh=finer,
        in_specs=placed,
        out_specs=(P(), P(NODES, None), P(), P(), P()),
        check_vma=False,
    )
```

time: 103 us -> 95.2 us (0.924)
  waiting for transfers between devices: 10.1 us -> 20.1 us
  Pallas kernels: 29.8 us -> 20.9 us
  local copies, waits for them, and re-layouts: 6.33 us -> 0.14 us
  starting transfers between devices: 23.2 us -> 20.7 us
    all_to_all x2, waiting for transfers between devices: 7.01 us -> 17 us  [everywhere(): return lax.all_to_all(parts, axis, 0, 0, tiled=True)]
    pallas_call x5, Pallas kernels: 28.4 us -> 19.6 us  [the longest x1 6.13 us: on_device(): call(functools.partial(step_body, total_seeds, 2), (shape((seeds, classes...]
    unnamed x21 -> x6, local copies, waits for them, and re-layouts: 5.67 us -> 0.01 us
    all_to_all x2, starting transfers between devices: 18.8 us -> 16.3 us  [everywhere(): return lax.all_to_all(parts, axis, 0, 0, tiled=True)]
  transfers between devices with their start and end apart: 4 -> 4, of which waited for: 4 -> 4; matrix products, arithmetic and copies ran while one was open for 1% -> 0% of each run, Pallas kernels for 11% -> 6%
where the time goes in v2:
time: 95.2 us; the launch traced here: 94.8 us
  blocking collectives  31.9 us (34%)
  Pallas kernels  20.9 us (22%)
  starting transfers between devices  20.7 us (22%)
  waiting for transfers between devices  20.1 us (21%)
    all_to_all x2, blocking collectives, everywhere(): return lax.all_to_all(parts, axis, 0, 0, tiled=True)  31.9 us
    all_to_all x2, waiting for transfers between devices, everywhere(): return lax.all_to_all(parts, axis, 0, 0, tiled=True)  17 us
    all_to_all x2, starting transfers between devices, everywhere(): return lax.all_to_all(parts, axis, 0, 0, tiled=True)  16.3 us
    pallas_call x1, Pallas kernels, on_device(): call(functools.partial(step_body, total_seeds, 2), (shape((seeds, classes...  6.13 us
    pallas_call x1, Pallas kernels, on_device(): call(functools.partial(serve_body, capacity), pltpu.HBM((slots, width), b...  5.66 us
    pallas_call x1, Pallas kernels, on_device(): call(functools.partial(spread_body, capacity, groups), (shape((seeds * ne...  3.91 us
    ppermute x1, starting transfers between devices, on_device(): other = lax.ppermute(own, CORE, swap)  3.22 us
    pallas_call x1, Pallas kernels, on_device(): call(functools.partial(request_body, capacity), shape((groups, LANES), i3...  1.97 us
  transfers between devices with their start and end apart: 4, of which 4 were waited for; matrix products, arithmetic and copies ran while one was open for 0% of the time, Pallas kernels for 6%

profile of v2, /device:TPU:1, one launch (start us, length us, event | category | flops | bytes accessed | tf_op | source)
XLA Modules:
  0.0 94.8 jit_solution(4814523471463826621)
XLA Ops:
  0.6 2.0 %shard_map.120 = s32[128,128]{1,0:T(8,128)} custom-call(s32[32,32]{1,0:T(8,128)} %owner_hbm.1, s32[32,32]{1,0:T(8,128)} %local_hbm.1), custom_call_target="tpu_custom_call" | custom-call | tf_op jit(solution)/shard_map/pallas_call | solution.py:281
  2.6 11.5 %all-to-all-start = ((s32[128,1,128]{2,1,0:T(1,128)}), s32[128,1,128]{2,1,0:T(1,128)S(1)}, u32[]{:S(2)}, u32[]{:S(2)}) async-start(s32[128,1,128]{2,1,0:T(1,128)} %bitcast.2), calls=%async_computation | async-start | bytes 131072 | tf_op jit(solution)/shard_map/all_to_all | solution.py:265
  14.1 1.9 %shard_map.121.held_ref = bf16[6144,2,128]{2,1,0:T(2,128)(2,1)S(1)} custom-call(bf16[8192,2,128]{2,1,0:T(2,128)(2,1)} %bitcast.19), custom_call_target="tpu_custom_call" | custom-call | tf_op jit(solution)/shard_map/pallas_call | solution.py:293
  16.0 7.4 %all-to-all-done = s32[128,1,128]{2,1,0:T(1,128)S(1)} async-done(((s32[128,1,128]{2,1,0:T(1,128)}), s32[128,1,128]{2,1,0:T(1,128)S(1)}, u32[]{:S(2)}, u32[]{:S(2)}) %all-to-all-start) | async-done | bytes 65568 | tf_op jit(solution)/shard_map/all_to_all | solution.py:265
  23.4 0.0 copy-start
  23.4 0.0 copy-start.1
  23.4 0.0 copy-start.2
  23.4 5.7 %shard_map.122 = bf16[2048,128]{1,0:T(8,128)(2,1)} custom-call(s32[128,128]{1,0:T(8,128)S(1)} %bitcast.18, bf16[6144,2,128]{2,1,0:T(2,128)(2,1)S(1)} %shard_map.121.held_ref, bf16[8192,2,128]{2,1,0:T(2,128)(2,1)} %bitcast.20), custom_call_target="tpu_custom_call" | custom-call | tf_op jit(solution)/shard_map/pallas_call | solution.py:304
  29.1 4.8 %all-to-all-start.1 = ((bf16[128,16,128]{2,1,0:T(8,128)(2,1)}), bf16[128,16,128]{2,1,0:T(8,128)(2,1)S(1)}, u32[]{:S(2)}, u32[]{:S(2)}) async-start(bf16[128,16,128]{2,1,0:T(8,128)(2,1)} %bitcast.21), calls=%async_computation.1 | async-start | bytes 1048576 | tf_op jit(solution)/shard_map/all_to_all | solution.py:265
  33.8 0.0 copy-done
  33.8 0.0 copy-done.1
  33.9 3.9 %shard_map.119 = (bf16[1024,128]{1,0:T(8,128)(2,1)S(1)}, f32[1024,128]{1,0:T(8,128)S(1)}) custom-call(s32[32,32]{1,0:T(8,128)S(1)} %copy-done, f32[32,32]{1,0:T(8,128)S(1)} %copy-done.1), custom_call_target="tpu_custom_call" | custom-call | tf_op jit(solution)/shard_map/pallas_call | solution.py:299
  37.8 0.0 copy-done.2
  37.8 0.1 copy.15.labels_ref
  37.9 9.7 %all-to-all-done.1 = bf16[128,16,128]{2,1,0:T(8,128)(2,1)S(1)} async-done(((bf16[128,16,128]{2,1,0:T(8,128)(2,1)}), bf16[128,16,128]{2,1,0:T(8,128)(2,1)S(1)}, u32[]{:S(2)}, u32[]{:S(2)}) %all-to-all-start.1) | async-done | bytes 524320 | tf_op jit(solution)/shard_map/all_to_all | solution.py:265
  47.5 6.1 %shard_map.123 = (f32[32,172]{1,0:T(8,128)}, f32[512,512]{1,0:T(8,128)S(1)}, bf16[512,512]{1,0:T(8,128)(2,1)S(1)}) custom-call(s32[1]{0:T(128)} %bitcast.core_ref, bf16[1024,128]{1,0:T(8,128)(2,1)S(1)} %get-tuple-element.14.codes_ref, bf16[2048,128]{1,0:T(8,128)(2,1)S(1)} %bitcast.15, f32[1024,128]{1,0:T(8,128)S(1)} %get-tuple-element.15.weights_ref, ...), custom_call_target="tpu_custom_call" | custom-call | tf_op jit(solution)/shard_map/pallas_call | solution.py:325
  53.7 1.2 %collective-permute-start = (bf16[512,512]{1,0:T(8,128)(2,1)S(1)}, bf16[512,512]{1,0:T(8,128)(2,1)S(1)}, u32[]{:S(2)}, u32[]{:S(2)}) collective-permute-start(bf16[512,512]{1,0:T(8,128)(2,1)S(1)} %get-tuple-element.17), channel_id=1, source_target_pairs={{0,1},{1,0},{2,3},{3,2},{4,5},{5,4},{6,7},{7,6},{8,9},{9,8},{10,11... | collective-permute-start | bytes 1572872 | tf_op jit(solution)/shard_map/ppermute | solution.py:336
  54.9 1.5 %collective-permute-done = bf16[512,512]{1,0:T(8,128)(2,1)S(1)} collective-permute-done((bf16[512,512]{1,0:T(8,128)(2,1)S(1)}, bf16[512,512]{1,0:T(8,128)(2,1)S(1)}, u32[]{:S(2)}, u32[]{:S(2)}) %collective-permute-start) | collective-permute-done | bytes 524320 | tf_op jit(solution)/shard_map/ppermute | solution.py:336
  56.5 0.2 fusion
  56.7 16.4 %all_to_all.20 = bf16[64,8,512]{2,1,0:T(8,128)(2,1)S(1)} all-to-all(bf16[64,8,512]{2,1,0:T(8,128)(2,1)S(1)} %fusion), channel_id=1, replica_groups=mesh['nodes_0'=4,'nodes_1'=4,'nodes_2'=4,'nodes_3'=2] {'nodes_0','nodes_..., dimensions={0} | all-to-all | bytes 1048576 | tf_op jit(solution)/shard_map/all_to_all | solution.py:265
  73.0 0.1 reduce_sum.12
  73.2 15.5 %all_to_all.21 = bf16[64,8,512]{2,1,0:T(8,128)(2,1)S(1)} all-to-all(bf16[64,8,512]{2,1,0:T(8,128)(2,1)S(1)} %broadcast_in_dim.2), channel_id=1, replica_groups=mesh['nodes_0'=4,'nodes_1'=4,'nodes_2'=4,'nodes_3'=2] {'nodes_0','nodes_..., dimensions={0} | all-to-all | bytes 1048576 | tf_op jit(solution)/shard_map/all_to_all | solution.py:265
  88.7 3.2 %collective-permute-start.1 = (bf16[512,512]{1,0:T(8,128)(2,1)S(1)}, bf16[512,512]{1,0:T(8,128)(2,1)S(1)}, u32[]{:S(2)}, u32[]{:S(2)}) collective-permute-start(bf16[512,512]{1,0:T(8,128)(2,1)S(1)} %bitcast.16), channel_id=1, source_target_pairs={{0,1},{1,0},{2,3},{3,2},{4,5},{5,4},{6,7},{7,6},{8,9},{9,8},{10,11... | collective-permute-start | bytes 1572872 | tf_op jit(solution)/shard_map/ppermute | solution.py:340
  91.9 1.5 %collective-permute-done.1.other_ref = bf16[512,512]{1,0:T(8,128)(2,1)S(1)} collective-permute-done((bf16[512,512]{1,0:T(8,128)(2,1)S(1)}, bf16[512,512]{1,0:T(8,128)(2,1)S(1)}, u32[]{:S(2)}, u32[]{:S(2)}) %collective-permute-start.1) | collective-permute-done | bytes 524320 | tf_op jit(solution)/shard_map/ppermute | solution.py:340
  93.4 1.3 %shard_map.124 = (f32[1,1]{1,0:T(1,128)}, f32[128,512]{1,0:T(8,128)}, f32[512,512]{1,0:T(8,128)}, f32[172,512]{1,0:T(8,128)}) custom-call(s32[1]{0:T(128)} %bitcast.core_ref, bf16[512,512]{1,0:T(8,128)(2,1)S(1)} %bitcast.17, bf16[512,512]{1,0:T(8,128)(2,1)S(1)} %collective-permute-done.1.other_ref), custom_call_target="tpu_custom_call" | custom-call | tf_op jit(solution)/shard_map/pallas_call | solution.py:341
  (1 shorter events, 0.0 us)
Async XLA Ops:
  2.6 20.8 %all-to-all-start = ((s32[128,1,128]{2,1,0:T(1,128)}), s32[128,1,128]{2,1,0:T(1,128)S(1)}, u32[]{:S(2)}, u32[]{:S(2)}) async-start(s32[128,1,128]{2,1,0:T(1,128)} %bitcast.2), calls=%async_computation | async-start | bytes 131072 | tf_op jit(solution)/shard_map/all_to_all | solution.py:265
  23.4 10.4 %copy-start = (s32[32,32]{1,0:T(8,128)S(1)}, s32[32,32]{1,0:T(8,128)}, u32[]{:S(2)}) copy-start(s32[32,32]{1,0:T(8,128)} %owner_hbm.1) | copy-start | bytes 12292
  23.4 10.4 %copy-start.1 = (f32[32,32]{1,0:T(8,128)S(1)}, f32[32,32]{1,0:T(8,128)}, u32[]{:S(2)}) copy-start(f32[32,32]{1,0:T(8,128)} %weight_ref.1) | copy-start | bytes 12292
  23.4 14.4 %copy-start.2 = (s32[32]{0:T(128)S(1)}, s32[32]{0:T(128)}, u32[]{:S(2)}) copy-start(s32[32]{0:T(128)} %param.12) | copy-start | bytes 388
  29.1 18.5 %all-to-all-start.1 = ((bf16[128,16,128]{2,1,0:T(8,128)(2,1)}), bf16[128,16,128]{2,1,0:T(8,128)(2,1)S(1)}, u32[]{:S(2)}, u32[]{:S(2)}) async-start(bf16[128,16,128]{2,1,0:T(8,128)(2,1)} %bitcast.21), calls=%async_computation.1 | async-start | bytes 1048576 | tf_op jit(solution)/shard_map/all_to_all | solution.py:265
  53.7 2.8 %collective-permute-start = (bf16[512,512]{1,0:T(8,128)(2,1)S(1)}, bf16[512,512]{1,0:T(8,128)(2,1)S(1)}, u32[]{:S(2)}, u32[]{:S(2)}) collective-permute-start(bf16[512,512]{1,0:T(8,128)(2,1)S(1)} %get-tuple-element.17), channel_id=1, source_target_pairs={{0,1},{1,0},{2,3},{3,2},{4,5},{5,4},{6,7},{7,6},{8,9},{9,8},{10,11... | collective-permute-start | bytes 1572872 | tf_op jit(solution)/shard_map/ppermute | solution.py:336
  88.7 4.8 %collective-permute-start.1 = (bf16[512,512]{1,0:T(8,128)(2,1)S(1)}, bf16[512,512]{1,0:T(8,128)(2,1)S(1)}, u32[]{:S(2)}, u32[]{:S(2)}) collective-permute-start(bf16[512,512]{1,0:T(8,128)(2,1)S(1)} %bitcast.16), channel_id=1, source_target_pairs={{0,1},{1,0},{2,3},{3,2},{4,5},{5,4},{6,7},{7,6},{8,9},{9,8},{10,11... | collective-permute-start | bytes 1572872 | tf_op jit(solution)/shard_map/ppermute | solution.py:340

commit v3 on v2

--- a/solution.py
+++ b/solution.py
@@ -88,7 +88,9 @@
     copy.wait()
 
 
-def spread_body(capacity, groups, owner_ref, weight_ref, codes_ref, weights_ref):
+def spread_body(capacity, groups, owner_ref, weight_ref, second_hbm, codes_ref, weights_ref, second_ref, arrival):
+    second = pltpu.make_async_copy(second_hbm, second_ref, arrival)
+    second.start()
     seeds, neighbours = owner_ref.shape
     _, earlier, _ = places(capacity, groups, owner_ref[...])
     code_of = coded_slots(iota((seeds, groups), 1) * capacity + earlier)
@@ -101,6 +103,7 @@
         code = jnp.sum(own, axis=1, keepdims=True)
         codes_ref[rows, :] = jnp.broadcast_to(code, (neighbours, codes_ref.shape[1])).astype(bf16)
         weights_ref[rows, :] = jnp.broadcast_to(weight_t[:, s : s + 1], (neighbours, weights_ref.shape[1]))
+    second.wait()
 
 
 def serve_body(
@@ -158,28 +161,23 @@
     arrived_ref,
     weights_ref,
     labels_ref,
-    first_hbm,
-    second_hbm,
-    third_t_hbm,
-    logits_ref,
-    keep_ref,
-    send_ref,
-    grads_ref,
     first_ref,
     second_ref,
     third_t_ref,
-    arrivals,
+    logits_ref,
+    send_ref,
+    terms_ref,
+    x_ref,
+    first_act_ref,
+    weighted_ref,
+    second_act_ref,
+    second_grad_ref,
+    first_grad_ref,
+    grads_ref,
 ):
-    sources = (first_hbm, second_hbm, third_t_hbm)
-    targets = (first_ref, second_ref, third_t_ref)
-    copies = [pltpu.make_async_copy(a, b, arrivals.at[i]) for i, (a, b) in enumerate(zip(sources, targets))]
-    for copy in copies:
-        copy.start()
     seeds, classes = logits_ref.shape
     rows = codes_ref.shape[0]
     neighbours = rows // seeds
-    features, hidden = first_ref.shape
-    half = keep_ref.shape[0]
     zero = jnp.zeros((), bf16)
     own_rows = [slice(b * rows // blocks, (b + 1) * rows // blocks) for b in range(blocks)]
     own_seeds = [slice(b * seeds // blocks, (b + 1) * seeds // blocks) for b in range(blocks)]
@@ -191,8 +189,11 @@
     def masked(act, grad):
         return jnp.where(act > zero, grad.astype(bf16), zero)
 
-    def joined(parts):
-        return jnp.concatenate(parts, axis=0)
+    def halves(ref, parts):
+        wide = ref.shape[2]
+        for part, r in zip(parts, own_rows):
+            for h in range(2):
+                ref[h, r, :] = part[:, h * wide : (h + 1) * wide]
 
     slots = arrived_ref.shape[0]
     every_code = coded_slots(iota((16, slots), 1)).astype(bf16)
@@ -202,11 +203,12 @@
         code = jnp.concatenate([codes_ref[r, :]] * (slots // LANES), axis=1)
         pick = jnp.where(code == every_code, jnp.ones((), bf16), zero)
         x.append(dot(pick, arrived_ref[...]).astype(bf16))
-    copies[0].wait()
+        x_ref[r, :] = x[-1]
     first_act = [rectified(dot(part, first_ref[...])) for part in x]
-    copies[1].wait()
-    copies[2].wait()
     second_act = [rectified(dot(part, second_ref[...])) for part in first_act]
+    for part, r in zip(first_act, own_rows):
+        first_act_ref[r, :] = part
+    halves(second_act_ref, second_act)
     weighted, terms = [], []
     for act, r, s in zip(second_act, own_rows, own_seeds):
         row_logits = dot(act, third_t_ref[...], ((1,), (1,)))
@@ -221,44 +223,105 @@
         logit_grad = (jnp.exp(logits - log_total) - onehot) / total_seeds
         every = jnp.broadcast_to(logit_grad[:, None, :], (seed_size, neighbours, classes)).reshape(size, classes)
         weighted.append((weight * every).astype(bf16))
+        weighted_ref[r, :] = weighted[-1]
     second_grad = [masked(a, dot(g, third_t_ref[...])) for a, g in zip(second_act, weighted)]
+    halves(second_grad_ref, second_grad)
     first_grad = [masked(a, dot(g, second_ref[...], ((1,), (1,)))) for a, g in zip(first_act, second_grad)]
-    end_first = features
-    end_second = end_first + hidden
-    end_third = end_second + classes
+    halves(first_grad_ref, first_grad)
+    diagonal = iota((seeds, LANES), 0) == iota((seeds, LANES), 1)
+    loss_row = jnp.sum(jnp.where(diagonal, jnp.concatenate(terms, axis=0), 0.0), axis=0, keepdims=True)
+    terms_ref[...] = jnp.broadcast_to(loss_row, terms_ref.shape)
+    other = 1 - core_ref[0]
+    write_half(
+        grads_ref, loss_row, x_ref, first_act_ref, weighted_ref, second_act_ref, second_grad_ref, first_grad_ref, other
+    )
+    send_ref[...] = grads_ref[...].astype(bf16)
+
+
+def write_half(out_ref, loss_row, x_ref, first_act_ref, weighted_ref, second_act_ref, second_grad_ref, first_grad_ref, half):
     down = ((0,), (0,))
-    grads_ref[end_second:end_third, :] = dot(joined(weighted), joined(second_act), down)
-    grads_ref[end_first:end_second, :] = dot(joined(first_act), joined(second_grad), down)
-    grads_ref[:end_first, :] = dot(joined(x), joined(first_grad), down)
-    grads_ref[end_third:, :] = jnp.zeros((2 * half - end_third, hidden), f32)
-    diagonal = iota((seeds, LANES), 0) == iota((seeds, LANES), 1)
-    grads_ref[end_third : end_third + 1, :LANES] = jnp.sum(jnp.where(diagonal, joined(terms), 0.0), axis=0, keepdims=True)
-    core = core_ref[0]
-    keep_ref[...] = grads_ref[pl.ds(pl.multiple_of(core * half, half), half), :]
-    send_ref[...] = grads_ref[pl.ds(pl.multiple_of((1 - core) * half, half), half), :].astype(bf16)
-
-
-def finish_body(total_seeds, core_ref, own_ref, other_ref, loss_ref, first_ref, second_ref, third_t_ref):
-    half = own_ref.shape[0]
-    end_first = first_ref.shape[0]
-    end_second = end_first + second_ref.shape[0]
-    end_third = end_second + third_t_ref.shape[0]
-
-    def write(low_ref, high_ref):
-        first_ref[...] = low_ref[:end_first, :].astype(f32)
-        second_ref[: half - end_first, :] = low_ref[end_first:, :].astype(f32)
-        second_ref[half - end_first :, :] = high_ref[: end_second - half, :].astype(f32)
-        third_t_ref[...] = high_ref[end_second - half : end_third - half, :].astype(f32)
-        terms = high_ref[end_third - half : end_third - half + 1, :LANES].astype(f32)
-        loss_ref[...] = jnp.sum(terms, axis=1, keepdims=True) / total_seeds
-
-    @pl.when(core_ref[0] == 0)
-    def _():
-        write(own_ref, other_ref)
-
-    @pl.when(core_ref[0] != 0)
-    def _():
-        write(other_ref, own_ref)
+    first = dot(x_ref[...], first_grad_ref[half], down)
+    second = dot(first_act_ref[...], second_grad_ref[half], down)
+    third = dot(weighted_ref[...], second_act_ref[half], down)
+    parts = first.shape[1] // LANES
+    tall = out_ref.shape[0] // parts
+    for j in range(parts):
+        at = j * tall
+        for piece in (first, second, third):
+            out_ref[at : at + piece.shape[0], :] = piece[:, j * LANES : (j + 1) * LANES]
+            at += piece.shape[0]
+        out_ref[at : (j + 1) * tall, :] = jnp.zeros(((j + 1) * tall - at, LANES), f32)
+        out_ref[at : at + 1, :] = loss_row
+
+
+def keep_body(
+    core_ref, terms_ref, x_ref, first_act_ref, weighted_ref, second_act_ref, second_grad_ref, first_grad_ref, keep_ref
+):
+    write_half(
+        keep_ref,
+        terms_ref[:1, :],
+        x_ref,
+        first_act_ref,
+        weighted_ref,
+        second_act_ref,
+        second_grad_ref,
+        first_grad_ref,
+        core_ref[0],
+    )
+
+
+def total_body(chips, parts_ref, total_ref):
+    rows = parts_ref.shape[0]
+    chunk = rows // chips
+    tall = -(-chunk // 8) * 8
+    column = iota((tall, rows), 1)
+    which = ((column.astype(f32) + 0.5) / chunk).astype(i32)
+    same = jnp.where(column - which * chunk == iota((tall, rows), 0), 1.0, 0.0).astype(bf16)
+    total = dot(same, parts_ref[...]).astype(bf16)
+    total_ref[...] = dot(same, total, ((0,), (0,))).astype(bf16)
+
+
+def columns(half, half_ref, outs, stages, arrivals):
+    copies = []
+    at = 0
+    for i, (out, stage) in enumerate(zip(outs, stages)):
+        size, wide = stage.shape
+        parts = wide // LANES
+        tall = half_ref.shape[0] // parts
+        for j in range(parts):
+            stage[:, j * LANES : (j + 1) * LANES] = half_ref[j * tall + at : j * tall + at + size, :].astype(f32)
+        span = pl.ds(pl.multiple_of(half * wide, wide), wide)
+        copies.append(pltpu.make_async_copy(stage, out.at[:, span], arrivals.at[i]))
+        copies[-1].start()
+        at += size
+    for copy in copies:
+        copy.wait()
+
+
+def own_body(core_ref, own_ref, first_hbm, second_hbm, third_t_hbm, *scratch):
+    columns(core_ref[0], own_ref, (first_hbm, second_hbm, third_t_hbm), scratch[:3], scratch[3])
+
+
+def other_body(
+    total_seeds,
+    core_ref,
+    own_ref,
+    other_ref,
+    given_first,
+    given_second,
+    given_third_t,
+    loss_ref,
+    first_hbm,
+    second_hbm,
+    third_t_hbm,
+    *scratch,
+):
+    del given_first, given_second, given_third_t
+    outs = (first_hbm, second_hbm, third_t_hbm)
+    at = sum(out.shape[0] for out in outs)
+    low = jnp.where(core_ref[0] == 0, own_ref[at : at + 1, :].astype(f32), other_ref[at : at + 1, :].astype(f32))
+    loss_ref[...] = jnp.sum(low, axis=1, keepdims=True) / total_seeds
+    columns(1 - core_ref[0], other_ref, outs, scratch[:3], scratch[3])
 
 
 def everywhere(parts, axis):
@@ -296,11 +359,16 @@
         [FAR],
         [pltpu.SemaphoreType.DMA],
     )(pairs)
-    codes, weights = call(
+    codes, weights, second = call(
         functools.partial(spread_body, capacity, groups),
-        (shape((seeds * neighbours, LANES), bf16), shape((seeds * neighbours, LANES), f32)),
-        [VMEM] * 2,
-    )(nbr_owner, ppr_weight)
+        (
+            shape((seeds * neighbours, LANES), bf16),
+            shape((seeds * neighbours, LANES), f32),
+            pltpu.VMEM(w_second.shape, bf16),
+        ),
+        [VMEM, VMEM, FAR],
+        [pltpu.SemaphoreType.DMA],
+    )(nbr_owner, ppr_weight, pltpu.with_memory_space_constraint(w_second, pltpu.HBM))
     served = call(
         functools.partial(serve_body, capacity),
         pltpu.HBM((slots, width), bf16),
@@ -319,35 +387,46 @@
     )(asked, held, pairs)
     arrived = everywhere(served.reshape(groups, capacity, width), NODES).reshape(slots, width)
 
-    tile = 8
-    half = chips * tile * -(-(width + hidden + classes + 1) // (2 * chips * tile))
-    params = [pltpu.with_memory_space_constraint(p, pltpu.HBM) for p in (w_first, w_second, w_third.T)]
-    seed_logits, keep, send = call(
+    rows = seeds * neighbours
+    half = hidden // 2
+    blocks = half // LANES
+    tall = 2 * chips // blocks * -(-(width + hidden + classes + 1) * blocks // (2 * chips))
+    grads = (blocks * tall, LANES)
+    seed_logits, send, *kept = call(
         functools.partial(step_body, total_seeds, 2),
-        (shape((seeds, classes), f32), shape((half, hidden), f32), shape((half, hidden), bf16)),
-        [SMEM] + [VMEM] * 4 + [FAR] * 3,
-        [
-            pltpu.VMEM((2 * half, hidden), f32),
-            *(pltpu.VMEM(p.shape, p.dtype) for p in params),
-            pltpu.SemaphoreType.DMA((3,)),
-        ],
-        24,
-    )(core, codes, arrived, weights, labels.reshape(-1, 1), *params)
+        (
+            shape((seeds, classes), f32),
+            shape(grads, bf16),
+            shape((8, LANES), f32),
+            shape((rows, width), bf16),
+            shape((rows, hidden), bf16),
+            shape((rows, classes), bf16),
+            *(shape((2, rows, half), bf16) for _ in range(3)),
+        ),
+        [SMEM] + [VMEM] * 7,
+        [pltpu.VMEM(grads, f32)],
+        32,
+    )(core, codes, arrived, weights, labels.reshape(-1, 1), w_first, second, w_third.T)
     near = lax.ppermute(send, CORE, swap)
-    parts = (keep + near.astype(f32)).astype(bf16).reshape(chips, half // chips, hidden)
-    mine = jnp.sum(everywhere(parts, CHIPS).astype(f32), axis=0).astype(bf16)
-    own = everywhere(jnp.broadcast_to(mine[None], parts.shape), CHIPS).reshape(half, hidden)
+    keep = call(keep_body, shape(grads, f32), [SMEM] + [VMEM] * 7, (), 16)(core, *kept)
+    parts = (keep + near.astype(f32)).astype(bf16)
+    mine = everywhere(parts.reshape(-1, 2, LANES), CHIPS).reshape(grads)
+    totals = call(functools.partial(total_body, chips), shape(grads, bf16), [VMEM])(mine)
+    own = everywhere(totals.reshape(-1, 2, LANES), CHIPS).reshape(grads)
     other = lax.ppermute(own, CORE, swap)
-    loss, grad_first, grad_second, grad_third_t = call(
-        functools.partial(finish_body, total_seeds),
-        (
-            shape((1, 1), f32),
-            shape((width, hidden), f32),
-            shape((hidden, hidden), f32),
-            shape((classes, hidden), f32),
-        ),
-        [SMEM, VMEM, VMEM],
-    )(core, own, other)
+    sizes = (width, hidden, classes)
+    scratch = [*(pltpu.VMEM((n, half), f32) for n in sizes), pltpu.SemaphoreType.DMA((3,))]
+    sums = tuple(pltpu.HBM((n, hidden), f32) for n in sizes)
+    started = call(own_body, sums, [SMEM, VMEM], scratch, 8, FAR)(core, own)
+    loss, grad_first, grad_second, grad_third_t = pl.pallas_call(
+        functools.partial(other_body, total_seeds),
+        out_shape=(shape((1, 1), f32), *sums),
+        in_specs=[SMEM, VMEM, VMEM, FAR, FAR, FAR],
+        out_specs=(VMEM, FAR, FAR, FAR),
+        scratch_shapes=scratch,
+        input_output_aliases={3: 1, 4: 2, 5: 3},
+        compiler_params=pltpu.CompilerParams(vmem_limit_bytes=8 << 20),
+    )(core, own, other, *started)
     return (loss.reshape(()), seed_logits, grad_first, grad_second, grad_third_t.T)
 
 

time: 95.2 us -> 91.7 us (0.963)
  waiting for transfers between devices: 20.1 us -> 17.6 us
  blocking collectives: 31.9 us -> 30.3 us
    pallas_call x1 -> x4, Pallas kernels: 1.35 us -> 3.52 us  [the longest x1 1.43 us: on_device(): pl.pallas_call(functools.partial(other_body, total_seeds), out_shape=(sha...]
    pallas_call x1, Pallas kernels: 6.13 us -> 4.15 us  [on_device(): call(functools.partial(step_body, total_seeds, 2), (shape((seeds, classes...]
    all_to_all x2, blocking collectives: 31.9 us -> 30.3 us  [everywhere(): return lax.all_to_all(parts, axis, 0, 0, tiled=True)]
    ppermute x1, waiting for transfers between devices: 1.54 us -> 0.47 us  [on_device(): other = lax.ppermute(own, CORE, swap)]
  transfers between devices with their start and end apart: 4 -> 4, of which waited for: 4 -> 4; matrix products, arithmetic and copies ran while one was open for 0% -> 1% of each run, Pallas kernels for 6% -> 8%
where the time goes in v3:
time: 91.7 us; the launch traced here: 91.2 us
  blocking collectives  30.3 us (33%)
  Pallas kernels  21.2 us (23%)
  starting transfers between devices  20.6 us (22%)
  waiting for transfers between devices  17.6 us (19%)
    all_to_all x2, blocking collectives, everywhere(): return lax.all_to_all(parts, axis, 0, 0, tiled=True)  30.3 us
    all_to_all x2, waiting for transfers between devices, everywhere(): return lax.all_to_all(parts, axis, 0, 0, tiled=True)  16.4 us
    all_to_all x2, starting transfers between devices, everywhere(): return lax.all_to_all(parts, axis, 0, 0, tiled=True)  16.3 us
    pallas_call x1, Pallas kernels, on_device(): call(functools.partial(serve_body, capacity), pltpu.HBM((slots, width), b...  5.69 us
    pallas_call x1, Pallas kernels, on_device(): call(functools.partial(step_body, total_seeds, 2), (shape((seeds, classes...  4.15 us
    pallas_call x1, Pallas kernels, on_device(): call(functools.partial(spread_body, capacity, groups), (shape((seeds * ne...  3.93 us
    ppermute x1, starting transfers between devices, on_device(): other = lax.ppermute(own, CORE, swap)  3.14 us
    pallas_call x1, Pallas kernels, on_device(): call(functools.partial(request_body, capacity), shape((groups, LANES), i3...  1.97 us
  transfers between devices with their start and end apart: 4, of which 4 were waited for; matrix products, arithmetic and copies ran while one was open for 1% of the time, Pallas kernels for 8%

profile of v3, /device:TPU:1, one launch (start us, length us, event | category | flops | bytes accessed | tf_op | source)
XLA Modules:
  0.0 91.2 jit_solution(13413606388502826706)
XLA Ops:
  0.6 2.0 %shard_map.120 = s32[128,128]{1,0:T(8,128)} custom-call(s32[32,32]{1,0:T(8,128)} %owner_hbm.1, s32[32,32]{1,0:T(8,128)} %local_hbm.1), custom_call_target="tpu_custom_call" | custom-call | tf_op jit(solution)/shard_map/pallas_call | solution.py:344
  2.6 11.5 %all-to-all-start = ((s32[128,1,128]{2,1,0:T(1,128)}), s32[128,1,128]{2,1,0:T(1,128)S(1)}, u32[]{:S(2)}, u32[]{:S(2)}) async-start(s32[128,1,128]{2,1,0:T(1,128)} %bitcast.2), calls=%async_computation | async-start | bytes 131072 | tf_op jit(solution)/shard_map/all_to_all | solution.py:328
  14.1 1.9 %shard_map.121.held_ref = bf16[6144,2,128]{2,1,0:T(2,128)(2,1)S(1)} custom-call(bf16[8192,2,128]{2,1,0:T(2,128)(2,1)} %bitcast.24), custom_call_target="tpu_custom_call" | custom-call | tf_op jit(solution)/shard_map/pallas_call | solution.py:356
  16.0 7.4 %all-to-all-done = s32[128,1,128]{2,1,0:T(1,128)S(1)} async-done(((s32[128,1,128]{2,1,0:T(1,128)}), s32[128,1,128]{2,1,0:T(1,128)S(1)}, u32[]{:S(2)}, u32[]{:S(2)}) %all-to-all-start) | async-done | bytes 65568 | tf_op jit(solution)/shard_map/all_to_all | solution.py:328
  23.4 0.0 copy-start.2
  23.4 0.0 copy-start.3
  23.4 0.0 copy-start
  23.4 0.0 copy-start.1
  23.4 5.7 %shard_map.122 = bf16[2048,128]{1,0:T(8,128)(2,1)} custom-call(s32[128,128]{1,0:T(8,128)S(1)} %bitcast.22, bf16[6144,2,128]{2,1,0:T(2,128)(2,1)S(1)} %shard_map.121.held_ref, bf16[8192,2,128]{2,1,0:T(2,128)(2,1)} %bitcast.25), custom_call_target="tpu_custom_call" | custom-call | tf_op jit(solution)/shard_map/pallas_call | solution.py:372
  29.1 4.8 %all-to-all-start.1 = ((bf16[128,16,128]{2,1,0:T(8,128)(2,1)}), bf16[128,16,128]{2,1,0:T(8,128)(2,1)S(1)}, u32[]{:S(2)}, u32[]{:S(2)}) async-start(bf16[128,16,128]{2,1,0:T(8,128)(2,1)} %bitcast.26), calls=%async_computation.1 | async-start | bytes 1048576 | tf_op jit(solution)/shard_map/all_to_all | solution.py:328
  33.9 0.7 copy.18.labels_ref
  34.6 0.0 copy-done.2
  34.6 0.0 copy-done.3
  34.6 3.9 %shard_map.119 = (bf16[1024,128]{1,0:T(8,128)(2,1)S(1)}, f32[1024,128]{1,0:T(8,128)S(1)}, bf16[512,512]{1,0:T(8,128)(2,1)S(1)}) custom-call(s32[32,32]{1,0:T(8,128)S(1)} %copy-done.2, f32[32,32]{1,0:T(8,128)S(1)} %copy-done.3, bf16[512,512]{1,0:T(8,128)(2,1)} %second_hbm.1), custom_call_target="tpu_custom_call" | custom-call | tf_op jit(solution)/shard_map/pallas_call | solution.py:362
  38.6 9.0 %all-to-all-done.1 = bf16[128,16,128]{2,1,0:T(8,128)(2,1)S(1)} async-done(((bf16[128,16,128]{2,1,0:T(8,128)(2,1)}), bf16[128,16,128]{2,1,0:T(8,128)(2,1)S(1)}, u32[]{:S(2)}, u32[]{:S(2)}) %all-to-all-start.1) | async-done | bytes 524320 | tf_op jit(solution)/shard_map/all_to_all | solution.py:328
  47.6 0.0 copy-done
  47.6 0.0 copy-done.1
  47.6 4.2 %shard_map.123 = (f32[32,172]{1,0:T(8,128)}, bf16[1664,128]{1,0:T(8,128)(2,1)S(1)}, f32[8,128]{1,0:T(8,128)S(1)}, bf16[1024,128]{1,0:T(8,128)(2,1)S(1)}, bf16[10...) custom-call(s32[1]{0:T(128)} %bitcast.core_ref, ...), custom_call_target="tpu_custom_call" | custom-call | tf_op jit(solution)/shard_map/pallas_call | solution.py:395
  51.7 1.2 %collective-permute-start = (bf16[1664,128]{1,0:T(8,128)(2,1)S(1)}, bf16[1664,128]{1,0:T(8,128)(2,1)S(1)}, u32[]{:S(2)}, u32[]{:S(2)}) collective-permute-start(bf16[1664,128]{1,0:T(8,128)(2,1)S(1)} %get-tuple-element.34), channel_id=1, source_target_pairs={{0,1},{1,0},{2,3},{3,2},{4,5},{5,4},{6,7},{7,6},{8,9},{9,8},{10,11... | collective-permute-start | bytes 1277960 | tf_op jit(solution)/shard_map/ppermute | solution.py:410
  53.0 0.7 shard_map.124
  53.7 0.7 collective-permute-done
  54.4 0.1 add_convert_fusion
  54.5 15.4 %all_to_all.20 = bf16[832,2,128]{2,1,0:T(2,128)(2,1)S(1)} all-to-all(bf16[832,2,128]{2,1,0:T(2,128)(2,1)S(1)} %bitcast.27), channel_id=1, replica_groups=mesh['nodes_0'=4,'nodes_1'=4,'nodes_2'=4,'nodes_3'=2] {'nodes_0','nodes_..., dimensions={0} | all-to-all | bytes 851968 | tf_op jit(solution)/shard_map/all_to_all | solution.py:328
  69.9 0.5 shard_map.125
  70.4 14.9 %all_to_all.21 = bf16[832,2,128]{2,1,0:T(2,128)(2,1)S(1)} all-to-all(bf16[832,2,128]{2,1,0:T(2,128)(2,1)S(1)} %bitcast.21), channel_id=1, replica_groups=mesh['nodes_0'=4,'nodes_1'=4,'nodes_2'=4,'nodes_3'=2] {'nodes_0','nodes_..., dimensions={0} | all-to-all | bytes 851968 | tf_op jit(solution)/shard_map/all_to_all | solution.py:328
  85.2 3.1 %collective-permute-start.1 = (bf16[1664,128]{1,0:T(8,128)(2,1)S(1)}, bf16[1664,128]{1,0:T(8,128)(2,1)S(1)}, u32[]{:S(2)}, u32[]{:S(2)}) collective-permute-start(bf16[1664,128]{1,0:T(8,128)(2,1)S(1)} %bitcast.16), channel_id=1, source_target_pairs={{0,1},{1,0},{2,3},{3,2},{4,5},{5,4},{6,7},{7,6},{8,9},{9,8},{10,11... | collective-permute-start | bytes 1277960 | tf_op jit(solution)/shard_map/ppermute | solution.py:416
  88.4 0.9 %shard_map.126 = (f32[128,512]{1,0:T(8,128)}, f32[512,512]{1,0:T(8,128)}, f32[172,512]{1,0:T(8,128)}) custom-call(s32[1]{0:T(128)} %bitcast.core_ref, bf16[1664,128]{1,0:T(8,128)(2,1)S(1)} %bitcast.17), custom_call_target="tpu_custom_call" | custom-call | tf_op jit(solution)/shard_map/pallas_call | solution.py:420
  89.3 0.5 collective-permute-done.1.other_ref
  89.8 1.4 %shard_map.127 = (f32[1,1]{1,0:T(1,128)}, f32[128,512]{1,0:T(8,128)}, f32[512,512]{1,0:T(8,128)}, f32[172,512]{1,0:T(8,128)}) custom-call(s32[1]{0:T(128)} %bitcast.core_ref, bf16[1664,128]{1,0:T(8,128)(2,1)S(1)} %bitcast.18, bf16[1664,128]{1,0:T(8,128)(2,1)S(1)} %collective-permute-done.1.other_ref, ...), custom_call_target="tpu_custom_call", output_to_operand_aliasing={{1}: (3, {}), {2}: (4, {}), {3}: (5, {})} | custom-call | tf_op jit(solution)/shard_map/pallas_call | solution.py:421
Async XLA Ops:
  2.6 20.8 %all-to-all-start = ((s32[128,1,128]{2,1,0:T(1,128)}), s32[128,1,128]{2,1,0:T(1,128)S(1)}, u32[]{:S(2)}, u32[]{:S(2)}) async-start(s32[128,1,128]{2,1,0:T(1,128)} %bitcast.2), calls=%async_computation | async-start | bytes 131072 | tf_op jit(solution)/shard_map/all_to_all | solution.py:328
  23.4 11.2 %copy-start.2 = (s32[32,32]{1,0:T(8,128)S(1)}, s32[32,32]{1,0:T(8,128)}, u32[]{:S(2)}) copy-start(s32[32,32]{1,0:T(8,128)} %owner_hbm.1) | copy-start | bytes 12292
  23.4 11.2 %copy-start.3 = (f32[32,32]{1,0:T(8,128)S(1)}, f32[32,32]{1,0:T(8,128)}, u32[]{:S(2)}) copy-start(f32[32,32]{1,0:T(8,128)} %weight_ref.1) | copy-start | bytes 12292
  23.4 24.2 %copy-start = (bf16[512,172]{0,1:T(8,128)(2,1)S(1)}, bf16[512,172]{0,1:T(8,128)(2,1)}, u32[]{:S(2)}) copy-start(bf16[512,172]{0,1:T(8,128)(2,1)} %param.15) | copy-start | bytes 528388
  23.4 24.2 %copy-start.1 = (bf16[128,512]{1,0:T(8,128)(2,1)S(1)}, bf16[128,512]{1,0:T(8,128)(2,1)}, u32[]{:S(2)}) copy-start(bf16[128,512]{1,0:T(8,128)(2,1)} %first_ref.1) | copy-start | bytes 393220
  29.1 18.5 %all-to-all-start.1 = ((bf16[128,16,128]{2,1,0:T(8,128)(2,1)}), bf16[128,16,128]{2,1,0:T(8,128)(2,1)S(1)}, u32[]{:S(2)}, u32[]{:S(2)}) async-start(bf16[128,16,128]{2,1,0:T(8,128)(2,1)} %bitcast.26), calls=%async_computation.1 | async-start | bytes 1048576 | tf_op jit(solution)/shard_map/all_to_all | solution.py:328
  51.7 2.6 %collective-permute-start = (bf16[1664,128]{1,0:T(8,128)(2,1)S(1)}, bf16[1664,128]{1,0:T(8,128)(2,1)S(1)}, u32[]{:S(2)}, u32[]{:S(2)}) collective-permute-start(bf16[1664,128]{1,0:T(8,128)(2,1)S(1)} %get-tuple-element.34), channel_id=1, source_target_pairs={{0,1},{1,0},{2,3},{3,2},{4,5},{5,4},{6,7},{7,6},{8,9},{9,8},{10,11... | collective-permute-start | bytes 1277960 | tf_op jit(solution)/shard_map/ppermute | solution.py:410
  85.2 4.5 %collective-permute-start.1 = (bf16[1664,128]{1,0:T(8,128)(2,1)S(1)}, bf16[1664,128]{1,0:T(8,128)(2,1)S(1)}, u32[]{:S(2)}, u32[]{:S(2)}) collective-permute-start(bf16[1664,128]{1,0:T(8,128)(2,1)S(1)} %bitcast.16), channel_id=1, source_target_pairs={{0,1},{1,0},{2,3},{3,2},{4,5},{5,4},{6,7},{7,6},{8,9},{9,8},{10,11... | collective-permute-start | bytes 1277960 | tf_op jit(solution)/shard_map/ppermute | solution.py:416

commit v4 on v3

--- a/solution.py
+++ b/solution.py
@@ -107,7 +107,7 @@
 
 
 def serve_body(
-    capacity, asked_ref, held_ref, pairs_hbm, rows_hbm, rows_ref, pairs_ref, stage_ref, turned_ref, index_ref, arrivals, leaving
+    capacity, asked_ref, held_ref, pairs_hbm, rows_hbm, rows_ref, pairs_ref, stage_ref, wide_ref, turned_ref, index_ref, arrivals, leaving
 ):
     held, pairs = held_ref.shape[0], pairs_ref.shape[0]
     rest = pl.ds(held, pairs - held)
@@ -115,42 +115,33 @@
     far = pltpu.make_async_copy(pairs_hbm.at[rest], pairs_ref.at[rest], arrivals.at[1])
     far.start()
     near.start()
-    asked = asked_ref[...].T[:capacity, :]
-    turned_ref[...] = asked >> 1
-    odd = (asked & 1).astype(f32)
+    asked = asked_ref[...]
+    turned_ref[...] = asked.T[:capacity, :] >> 1
     index = pltpu.make_async_copy(turned_ref, index_ref, arrivals.at[2])
     index.start()
     index.wait()
     near.wait()
     far.wait()
-    sources = asked.shape[1]
-    together = stage_ref.shape[0] // (2 * capacity)
-
-    def some(step, carry):
-        for j in range(together):
-            source = step * together + j
-            low = 2 * j * capacity
-            for p in range(capacity):
-                stage_ref[low + 2 * p : low + 2 * p + 2, :] = pairs_ref[index_ref[p, source]].astype(f32)
-            later = jnp.broadcast_to(pltpu.roll(odd, sources - source, 1)[:, 0:1], (capacity, stage_ref.shape[1])) > 0
-            first = stage_ref[pl.ds(low, capacity, stride=2), :]
-            second = stage_ref[pl.ds(low + 1, capacity, stride=2), :]
-            base = pl.multiple_of(source * capacity, capacity)
-            rows_ref[pl.ds(base, capacity), :] = jnp.where(later, second, first).astype(bf16)
-        out(step).start()
-        return carry
-
-    def out(step):
-        size = together * capacity
-        span = pl.ds(pl.multiple_of(step * size, size), size)
-        return pltpu.make_async_copy(rows_ref.at[span], rows_hbm.at[span], leaving.at[step])
-
-    def last(step, carry):
-        out(step).wait()
-        return carry
-
-    lax.fori_loop(0, sources // together, some, 0)
-    lax.fori_loop(0, sources // together, last, 0)
+    odd = (asked & 1) > 0
+    sources, width = asked.shape[0], stage_ref.shape[2]
+    together = capacity // leaving.shape[0]
+    copies = []
+    for group in range(leaving.shape[0]):
+        for p in range(group * together, (group + 1) * together):
+            stage = stage_ref.at[p % stage_ref.shape[0]]
+            for source in range(sources):
+                stage[2 * source : 2 * source + 2, :] = pairs_ref[index_ref[p, source]].astype(f32)
+            first = stage[pl.ds(0, sources, stride=2), :]
+            second = stage[pl.ds(1, sources, stride=2), :]
+            at = pl.ds(p - group * together, sources, stride=together)
+            wide_ref[group, at, :] = jnp.where(odd[:, p : p + 1], second, first)
+        ready = wide_ref[group].reshape(sources, together, width).astype(bf16)
+        rows_ref[group] = ready
+        span = pl.ds(group * together, together)
+        copies.append(pltpu.make_async_copy(rows_ref.at[group], rows_hbm.at[:, span, :], leaving.at[group]))
+        copies[-1].start()
+    for copy in copies:
+        copy.wait()
 
 
 def step_body(
@@ -196,13 +187,19 @@
                 ref[h, r, :] = part[:, h * wide : (h + 1) * wide]
 
     slots = arrived_ref.shape[0]
-    every_code = coded_slots(iota((16, slots), 1)).astype(bf16)
+    side = slots // 2
+    arrived = jnp.concatenate([arrived_ref[:side, :], arrived_ref[side:, :]], axis=1)
+    every_code = coded_slots(iota((16, side), 1)).astype(bf16)
     every_code = jnp.concatenate([every_code] * (size // 16), axis=0)
+    bound = float(128 << (side >> 7))
     x = []
     for r in own_rows:
-        code = jnp.concatenate([codes_ref[r, :]] * (slots // LANES), axis=1)
+        late = codes_ref[r, :] >= jnp.asarray(bound, bf16)
+        code = jnp.where(late, codes_ref[r, :] * jnp.asarray(128.0 / bound, bf16), codes_ref[r, :])
+        code = jnp.concatenate([code] * (side // LANES), axis=1)
         pick = jnp.where(code == every_code, jnp.ones((), bf16), zero)
-        x.append(dot(pick, arrived_ref[...]).astype(bf16))
+        both = dot(pick, arrived).astype(bf16)
+        x.append(jnp.where(late, both[:, LANES:], both[:, :LANES]))
         x_ref[r, :] = x[-1]
     first_act = [rectified(dot(part, first_ref[...])) for part in x]
     second_act = [rectified(dot(part, second_ref[...])) for part in first_act]
@@ -371,21 +368,22 @@
     )(nbr_owner, ppr_weight, pltpu.with_memory_space_constraint(w_second, pltpu.HBM))
     served = call(
         functools.partial(serve_body, capacity),
-        pltpu.HBM((slots, width), bf16),
+        pltpu.HBM((groups, capacity, width), bf16),
         [VMEM, VMEM, FAR],
         [
-            pltpu.VMEM((slots, width), bf16),
+            pltpu.VMEM((2, groups, capacity // 2, width), bf16),
             pltpu.VMEM(pairs.shape, bf16),
-            pltpu.VMEM((8 * 2 * capacity, width), f32),
+            pltpu.VMEM((2, 2 * groups, width), f32),
+            pltpu.VMEM((2, groups * capacity // 2, width), f32),
             pltpu.VMEM((capacity, groups), i32),
             pltpu.SMEM((capacity, groups), i32),
             pltpu.SemaphoreType.DMA((3,)),
-            pltpu.SemaphoreType.DMA((groups // 8,)),
+            pltpu.SemaphoreType.DMA((2,)),
         ],
         16,
         FAR,
     )(asked, held, pairs)
-    arrived = everywhere(served.reshape(groups, capacity, width), NODES).reshape(slots, width)
+    arrived = everywhere(served, NODES).reshape(slots, width)
 
     rows = seeds * neighbours
     half = hidden // 2

time: 91.7 us -> 89.3 us (0.974)
  Pallas kernels: 21.2 us -> 18.8 us
    pallas_call x1, Pallas kernels: 5.69 us -> 3.86 us  [on_device(): call(functools.partial(serve_body, capacity), pltpu.HBM((groups, capacity...]
where the time goes in v4:
time: 89.3 us; the launch traced here: 88.9 us
  blocking collectives  30.3 us (34%)
  starting transfers between devices  20.6 us (23%)
  Pallas kernels  18.8 us (21%)
  waiting for transfers between devices  17.6 us (20%)
    all_to_all x2, blocking collectives, everywhere(): return lax.all_to_all(parts, axis, 0, 0, tiled=True)  30.3 us
    all_to_all x2, waiting for transfers between devices, everywhere(): return lax.all_to_all(parts, axis, 0, 0, tiled=True)  16.4 us
    all_to_all x2, starting transfers between devices, everywhere(): return lax.all_to_all(parts, axis, 0, 0, tiled=True)  16.3 us
    pallas_call x1, Pallas kernels, on_device(): call(functools.partial(spread_body, capacity, groups), (shape((seeds * ne...  3.93 us
    pallas_call x1, Pallas kernels, on_device(): call(functools.partial(serve_body, capacity), pltpu.HBM((groups, capacity...  3.86 us
    pallas_call x1, Pallas kernels, on_device(): call(functools.partial(step_body, total_seeds, 2), (shape((seeds, classes...  3.62 us
    ppermute x1, starting transfers between devices, on_device(): other = lax.ppermute(own, CORE, swap)  3.15 us
    pallas_call x1, Pallas kernels, on_device(): call(functools.partial(request_body, capacity), shape((groups, LANES), i3...  1.97 us
  transfers between devices with their start and end apart: 4, of which 4 were waited for; matrix products, arithmetic and copies ran while one was open for 1% of the time, Pallas kernels for 8%

profile of v4, /device:TPU:1, one launch (start us, length us, event | category | flops | bytes accessed | tf_op | source)
XLA Modules:
  0.0 88.9 jit_solution(5706051296553050035)
XLA Ops:
  0.6 2.0 %shard_map.120 = s32[128,128]{1,0:T(8,128)} custom-call(s32[32,32]{1,0:T(8,128)} %owner_hbm.1, s32[32,32]{1,0:T(8,128)} %local_hbm.1), custom_call_target="tpu_custom_call" | custom-call | tf_op jit(solution)/shard_map/pallas_call | solution.py:341
  2.6 11.5 %all-to-all-start = ((s32[128,1,128]{2,1,0:T(1,128)}), s32[128,1,128]{2,1,0:T(1,128)S(1)}, u32[]{:S(2)}, u32[]{:S(2)}) async-start(s32[128,1,128]{2,1,0:T(1,128)} %bitcast.2), calls=%async_computation | async-start | bytes 131072 | tf_op jit(solution)/shard_map/all_to_all | solution.py:325
  14.1 1.9 %shard_map.121.held_ref = bf16[6144,2,128]{2,1,0:T(2,128)(2,1)S(1)} custom-call(bf16[8192,2,128]{2,1,0:T(2,128)(2,1)} %bitcast.23), custom_call_target="tpu_custom_call" | custom-call | tf_op jit(solution)/shard_map/pallas_call | solution.py:353
  16.0 7.4 %all-to-all-done = s32[128,1,128]{2,1,0:T(1,128)S(1)} async-done(((s32[128,1,128]{2,1,0:T(1,128)}), s32[128,1,128]{2,1,0:T(1,128)S(1)}, u32[]{:S(2)}, u32[]{:S(2)}) %all-to-all-start) | async-done | bytes 65568 | tf_op jit(solution)/shard_map/all_to_all | solution.py:325
  23.4 0.0 copy-start.2
  23.4 0.0 copy-start.3
  23.4 0.0 copy-start
  23.4 0.0 copy-start.1
  23.4 3.9 %shard_map.122 = bf16[128,16,128]{2,1,0:T(8,128)(2,1)} custom-call(s32[128,128]{1,0:T(8,128)S(1)} %bitcast.21, bf16[6144,2,128]{2,1,0:T(2,128)(2,1)S(1)} %shard_map.121.held_ref, bf16[8192,2,128]{2,1,0:T(2,128)(2,1)} %bitcast.24), custom_call_target="tpu_custom_call" | custom-call | tf_op jit(solution)/shard_map/pallas_call | solution.py:369
  27.3 4.8 %all-to-all-start.1 = ((bf16[128,16,128]{2,1,0:T(8,128)(2,1)}), bf16[128,16,128]{2,1,0:T(8,128)(2,1)S(1)}, u32[]{:S(2)}, u32[]{:S(2)}) async-start(bf16[128,16,128]{2,1,0:T(8,128)(2,1)} %shard_map.122), calls=%async_computation.1 | async-start | bytes 1048576 | tf_op jit(solution)/shard_map/all_to_all | solution.py:325
  32.1 0.7 copy.18.labels_ref
  32.8 0.0 copy-done.2
  32.8 0.0 copy-done.3
  32.8 3.9 %shard_map.119 = (bf16[1024,128]{1,0:T(8,128)(2,1)S(1)}, f32[1024,128]{1,0:T(8,128)S(1)}, bf16[512,512]{1,0:T(8,128)(2,1)S(1)}) custom-call(s32[32,32]{1,0:T(8,128)S(1)} %copy-done.2, f32[32,32]{1,0:T(8,128)S(1)} %copy-done.3, bf16[512,512]{1,0:T(8,128)(2,1)} %second_hbm.1), custom_call_target="tpu_custom_call" | custom-call | tf_op jit(solution)/shard_map/pallas_call | solution.py:359
  36.7 9.0 %all-to-all-done.1 = bf16[128,16,128]{2,1,0:T(8,128)(2,1)S(1)} async-done(((bf16[128,16,128]{2,1,0:T(8,128)(2,1)}), bf16[128,16,128]{2,1,0:T(8,128)(2,1)S(1)}, u32[]{:S(2)}, u32[]{:S(2)}) %all-to-all-start.1) | async-done | bytes 524320 | tf_op jit(solution)/shard_map/all_to_all | solution.py:325
  45.8 0.0 copy-done
  45.8 0.0 copy-done.1
  45.8 3.6 %shard_map.123 = (f32[32,172]{1,0:T(8,128)}, bf16[1664,128]{1,0:T(8,128)(2,1)S(1)}, f32[8,128]{1,0:T(8,128)S(1)}, bf16[1024,128]{1,0:T(8,128)(2,1)S(1)}, bf16[10...) custom-call(s32[1]{0:T(128)} %bitcast.core_ref, ...), custom_call_target="tpu_custom_call" | custom-call | tf_op jit(solution)/shard_map/pallas_call | solution.py:393
  49.4 1.2 %collective-permute-start = (bf16[1664,128]{1,0:T(8,128)(2,1)S(1)}, bf16[1664,128]{1,0:T(8,128)(2,1)S(1)}, u32[]{:S(2)}, u32[]{:S(2)}) collective-permute-start(bf16[1664,128]{1,0:T(8,128)(2,1)S(1)} %get-tuple-element.34), channel_id=1, source_target_pairs={{0,1},{1,0},{2,3},{3,2},{4,5},{5,4},{6,7},{7,6},{8,9},{9,8},{10,11... | collective-permute-start | bytes 1277960 | tf_op jit(solution)/shard_map/ppermute | solution.py:408
  50.6 0.7 shard_map.124
  51.3 0.7 collective-permute-done
  52.0 0.1 add_convert_fusion
  52.1 15.4 %all_to_all.20 = bf16[832,2,128]{2,1,0:T(2,128)(2,1)S(1)} all-to-all(bf16[832,2,128]{2,1,0:T(2,128)(2,1)S(1)} %bitcast.25), channel_id=1, replica_groups=mesh['nodes_0'=4,'nodes_1'=4,'nodes_2'=4,'nodes_3'=2] {'nodes_0','nodes_..., dimensions={0} | all-to-all | bytes 851968 | tf_op jit(solution)/shard_map/all_to_all | solution.py:325
  67.5 0.5 shard_map.125
  68.0 14.9 %all_to_all.21 = bf16[832,2,128]{2,1,0:T(2,128)(2,1)S(1)} all-to-all(bf16[832,2,128]{2,1,0:T(2,128)(2,1)S(1)} %bitcast.20), channel_id=1, replica_groups=mesh['nodes_0'=4,'nodes_1'=4,'nodes_2'=4,'nodes_3'=2] {'nodes_0','nodes_..., dimensions={0} | all-to-all | bytes 851968 | tf_op jit(solution)/shard_map/all_to_all | solution.py:325
  82.9 3.2 %collective-permute-start.1 = (bf16[1664,128]{1,0:T(8,128)(2,1)S(1)}, bf16[1664,128]{1,0:T(8,128)(2,1)S(1)}, u32[]{:S(2)}, u32[]{:S(2)}) collective-permute-start(bf16[1664,128]{1,0:T(8,128)(2,1)S(1)} %bitcast.15), channel_id=1, source_target_pairs={{0,1},{1,0},{2,3},{3,2},{4,5},{5,4},{6,7},{7,6},{8,9},{9,8},{10,11... | collective-permute-start | bytes 1277960 | tf_op jit(solution)/shard_map/ppermute | solution.py:414
  86.0 0.9 %shard_map.126 = (f32[128,512]{1,0:T(8,128)}, f32[512,512]{1,0:T(8,128)}, f32[172,512]{1,0:T(8,128)}) custom-call(s32[1]{0:T(128)} %bitcast.core_ref, bf16[1664,128]{1,0:T(8,128)(2,1)S(1)} %bitcast.16), custom_call_target="tpu_custom_call" | custom-call | tf_op jit(solution)/shard_map/pallas_call | solution.py:418
  87.0 0.5 collective-permute-done.1.other_ref
  87.4 1.4 %shard_map.127 = (f32[1,1]{1,0:T(1,128)}, f32[128,512]{1,0:T(8,128)}, f32[512,512]{1,0:T(8,128)}, f32[172,512]{1,0:T(8,128)}) custom-call(s32[1]{0:T(128)} %bitcast.core_ref, bf16[1664,128]{1,0:T(8,128)(2,1)S(1)} %bitcast.17, bf16[1664,128]{1,0:T(8,128)(2,1)S(1)} %collective-permute-done.1.other_ref, ...), custom_call_target="tpu_custom_call", output_to_operand_aliasing={{1}: (3, {}), {2}: (4, {}), {3}: (5, {})} | custom-call | tf_op jit(solution)/shard_map/pallas_call | solution.py:419
Async XLA Ops:
  2.6 20.8 %all-to-all-start = ((s32[128,1,128]{2,1,0:T(1,128)}), s32[128,1,128]{2,1,0:T(1,128)S(1)}, u32[]{:S(2)}, u32[]{:S(2)}) async-start(s32[128,1,128]{2,1,0:T(1,128)} %bitcast.2), calls=%async_computation | async-start | bytes 131072 | tf_op jit(solution)/shard_map/all_to_all | solution.py:325
  23.4 9.4 %copy-start.2 = (s32[32,32]{1,0:T(8,128)S(1)}, s32[32,32]{1,0:T(8,128)}, u32[]{:S(2)}) copy-start(s32[32,32]{1,0:T(8,128)} %owner_hbm.1) | copy-start | bytes 12292
  23.4 9.4 %copy-start.3 = (f32[32,32]{1,0:T(8,128)S(1)}, f32[32,32]{1,0:T(8,128)}, u32[]{:S(2)}) copy-start(f32[32,32]{1,0:T(8,128)} %weight_ref.1) | copy-start | bytes 12292
  23.4 22.4 %copy-start = (bf16[512,172]{0,1:T(8,128)(2,1)S(1)}, bf16[512,172]{0,1:T(8,128)(2,1)}, u32[]{:S(2)}) copy-start(bf16[512,172]{0,1:T(8,128)(2,1)} %param.15) | copy-start | bytes 528388
  23.4 22.4 %copy-start.1 = (bf16[128,512]{1,0:T(8,128)(2,1)S(1)}, bf16[128,512]{1,0:T(8,128)(2,1)}, u32[]{:S(2)}) copy-start(bf16[128,512]{1,0:T(8,128)(2,1)} %first_ref.1) | copy-start | bytes 393220
  27.3 18.5 %all-to-all-start.1 = ((bf16[128,16,128]{2,1,0:T(8,128)(2,1)}), bf16[128,16,128]{2,1,0:T(8,128)(2,1)S(1)}, u32[]{:S(2)}, u32[]{:S(2)}) async-start(bf16[128,16,128]{2,1,0:T(8,128)(2,1)} %shard_map.122), calls=%async_computation.1 | async-start | bytes 1048576 | tf_op jit(solution)/shard_map/all_to_all | solution.py:325
  49.4 2.6 %collective-permute-start = (bf16[1664,128]{1,0:T(8,128)(2,1)S(1)}, bf16[1664,128]{1,0:T(8,128)(2,1)S(1)}, u32[]{:S(2)}, u32[]{:S(2)}) collective-permute-start(bf16[1664,128]{1,0:T(8,128)(2,1)S(1)} %get-tuple-element.34), channel_id=1, source_target_pairs={{0,1},{1,0},{2,3},{3,2},{4,5},{5,4},{6,7},{7,6},{8,9},{9,8},{10,11... | collective-permute-start | bytes 1277960 | tf_op jit(solution)/shard_map/ppermute | solution.py:408
  82.9 4.5 %collective-permute-start.1 = (bf16[1664,128]{1,0:T(8,128)(2,1)S(1)}, bf16[1664,128]{1,0:T(8,128)(2,1)S(1)}, u32[]{:S(2)}, u32[]{:S(2)}) collective-permute-start(bf16[1664,128]{1,0:T(8,128)(2,1)S(1)} %bitcast.15), channel_id=1, source_target_pairs={{0,1},{1,0},{2,3},{3,2},{4,5},{5,4},{6,7},{7,6},{8,9},{9,8},{10,11... | collective-permute-start | bytes 1277960 | tf_op jit(solution)/shard_map/ppermute | solution.py:414

commit v5 on v4

--- a/solution.py
+++ b/solution.py
@@ -31,12 +31,13 @@
 FAR = pl.BlockSpec(memory_space=pltpu.HBM)
 
 
-def call(body, outs, ins, scratch=(), megabytes=8, where=VMEM):
+def call(body, outs, ins, scratch=(), megabytes=8, where=VMEM, aliases=()):
     return pl.pallas_call(
         body,
         out_shape=outs,
         in_specs=ins,
-        out_specs=jax.tree.map(lambda _: where, outs),
+        out_specs=where if isinstance(where, tuple) else jax.tree.map(lambda _: where, outs),
+        input_output_aliases=dict(aliases),
         scratch_shapes=scratch,
         compiler_params=pltpu.CompilerParams(vmem_limit_bytes=megabytes << 20),
     )
@@ -57,13 +58,15 @@
     return named > 0, earlier, wanted
 
 
-def request_body(capacity, owner_hbm, local_hbm, table_ref, owner_ref, local_ref, arrivals):
+def request_body(capacity, owner_hbm, local_hbm, pairs_hbm, table_ref, pairs_ref, owner_ref, local_ref, arrivals):
     copies = [
         pltpu.make_async_copy(owner_hbm, owner_ref, arrivals.at[0]),
         pltpu.make_async_copy(local_hbm, local_ref, arrivals.at[1]),
     ]
     for copy in copies:
         copy.start()
+    pairs = pltpu.make_async_copy(pairs_hbm, pairs_ref, arrivals.at[2])
+    pairs.start()
     for copy in copies:
         copy.wait()
     groups = table_ref.shape[0]
@@ -76,16 +79,11 @@
         table = jnp.where(place[s : s + 1, :] == slot, wanted[s : s + 1, :], table)
     spare = jnp.zeros((LANES - capacity, groups), i32)
     table_ref[...] = jnp.concatenate([table, spare], axis=0).T
+    pairs.wait()
 
 
 def coded_slots(slot):
     return ((128 + (slot & 127)) * (1 << (slot >> 7))).astype(f32)
-
-
-def hold_body(pairs_hbm, held_ref, arrival):
-    copy = pltpu.make_async_copy(pairs_hbm.at[pl.ds(0, held_ref.shape[0])], held_ref, arrival)
-    copy.start()
-    copy.wait()
 
 
 def spread_body(capacity, groups, owner_ref, weight_ref, second_hbm, codes_ref, weights_ref, second_ref, arrival):
@@ -107,38 +105,28 @@
 
 
 def serve_body(
-    capacity, asked_ref, held_ref, pairs_hbm, rows_hbm, rows_ref, pairs_ref, stage_ref, wide_ref, turned_ref, index_ref, arrivals, leaving
+    capacity, asked_ref, pairs_ref, rows_hbm, rows_ref, stage_ref, wide_ref, turned_ref, index_ref, arrival, leaving
 ):
-    held, pairs = held_ref.shape[0], pairs_ref.shape[0]
-    rest = pl.ds(held, pairs - held)
-    near = pltpu.make_async_copy(held_ref, pairs_ref.at[pl.ds(0, held)], arrivals.at[0])
-    far = pltpu.make_async_copy(pairs_hbm.at[rest], pairs_ref.at[rest], arrivals.at[1])
-    far.start()
-    near.start()
     asked = asked_ref[...]
     turned_ref[...] = asked.T[:capacity, :] >> 1
-    index = pltpu.make_async_copy(turned_ref, index_ref, arrivals.at[2])
+    index = pltpu.make_async_copy(turned_ref, index_ref, arrival)
     index.start()
     index.wait()
-    near.wait()
-    far.wait()
     odd = (asked & 1) > 0
-    sources, width = asked.shape[0], stage_ref.shape[2]
-    together = capacity // leaving.shape[0]
+    groups = leaving.shape[0]
+    size = asked.shape[0] // groups
     copies = []
-    for group in range(leaving.shape[0]):
-        for p in range(group * together, (group + 1) * together):
+    for group in range(groups):
+        span = slice(group * size, (group + 1) * size)
+        for p in range(capacity):
             stage = stage_ref.at[p % stage_ref.shape[0]]
-            for source in range(sources):
-                stage[2 * source : 2 * source + 2, :] = pairs_ref[index_ref[p, source]].astype(f32)
-            first = stage[pl.ds(0, sources, stride=2), :]
-            second = stage[pl.ds(1, sources, stride=2), :]
-            at = pl.ds(p - group * together, sources, stride=together)
-            wide_ref[group, at, :] = jnp.where(odd[:, p : p + 1], second, first)
-        ready = wide_ref[group].reshape(sources, together, width).astype(bf16)
-        rows_ref[group] = ready
-        span = pl.ds(group * together, together)
-        copies.append(pltpu.make_async_copy(rows_ref.at[group], rows_hbm.at[:, span, :], leaving.at[group]))
+            for source in range(size):
+                stage[2 * source : 2 * source + 2, :] = pairs_ref[index_ref[p, span.start + source]].astype(f32)
+            first = stage[pl.ds(0, size, stride=2), :]
+            second = stage[pl.ds(1, size, stride=2), :]
+            wide_ref[group, pl.ds(p, size, stride=capacity), :] = jnp.where(odd[span, p : p + 1], second, first)
+        rows_ref[span] = wide_ref[group].reshape(size, capacity, -1).astype(bf16)
+        copies.append(pltpu.make_async_copy(rows_ref.at[span], rows_hbm.at[span], leaving.at[group]))
         copies[-1].start()
     for copy in copies:
         copy.wait()
@@ -155,7 +143,7 @@
     first_ref,
     second_ref,
     third_t_ref,
-    logits_ref,
+    logits_hbm,
     send_ref,
     terms_ref,
     x_ref,
@@ -165,6 +153,8 @@
     second_grad_ref,
     first_grad_ref,
     grads_ref,
+    logits_ref,
+    leaving,
 ):
     seeds, classes = logits_ref.shape
     rows = codes_ref.shape[0]
@@ -221,18 +211,22 @@
         every = jnp.broadcast_to(logit_grad[:, None, :], (seed_size, neighbours, classes)).reshape(size, classes)
         weighted.append((weight * every).astype(bf16))
         weighted_ref[r, :] = weighted[-1]
+    logits_copy = pltpu.make_async_copy(logits_ref, logits_hbm, leaving)
+    logits_copy.start()
     second_grad = [masked(a, dot(g, third_t_ref[...])) for a, g in zip(second_act, weighted)]
     halves(second_grad_ref, second_grad)
     first_grad = [masked(a, dot(g, second_ref[...], ((1,), (1,)))) for a, g in zip(first_act, second_grad)]
     halves(first_grad_ref, first_grad)
     diagonal = iota((seeds, LANES), 0) == iota((seeds, LANES), 1)
     loss_row = jnp.sum(jnp.where(diagonal, jnp.concatenate(terms, axis=0), 0.0), axis=0, keepdims=True)
+    loss_row = loss_row.astype(bf16).astype(f32)
     terms_ref[...] = jnp.broadcast_to(loss_row, terms_ref.shape)
     other = 1 - core_ref[0]
     write_half(
         grads_ref, loss_row, x_ref, first_act_ref, weighted_ref, second_act_ref, second_grad_ref, first_grad_ref, other
     )
     send_ref[...] = grads_ref[...].astype(bf16)
+    logits_copy.wait()
 
 
 def write_half(out_ref, loss_row, x_ref, first_act_ref, weighted_ref, second_act_ref, second_grad_ref, first_grad_ref, half):
@@ -295,30 +289,16 @@
         copy.wait()
 
 
-def own_body(core_ref, own_ref, first_hbm, second_hbm, third_t_hbm, *scratch):
-    columns(core_ref[0], own_ref, (first_hbm, second_hbm, third_t_hbm), scratch[:3], scratch[3])
-
-
-def other_body(
-    total_seeds,
-    core_ref,
-    own_ref,
-    other_ref,
-    given_first,
-    given_second,
-    given_third_t,
-    loss_ref,
-    first_hbm,
-    second_hbm,
-    third_t_hbm,
-    *scratch,
-):
-    del given_first, given_second, given_third_t
+def own_body(total_seeds, core_ref, own_ref, first_hbm, second_hbm, third_t_hbm, loss_ref, *scratch):
     outs = (first_hbm, second_hbm, third_t_hbm)
     at = sum(out.shape[0] for out in outs)
-    low = jnp.where(core_ref[0] == 0, own_ref[at : at + 1, :].astype(f32), other_ref[at : at + 1, :].astype(f32))
-    loss_ref[...] = jnp.sum(low, axis=1, keepdims=True) / total_seeds
-    columns(1 - core_ref[0], other_ref, outs, scratch[:3], scratch[3])
+    loss_ref[...] = jnp.sum(own_ref[at : at + 1, :].astype(f32), axis=1, keepdims=True) / total_seeds
+    columns(core_ref[0], own_ref, outs, scratch[:3], scratch[3])
+
+
+def other_body(core_ref, other_ref, given_first, given_second, given_third_t, first_hbm, second_hbm, third_t_hbm, *scratch):
+    del given_first, given_second, given_third_t
+    columns(1 - core_ref[0], other_ref, (first_hbm, second_hbm, third_t_hbm), scratch[:3], scratch[3])
 
 
 def everywhere(parts, axis):
@@ -338,24 +318,18 @@
     core = lax.axis_index(CORE).astype(i32).reshape(1)
     swap = [(0, 1), (1, 0)]
 
-    table = call(
+    pairs = features.reshape(-1, 2, width)
+    table, pairs = call(
         functools.partial(request_body, capacity),
-        shape((groups, LANES), i32),
-        [FAR, FAR],
+        (shape((groups, LANES), i32), pltpu.VMEM(pairs.shape, bf16)),
+        [FAR] * 3,
         [
             pltpu.VMEM((seeds, neighbours), i32),
             pltpu.VMEM((seeds, neighbours), i32),
-            pltpu.SemaphoreType.DMA((2,)),
+            pltpu.SemaphoreType.DMA((3,)),
         ],
-    )(*(pltpu.with_memory_space_constraint(a, pltpu.HBM) for a in (nbr_owner, nbr_local)))
+    )(*(pltpu.with_memory_space_constraint(a, pltpu.HBM) for a in (nbr_owner, nbr_local, pairs)))
     asked = everywhere(table.reshape(groups, 1, LANES), NODES).reshape(groups, LANES)
-    pairs = pltpu.with_memory_space_constraint(features.reshape(-1, 2, width), pltpu.HBM)
-    held = call(
-        hold_body,
-        pltpu.VMEM((pairs.shape[0] * 3 // 4, 2, width), bf16),
-        [FAR],
-        [pltpu.SemaphoreType.DMA],
-    )(pairs)
     codes, weights, second = call(
         functools.partial(spread_body, capacity, groups),
         (
@@ -369,20 +343,19 @@
     served = call(
         functools.partial(serve_body, capacity),
         pltpu.HBM((groups, capacity, width), bf16),
-        [VMEM, VMEM, FAR],
+        [VMEM, VMEM],
         [
-            pltpu.VMEM((2, groups, capacity // 2, width), bf16),
-            pltpu.VMEM(pairs.shape, bf16),
-            pltpu.VMEM((2, 2 * groups, width), f32),
-            pltpu.VMEM((2, groups * capacity // 2, width), f32),
+            pltpu.VMEM((groups, capacity, width), bf16),
+            pltpu.VMEM((4, 2 * groups // 4, width), f32),
+            pltpu.VMEM((4, groups * capacity // 4, width), f32),
             pltpu.VMEM((capacity, groups), i32),
             pltpu.SMEM((capacity, groups), i32),
-            pltpu.SemaphoreType.DMA((3,)),
-            pltpu.SemaphoreType.DMA((2,)),
+            pltpu.SemaphoreType.DMA,
+            pltpu.SemaphoreType.DMA((4,)),
         ],
         16,
         FAR,
-    )(asked, held, pairs)
+    )(asked, pairs)
     arrived = everywhere(served, NODES).reshape(slots, width)
 
     rows = seeds * neighbours
@@ -393,7 +366,7 @@
     seed_logits, send, *kept = call(
         functools.partial(step_body, total_seeds, 2),
         (
-            shape((seeds, classes), f32),
+            pltpu.HBM((seeds, classes), f32),
             shape(grads, bf16),
             shape((8, LANES), f32),
             shape((rows, width), bf16),
@@ -402,8 +375,9 @@
             *(shape((2, rows, half), bf16) for _ in range(3)),
         ),
         [SMEM] + [VMEM] * 7,
-        [pltpu.VMEM(grads, f32)],
+        [pltpu.VMEM(grads, f32), pltpu.VMEM((seeds, classes), f32), pltpu.SemaphoreType.DMA],
         32,
+        (FAR, *[VMEM] * 8),
     )(core, codes, arrived, weights, labels.reshape(-1, 1), w_first, second, w_third.T)
     near = lax.ppermute(send, CORE, swap)
     keep = call(keep_body, shape(grads, f32), [SMEM] + [VMEM] * 7, (), 16)(core, *kept)
@@ -415,16 +389,17 @@
     sizes = (width, hidden, classes)
     scratch = [*(pltpu.VMEM((n, half), f32) for n in sizes), pltpu.SemaphoreType.DMA((3,))]
     sums = tuple(pltpu.HBM((n, hidden), f32) for n in sizes)
-    started = call(own_body, sums, [SMEM, VMEM], scratch, 8, FAR)(core, own)
-    loss, grad_first, grad_second, grad_third_t = pl.pallas_call(
-        functools.partial(other_body, total_seeds),
-        out_shape=(shape((1, 1), f32), *sums),
-        in_specs=[SMEM, VMEM, VMEM, FAR, FAR, FAR],
-        out_specs=(VMEM, FAR, FAR, FAR),
-        scratch_shapes=scratch,
-        input_output_aliases={3: 1, 4: 2, 5: 3},
-        compiler_params=pltpu.CompilerParams(vmem_limit_bytes=8 << 20),
-    )(core, own, other, *started)
+    *started, loss = call(
+        functools.partial(own_body, total_seeds),
+        (*sums, shape((1, 1), f32)),
+        [SMEM, VMEM],
+        scratch,
+        8,
+        (FAR, FAR, FAR, VMEM),
+    )(core, own)
+    grad_first, grad_second, grad_third_t = call(
+        other_body, sums, [SMEM, VMEM, FAR, FAR, FAR], scratch, 8, FAR, {2: 0, 3: 1, 4: 2}
+    )(core, other, *started)
     return (loss.reshape(()), seed_logits, grad_first, grad_second, grad_third_t.T)
 
 

time: 89.3 us -> 88.3 us (0.989)
  blocking collectives: 30.3 us -> 51 us
  starting transfers between devices: 20.6 us -> 9.1 us
  waiting for transfers between devices: 17.6 us -> 10.4 us
  Pallas kernels: 18.8 us -> 16.6 us
    all_to_all x2 -> x3, blocking collectives: 30.3 us -> 51 us  [everywhere(): return lax.all_to_all(parts, axis, 0, 0, tiled=True)]
    all_to_all x2 -> x1, starting transfers between devices: 16.3 us -> 4.74 us  [everywhere(): return lax.all_to_all(parts, axis, 0, 0, tiled=True)]
    all_to_all x2 -> x1, waiting for transfers between devices: 16.4 us -> 9.67 us  [everywhere(): return lax.all_to_all(parts, axis, 0, 0, tiled=True)]
    pallas_call x5 -> x4, Pallas kernels: 9.84 us -> 8.24 us  [the longest x1 3.61 us: on_device(): call(functools.partial(step_body, total_seeds, 2), (pltpu.HBM((seeds, cla...]
  transfers between devices with their start and end apart: 4 -> 3, of which waited for: 4 -> 2; matrix products, arithmetic and copies ran while one was open for 1% -> 0% of each run, Pallas kernels for 8% -> 7%
where the time goes in v5:
time: 88.3 us; the launch traced here: 88 us
  blocking collectives  51 us (58%)
  Pallas kernels  16.6 us (19%)
  waiting for transfers between devices  10.4 us (12%)
  starting transfers between devices  9.1 us (10%)
    all_to_all x3, blocking collectives, everywhere(): return lax.all_to_all(parts, axis, 0, 0, tiled=True)  51 us
    all_to_all x1, waiting for transfers between devices, everywhere(): return lax.all_to_all(parts, axis, 0, 0, tiled=True)  9.67 us
    all_to_all x1, starting transfers between devices, everywhere(): return lax.all_to_all(parts, axis, 0, 0, tiled=True)  4.74 us
    pallas_call x1, Pallas kernels, on_device(): call(functools.partial(spread_body, capacity, groups), (shape((seeds * ne...  3.93 us
    pallas_call x1, Pallas kernels, on_device(): call(functools.partial(step_body, total_seeds, 2), (pltpu.HBM((seeds, cla...  3.61 us
    pallas_call x1, Pallas kernels, on_device(): call(functools.partial(serve_body, capacity), pltpu.HBM((groups, capacity...  3.27 us
    ppermute x1, starting transfers between devices, on_device(): other = lax.ppermute(own, CORE, swap)  3.15 us
    pallas_call x1, Pallas kernels, on_device(): call(functools.partial(request_body, capacity), (shape((groups, LANES), i...  2.27 us
  transfers between devices with their start and end apart: 3, of which 2 were waited for; matrix products, arithmetic and copies ran while one was open for 0% of the time, Pallas kernels for 7%

profile of v5, /device:TPU:1, one launch (start us, length us, event | category | flops | bytes accessed | tf_op | source)
XLA Modules:
  0.0 88.0 jit_solution(3415135634872095991)
XLA Ops:
  0.6 0.0 copy-start.4
  0.6 0.0 copy-start.2
  0.7 0.0 copy-start.3
  0.7 2.3 %shard_map.120 = (s32[128,128]{1,0:T(8,128)S(1)}, bf16[8192,2,128]{2,1,0:T(2,128)(2,1)S(1)}) custom-call(s32[32,32]{1,0:T(8,128)} %owner_hbm.1, s32[32,32]{1,0:T(8,128)} %local_hbm.1, bf16[8192,2,128]{2,1,0:T(2,128)(2,1)} %bitcast.23), custom_call_target="tpu_custom_call" | custom-call | tf_op jit(solution)/shard_map/pallas_call | solution.py:322
  2.9 0.0 copy-start
  2.9 0.0 copy-start.1
  3.0 20.7 %all_to_all.20 = s32[128,1,128]{2,1,0:T(1,128)S(1)} all-to-all(s32[128,1,128]{2,1,0:T(1,128)S(1)} %bitcast.22), channel_id=1, replica_groups=mesh['nodes_0'=4,'nodes_1'=4,'nodes_2'=4,'nodes_3'=2] {'nodes_0','nodes_..., dimensions={0} | all-to-all | bytes 131072 | tf_op jit(solution)/shard_map/all_to_all | solution.py:305
  23.6 3.3 %shard_map.121 = bf16[128,16,128]{2,1,0:T(8,128)(2,1)} custom-call(s32[128,128]{1,0:T(8,128)S(1)} %bitcast.20, bf16[8192,2,128]{2,1,0:T(2,128)(2,1)S(1)} %get-tuple-element.28.pairs_ref), custom_call_target="tpu_custom_call" | custom-call | tf_op jit(solution)/shard_map/pallas_call | solution.py:343
  26.9 4.7 %all-to-all-start.1 = ((bf16[128,16,128]{2,1,0:T(8,128)(2,1)}), bf16[128,16,128]{2,1,0:T(8,128)(2,1)S(1)}, u32[]{:S(2)}, u32[]{:S(2)}) async-start(bf16[128,16,128]{2,1,0:T(8,128)(2,1)} %shard_map.121), calls=%async_computation.1 | async-start | bytes 1048576 | tf_op jit(solution)/shard_map/all_to_all | solution.py:305
  31.7 0.0 copy-done.4
  31.7 0.1 copy.18.labels_ref
  31.8 0.0 copy-done.2
  31.8 0.0 copy-done.3
  31.8 3.9 %shard_map.119 = (bf16[1024,128]{1,0:T(8,128)(2,1)S(1)}, f32[1024,128]{1,0:T(8,128)S(1)}, bf16[512,512]{1,0:T(8,128)(2,1)S(1)}) custom-call(s32[32,32]{1,0:T(8,128)S(1)} %copy-done.2, f32[32,32]{1,0:T(8,128)S(1)} %copy-done.3, bf16[512,512]{1,0:T(8,128)(2,1)} %second_hbm.1), custom_call_target="tpu_custom_call" | custom-call | tf_op jit(solution)/shard_map/pallas_call | solution.py:333
  35.7 9.7 %all-to-all-done.1 = bf16[128,16,128]{2,1,0:T(8,128)(2,1)S(1)} async-done(((bf16[128,16,128]{2,1,0:T(8,128)(2,1)}), bf16[128,16,128]{2,1,0:T(8,128)(2,1)S(1)}, u32[]{:S(2)}, u32[]{:S(2)}) %all-to-all-start.1) | async-done | bytes 524320 | tf_op jit(solution)/shard_map/all_to_all | solution.py:305
  45.4 0.0 copy-done
  45.4 0.0 copy-done.1
  45.4 3.6 %shard_map.122 = (f32[32,172]{1,0:T(8,128)}, bf16[1664,128]{1,0:T(8,128)(2,1)S(1)}, f32[8,128]{1,0:T(8,128)S(1)}, bf16[1024,128]{1,0:T(8,128)(2,1)S(1)}, bf16[10...) custom-call(s32[1]{0:T(128)} %bitcast.core_ref, ...), custom_call_target="tpu_custom_call" | custom-call | tf_op jit(solution)/shard_map/pallas_call | solution.py:366
  49.0 1.2 %collective-permute-start = (bf16[1664,128]{1,0:T(8,128)(2,1)S(1)}, bf16[1664,128]{1,0:T(8,128)(2,1)S(1)}, u32[]{:S(2)}, u32[]{:S(2)}) collective-permute-start(bf16[1664,128]{1,0:T(8,128)(2,1)S(1)} %get-tuple-element.38), channel_id=1, source_target_pairs={{0,1},{1,0},{2,3},{3,2},{4,5},{5,4},{6,7},{7,6},{8,9},{9,8},{10,11... | collective-permute-start | bytes 1277960 | tf_op jit(solution)/shard_map/ppermute | solution.py:382
  50.2 0.7 shard_map.123
  50.9 0.7 collective-permute-done
  51.6 0.1 add_convert_fusion
  51.7 15.4 %all_to_all.21 = bf16[832,2,128]{2,1,0:T(2,128)(2,1)S(1)} all-to-all(bf16[832,2,128]{2,1,0:T(2,128)(2,1)S(1)} %bitcast.24), channel_id=1, replica_groups=mesh['nodes_0'=4,'nodes_1'=4,'nodes_2'=4,'nodes_3'=2] {'nodes_0','nodes_..., dimensions={0} | all-to-all | bytes 851968 | tf_op jit(solution)/shard_map/all_to_all | solution.py:305
  67.1 0.5 shard_map.124
  67.6 14.9 %all_to_all.22 = bf16[832,2,128]{2,1,0:T(2,128)(2,1)S(1)} all-to-all(bf16[832,2,128]{2,1,0:T(2,128)(2,1)S(1)} %bitcast.19), channel_id=1, replica_groups=mesh['nodes_0'=4,'nodes_1'=4,'nodes_2'=4,'nodes_3'=2] {'nodes_0','nodes_..., dimensions={0} | all-to-all | bytes 851968 | tf_op jit(solution)/shard_map/all_to_all | solution.py:305
  82.5 3.1 %collective-permute-start.1 = (bf16[1664,128]{1,0:T(8,128)(2,1)S(1)}, bf16[1664,128]{1,0:T(8,128)(2,1)S(1)}, u32[]{:S(2)}, u32[]{:S(2)}) collective-permute-start(bf16[1664,128]{1,0:T(8,128)(2,1)S(1)} %bitcast.16), channel_id=1, source_target_pairs={{0,1},{1,0},{2,3},{3,2},{4,5},{5,4},{6,7},{7,6},{8,9},{9,8},{10,11... | collective-permute-start | bytes 1277960 | tf_op jit(solution)/shard_map/ppermute | solution.py:388
  85.6 1.4 %shard_map.125 = (f32[128,512]{1,0:T(8,128)}, f32[512,512]{1,0:T(8,128)}, f32[172,512]{1,0:T(8,128)}, f32[1,1]{1,0:T(1,128)}) custom-call(s32[1]{0:T(128)} %bitcast.core_ref, bf16[1664,128]{1,0:T(8,128)(2,1)S(1)} %bitcast.17), custom_call_target="tpu_custom_call" | custom-call | tf_op jit(solution)/shard_map/pallas_call | solution.py:392
  87.1 0.0 collective-permute-done.1.other_ref
  87.1 0.9 %shard_map.126 = (f32[128,512]{1,0:T(8,128)}, f32[512,512]{1,0:T(8,128)}, f32[172,512]{1,0:T(8,128)}) custom-call(s32[1]{0:T(128)} %bitcast.core_ref, bf16[1664,128]{1,0:T(8,128)(2,1)S(1)} %collective-permute-done.1.other_ref, f32[128,512]{1,0:T(8,128)} %get-tuple-element.41.given_first, ...), custom_call_target="tpu_custom_call", output_to_operand_aliasing={{0}: (2, {}), {1}: (3, {}), {2}: (4, {})} | custom-call | tf_op jit(solution)/shard_map/pallas_call | solution.py:400
Async XLA Ops:
  0.6 31.0 %copy-start.4 = (s32[32]{0:T(128)S(1)}, s32[32]{0:T(128)}, u32[]{:S(2)}) copy-start(s32[32]{0:T(128)} %param.12) | copy-start | bytes 388
  0.6 31.1 %copy-start.2 = (s32[32,32]{1,0:T(8,128)S(1)}, s32[32,32]{1,0:T(8,128)}, u32[]{:S(2)}) copy-start(s32[32,32]{1,0:T(8,128)} %owner_hbm.1) | copy-start | bytes 12292
  0.7 31.1 %copy-start.3 = (f32[32,32]{1,0:T(8,128)S(1)}, f32[32,32]{1,0:T(8,128)}, u32[]{:S(2)}) copy-start(f32[32,32]{1,0:T(8,128)} %weight_ref.1) | copy-start | bytes 12292
  2.9 42.4 %copy-start = (bf16[512,172]{0,1:T(8,128)(2,1)S(1)}, bf16[512,172]{0,1:T(8,128)(2,1)}, u32[]{:S(2)}) copy-start(bf16[512,172]{0,1:T(8,128)(2,1)} %param.15) | copy-start | bytes 528388
  2.9 42.4 %copy-start.1 = (bf16[128,512]{1,0:T(8,128)(2,1)S(1)}, bf16[128,512]{1,0:T(8,128)(2,1)}, u32[]{:S(2)}) copy-start(bf16[128,512]{1,0:T(8,128)(2,1)} %first_ref.1) | copy-start | bytes 393220
  26.9 18.5 %all-to-all-start.1 = ((bf16[128,16,128]{2,1,0:T(8,128)(2,1)}), bf16[128,16,128]{2,1,0:T(8,128)(2,1)S(1)}, u32[]{:S(2)}, u32[]{:S(2)}) async-start(bf16[128,16,128]{2,1,0:T(8,128)(2,1)} %shard_map.121), calls=%async_computation.1 | async-start | bytes 1048576 | tf_op jit(solution)/shard_map/all_to_all | solution.py:305
  49.0 2.6 %collective-permute-start = (bf16[1664,128]{1,0:T(8,128)(2,1)S(1)}, bf16[1664,128]{1,0:T(8,128)(2,1)S(1)}, u32[]{:S(2)}, u32[]{:S(2)}) collective-permute-start(bf16[1664,128]{1,0:T(8,128)(2,1)S(1)} %get-tuple-element.38), channel_id=1, source_target_pairs={{0,1},{1,0},{2,3},{3,2},{4,5},{5,4},{6,7},{7,6},{8,9},{9,8},{10,11... | collective-permute-start | bytes 1277960 | tf_op jit(solution)/shard_map/ppermute | solution.py:382
  82.5 4.6 %collective-permute-start.1 = (bf16[1664,128]{1,0:T(8,128)(2,1)S(1)}, bf16[1664,128]{1,0:T(8,128)(2,1)S(1)}, u32[]{:S(2)}, u32[]{:S(2)}) collective-permute-start(bf16[1664,128]{1,0:T(8,128)(2,1)S(1)} %bitcast.16), channel_id=1, source_target_pairs={{0,1},{1,0},{2,3},{3,2},{4,5},{5,4},{6,7},{7,6},{8,9},{9,8},{10,11... | collective-permute-start | bytes 1277960 | tf_op jit(solution)/shard_map/ppermute | solution.py:388

commit v6 on v5

--- a/solution.py
+++ b/solution.py
@@ -43,7 +43,7 @@
     )
 
 
-def places(capacity, groups, owner, local=None):
+def places(capacity, groups, owner, local):
     seeds, neighbours = owner.shape
     lane = iota((seeds, groups), 1)
     named = jnp.zeros((seeds, groups), f32)
@@ -51,27 +51,44 @@
     for k in range(neighbours):
         hit = owner[:, k : k + 1] == lane
         named = jnp.where(hit, 1.0, named)
-        if local is not None:
-            wanted = jnp.where(hit, local[:, k : k + 1], wanted)
+        wanted = jnp.where(hit, local[:, k : k + 1], wanted)
     before = (iota((seeds, seeds), 1) < iota((seeds, seeds), 0)).astype(f32)
     earlier = dot(before.astype(bf16), named.astype(bf16)).astype(i32)
     return named > 0, earlier, wanted
 
 
-def request_body(capacity, owner_hbm, local_hbm, pairs_hbm, table_ref, pairs_ref, owner_ref, local_ref, arrivals):
-    copies = [
-        pltpu.make_async_copy(owner_hbm, owner_ref, arrivals.at[0]),
-        pltpu.make_async_copy(local_hbm, local_ref, arrivals.at[1]),
-    ]
+def request_body(
+    capacity,
+    core_ref,
+    owner_hbm,
+    local_hbm,
+    weight_hbm,
+    labels_hbm,
+    pairs_hbm,
+    table_ref,
+    codes_ref,
+    weights_ref,
+    onehot_ref,
+    pairs_ref,
+    owner_ref,
+    local_ref,
+    weight_ref,
+    labels_ref,
+    arrivals,
+):
+    del core_ref
+    small = zip((owner_hbm, local_hbm, weight_hbm, labels_hbm), (owner_ref, local_ref, weight_ref, labels_ref))
+    copies = [pltpu.make_async_copy(source, target, arrivals.at[i]) for i, (source, target) in enumerate(small)]
     for copy in copies:
         copy.start()
-    pairs = pltpu.make_async_copy(pairs_hbm, pairs_ref, arrivals.at[2])
+    pairs = pltpu.make_async_copy(pairs_hbm, pairs_ref, arrivals.at[len(copies)])
     pairs.start()
     for copy in copies:
         copy.wait()
     groups = table_ref.shape[0]
-    seeds = owner_ref.shape[0]
-    named, earlier, wanted = places(capacity, groups, owner_ref[...], local_ref[...])
+    owner = owner_ref[...]
+    seeds, neighbours = owner.shape
+    named, earlier, wanted = places(capacity, groups, owner, local_ref[...])
     place = jnp.where(named, earlier, -1)
     slot = iota((capacity, groups), 0)
     table = jnp.zeros((capacity, groups), i32)
@@ -79,6 +96,20 @@
         table = jnp.where(place[s : s + 1, :] == slot, wanted[s : s + 1, :], table)
     spare = jnp.zeros((LANES - capacity, groups), i32)
     table_ref[...] = jnp.concatenate([table, spare], axis=0).T
+    code_of = coded_slots(iota((seeds, groups), 1) * capacity + earlier)
+    owner_t = owner.T
+    weight_t = weight_ref[...].T
+    lane = iota((neighbours, groups), 1)
+    own = []
+    for s in range(seeds):
+        own.append(jnp.where(owner_t[:, s : s + 1] == lane, code_of[s : s + 1, :], 0.0).astype(bf16))
+        rows = pl.ds(s * neighbours, neighbours)
+        weights_ref[rows, :] = jnp.broadcast_to(weight_t[:, s : s + 1], (neighbours, weights_ref.shape[1]))
+    everything = jnp.ones((groups, codes_ref.shape[1]), bf16)
+    codes_ref[...] = dot(jnp.concatenate(own, axis=0), everything).astype(bf16)
+    diagonal = iota((seeds, seeds), 0) == iota((seeds, seeds), 1)
+    label = jnp.sum(jnp.where(diagonal, labels_ref[...].astype(f32), 0.0), axis=1, keepdims=True).astype(i32)
+    onehot_ref[...] = jnp.where(label == iota(onehot_ref.shape, 1), 1.0, 0.0)
     pairs.wait()
 
 
@@ -86,26 +117,8 @@
     return ((128 + (slot & 127)) * (1 << (slot >> 7))).astype(f32)
 
 
-def spread_body(capacity, groups, owner_ref, weight_ref, second_hbm, codes_ref, weights_ref, second_ref, arrival):
-    second = pltpu.make_async_copy(second_hbm, second_ref, arrival)
-    second.start()
-    seeds, neighbours = owner_ref.shape
-    _, earlier, _ = places(capacity, groups, owner_ref[...])
-    code_of = coded_slots(iota((seeds, groups), 1) * capacity + earlier)
-    owner_t = owner_ref[...].T
-    weight_t = weight_ref[...].T
-    lane = iota((neighbours, groups), 1)
-    for s in range(seeds):
-        rows = pl.ds(s * neighbours, neighbours)
-        own = jnp.where(owner_t[:, s : s + 1] == lane, code_of[s : s + 1, :], 0.0)
-        code = jnp.sum(own, axis=1, keepdims=True)
-        codes_ref[rows, :] = jnp.broadcast_to(code, (neighbours, codes_ref.shape[1])).astype(bf16)
-        weights_ref[rows, :] = jnp.broadcast_to(weight_t[:, s : s + 1], (neighbours, weights_ref.shape[1]))
-    second.wait()
-
-
 def serve_body(
-    capacity, asked_ref, pairs_ref, rows_hbm, rows_ref, stage_ref, wide_ref, turned_ref, index_ref, arrival, leaving
+    capacity, asked_ref, pairs_ref, rows_ref, stage_ref, wide_ref, turned_ref, index_ref, arrival
 ):
     asked = asked_ref[...]
     turned_ref[...] = asked.T[:capacity, :] >> 1
@@ -113,9 +126,8 @@
     index.start()
     index.wait()
     odd = (asked & 1) > 0
-    groups = leaving.shape[0]
+    groups = wide_ref.shape[0]
     size = asked.shape[0] // groups
-    copies = []
     for group in range(groups):
         span = slice(group * size, (group + 1) * size)
         for p in range(capacity):
@@ -126,10 +138,6 @@
             second = stage[pl.ds(1, size, stride=2), :]
             wide_ref[group, pl.ds(p, size, stride=capacity), :] = jnp.where(odd[span, p : p + 1], second, first)
         rows_ref[span] = wide_ref[group].reshape(size, capacity, -1).astype(bf16)
-        copies.append(pltpu.make_async_copy(rows_ref.at[span], rows_hbm.at[span], leaving.at[group]))
-        copies[-1].start()
-    for copy in copies:
-        copy.wait()
 
 
 def step_body(
@@ -139,7 +147,7 @@
     codes_ref,
     arrived_ref,
     weights_ref,
-    labels_ref,
+    onehot_ref,
     first_ref,
     second_ref,
     third_t_ref,
@@ -205,7 +213,7 @@
         logits_ref[s, :] = logits
         highest = jnp.max(logits, axis=1, keepdims=True)
         log_total = jnp.log(jnp.sum(jnp.exp(logits - highest), axis=1, keepdims=True)) + highest
-        onehot = jnp.where(labels_ref[s, :] == iota((seed_size, classes), 1), 1.0, 0.0)
+        onehot = onehot_ref[s, :]
         terms.append(log_total - jnp.sum(onehot * logits, axis=1, keepdims=True))
         logit_grad = (jnp.exp(logits - log_total) - onehot) / total_seeds
         every = jnp.broadcast_to(logit_grad[:, None, :], (seed_size, neighbours, classes)).reshape(size, classes)
@@ -319,46 +327,45 @@
     swap = [(0, 1), (1, 0)]
 
     pairs = features.reshape(-1, 2, width)
-    table, pairs = call(
+    rows = seeds * neighbours
+    table, codes, weights, onehot, pairs = call(
         functools.partial(request_body, capacity),
-        (shape((groups, LANES), i32), pltpu.VMEM(pairs.shape, bf16)),
-        [FAR] * 3,
+        (
+            shape((groups, LANES), i32),
+            shape((rows, LANES), bf16),
+            shape((rows, LANES), f32),
+            shape((seeds, classes), f32),
+            pltpu.VMEM(pairs.shape, bf16),
+        ),
+        [SMEM] + [FAR] * 5,
         [
-            pltpu.VMEM((seeds, neighbours), i32),
-            pltpu.VMEM((seeds, neighbours), i32),
-            pltpu.SemaphoreType.DMA((3,)),
+            *(pltpu.VMEM((seeds, neighbours), t) for t in (i32, i32, f32)),
+            pltpu.VMEM((1, seeds), i32),
+            pltpu.SemaphoreType.DMA((5,)),
         ],
-    )(*(pltpu.with_memory_space_constraint(a, pltpu.HBM) for a in (nbr_owner, nbr_local, pairs)))
+    )(
+        core,
+        *(
+            pltpu.with_memory_space_constraint(a, pltpu.HBM)
+            for a in (nbr_owner, nbr_local, ppr_weight, labels.reshape(1, -1), pairs)
+        ),
+    )
     asked = everywhere(table.reshape(groups, 1, LANES), NODES).reshape(groups, LANES)
-    codes, weights, second = call(
-        functools.partial(spread_body, capacity, groups),
-        (
-            shape((seeds * neighbours, LANES), bf16),
-            shape((seeds * neighbours, LANES), f32),
-            pltpu.VMEM(w_second.shape, bf16),
-        ),
-        [VMEM, VMEM, FAR],
-        [pltpu.SemaphoreType.DMA],
-    )(nbr_owner, ppr_weight, pltpu.with_memory_space_constraint(w_second, pltpu.HBM))
     served = call(
         functools.partial(serve_body, capacity),
-        pltpu.HBM((groups, capacity, width), bf16),
+        shape((groups, capacity, width), bf16),
         [VMEM, VMEM],
         [
-            pltpu.VMEM((groups, capacity, width), bf16),
             pltpu.VMEM((4, 2 * groups // 4, width), f32),
             pltpu.VMEM((4, groups * capacity // 4, width), f32),
             pltpu.VMEM((capacity, groups), i32),
             pltpu.SMEM((capacity, groups), i32),
             pltpu.SemaphoreType.DMA,
-            pltpu.SemaphoreType.DMA((4,)),
         ],
         16,
-        FAR,
     )(asked, pairs)
     arrived = everywhere(served, NODES).reshape(slots, width)
 
-    rows = seeds * neighbours
     half = hidden // 2
     blocks = half // LANES
     tall = 2 * chips // blocks * -(-(width + hidden + classes + 1) * blocks // (2 * chips))
@@ -378,7 +385,7 @@
         [pltpu.VMEM(grads, f32), pltpu.VMEM((seeds, classes), f32), pltpu.SemaphoreType.DMA],
         32,
         (FAR, *[VMEM] * 8),
-    )(core, codes, arrived, weights, labels.reshape(-1, 1), w_first, second, w_third.T)
+    )(core, codes, arrived, weights, onehot, w_first, w_second, w_third.T)
     near = lax.ppermute(send, CORE, swap)
     keep = call(keep_body, shape(grads, f32), [SMEM] + [VMEM] * 7, (), 16)(core, *kept)
     parts = (keep + near.astype(f32)).astype(bf16)

time: 88.3 us -> 87.6 us (level)
  blocking collectives: 51 us -> 69.2 us
  waiting for transfers between devices: 10.4 us -> 0.7 us
  starting transfers between devices: 9.1 us -> 4.38 us
  Pallas kernels: 16.6 us -> 12.2 us
    all_to_all x3 -> x4, blocking collectives: 51 us -> 69.2 us  [everywhere(): return lax.all_to_all(parts, axis, 0, 0, tiled=True)]
    all_to_all x1 -> x0, waiting for transfers between devices: 9.67 us -> none  [everywhere(): return lax.all_to_all(parts, axis, 0, 0, tiled=True)]
    all_to_all x1 -> x0, starting transfers between devices: 4.74 us -> none  [everywhere(): return lax.all_to_all(parts, axis, 0, 0, tiled=True)]
    pallas_call x2 -> x1, Pallas kernels: 7.21 us -> 2.56 us  [on_device(): call(functools.partial(serve_body, capacity), shape((groups, capacity, wi...]
  transfers between devices with their start and end apart: 3 -> 2, of which waited for: 2 -> 1; matrix products, arithmetic and copies ran while one was open for 0% -> 0% of each run, Pallas kernels for 7% -> 2%
where the time goes in v6:
time: 87.6 us; the launch traced here: 87.3 us
  blocking collectives  69.2 us (79%)
  Pallas kernels  12.2 us (14%)
  starting transfers between devices  4.38 us (5%)
    all_to_all x4, blocking collectives, everywhere(): return lax.all_to_all(parts, axis, 0, 0, tiled=True)  69.2 us
    pallas_call x1, Pallas kernels, on_device(): call(functools.partial(step_body, total_seeds, 2), (pltpu.HBM((seeds, cla...  3.78 us
    ppermute x1, starting transfers between devices, on_device(): other = lax.ppermute(own, CORE, swap)  3.15 us
    pallas_call x1, Pallas kernels, on_device(): call(functools.partial(serve_body, capacity), shape((groups, capacity, wi...  2.56 us
    pallas_call x1, Pallas kernels, on_device(): call(functools.partial(request_body, capacity), (shape((groups, LANES), i...  2.37 us
  transfers between devices with their start and end apart: 2, of which 1 were waited for; matrix products, arithmetic and copies ran while one was open for 0% of the time, Pallas kernels for 2%

profile of v6, /device:TPU:1, one launch (start us, length us, event | category | flops | bytes accessed | tf_op | source)
XLA Modules:
  0.0 87.3 jit_solution(7575450165891964053)
XLA Ops:
  0.6 0.0 copy-start
  0.6 0.0 copy-start.1
  0.7 0.0 copy-start.2
  0.7 2.4 %shard_map.119 = (s32[128,128]{1,0:T(8,128)S(1)}, bf16[1024,128]{1,0:T(8,128)(2,1)S(1)}, f32[1024,128]{1,0:T(8,128)S(1)}, f32[32,172]{1,0:T(8,128)S(1)}, bf16[8192,2,128]{2,1,0:T(2,128)(2,1)S(1)}) custom-call(s32[1]{0:T(128)} %bitcast.core_ref, s32[32,32]{1,0:T(8,128)} %owner_hbm.1, s32[32,32]{1,0:T(8,128)} %local_hbm.1, f32[32,32]{1,0:T(8,128)} %weight_hbm.1, ...), custom_call_target="tpu_custom_call" | custom-call | tf_op jit(solution)/shard_map/pallas_call | solution.py:331
  3.0 20.7 %all_to_all.20 = s32[128,1,128]{2,1,0:T(1,128)S(1)} all-to-all(s32[128,1,128]{2,1,0:T(1,128)S(1)} %bitcast.22), channel_id=1, replica_groups=mesh['nodes_0'=4,'nodes_1'=4,'nodes_2'=4,'nodes_3'=2] {'nodes_0','nodes_..., dimensions={0} | all-to-all | bytes 131072 | tf_op jit(solution)/shard_map/all_to_all | solution.py:313
  23.7 2.6 %shard_map.120 = bf16[128,16,128]{2,1,0:T(8,128)(2,1)S(1)} custom-call(s32[128,128]{1,0:T(8,128)S(1)} %bitcast.20, bf16[8192,2,128]{2,1,0:T(2,128)(2,1)S(1)} %get-tuple-element.28.pairs_ref), custom_call_target="tpu_custom_call" | custom-call | tf_op jit(solution)/shard_map/pallas_call | solution.py:354
  26.3 18.2 %all_to_all.21 = bf16[128,16,128]{2,1,0:T(8,128)(2,1)S(1)} all-to-all(bf16[128,16,128]{2,1,0:T(8,128)(2,1)S(1)} %shard_map.120), channel_id=1, replica_groups=mesh['nodes_0'=4,'nodes_1'=4,'nodes_2'=4,'nodes_3'=2] {'nodes_0','nodes_..., dimensions={0} | all-to-all | bytes 1048576 | tf_op jit(solution)/shard_map/all_to_all | solution.py:313
  44.5 0.0 copy-done
  44.5 0.0 copy-done.1
  44.5 0.0 copy-done.2
  44.5 3.8 %shard_map.121 = (f32[32,172]{1,0:T(8,128)}, bf16[1664,128]{1,0:T(8,128)(2,1)S(1)}, f32[8,128]{1,0:T(8,128)S(1)}, bf16[1024,128]{1,0:T(8,128)(2,1)S(1)}, bf16[10...) custom-call(s32[1]{0:T(128)} %bitcast.core_ref, ...), custom_call_target="tpu_custom_call" | custom-call | tf_op jit(solution)/shard_map/pallas_call | solution.py:373
  48.3 1.2 %collective-permute-start = (bf16[1664,128]{1,0:T(8,128)(2,1)S(1)}, bf16[1664,128]{1,0:T(8,128)(2,1)S(1)}, u32[]{:S(2)}, u32[]{:S(2)}) collective-permute-start(bf16[1664,128]{1,0:T(8,128)(2,1)S(1)} %get-tuple-element.38), channel_id=1, source_target_pairs={{0,1},{1,0},{2,3},{3,2},{4,5},{5,4},{6,7},{7,6},{8,9},{9,8},{10,11... | collective-permute-start | bytes 1277960 | tf_op jit(solution)/shard_map/ppermute | solution.py:389
  49.6 0.7 shard_map.122
  50.3 0.7 collective-permute-done
  50.9 0.1 add_convert_fusion
  51.1 15.4 %all_to_all.22 = bf16[832,2,128]{2,1,0:T(2,128)(2,1)S(1)} all-to-all(bf16[832,2,128]{2,1,0:T(2,128)(2,1)S(1)} %bitcast.24), channel_id=1, replica_groups=mesh['nodes_0'=4,'nodes_1'=4,'nodes_2'=4,'nodes_3'=2] {'nodes_0','nodes_..., dimensions={0} | all-to-all | bytes 851968 | tf_op jit(solution)/shard_map/all_to_all | solution.py:313
  66.5 0.5 shard_map.123
  66.9 14.9 %all_to_all.23 = bf16[832,2,128]{2,1,0:T(2,128)(2,1)S(1)} all-to-all(bf16[832,2,128]{2,1,0:T(2,128)(2,1)S(1)} %bitcast.19), channel_id=1, replica_groups=mesh['nodes_0'=4,'nodes_1'=4,'nodes_2'=4,'nodes_3'=2] {'nodes_0','nodes_..., dimensions={0} | all-to-all | bytes 851968 | tf_op jit(solution)/shard_map/all_to_all | solution.py:313
  81.8 3.2 %collective-permute-start.1 = (bf16[1664,128]{1,0:T(8,128)(2,1)S(1)}, bf16[1664,128]{1,0:T(8,128)(2,1)S(1)}, u32[]{:S(2)}, u32[]{:S(2)}) collective-permute-start(bf16[1664,128]{1,0:T(8,128)(2,1)S(1)} %bitcast.16), channel_id=1, source_target_pairs={{0,1},{1,0},{2,3},{3,2},{4,5},{5,4},{6,7},{7,6},{8,9},{9,8},{10,11... | collective-permute-start | bytes 1277960 | tf_op jit(solution)/shard_map/ppermute | solution.py:395
  85.0 1.4 %shard_map.124 = (f32[128,512]{1,0:T(8,128)}, f32[512,512]{1,0:T(8,128)}, f32[172,512]{1,0:T(8,128)}, f32[1,1]{1,0:T(1,128)}) custom-call(s32[1]{0:T(128)} %bitcast.core_ref, bf16[1664,128]{1,0:T(8,128)(2,1)S(1)} %bitcast.17), custom_call_target="tpu_custom_call" | custom-call | tf_op jit(solution)/shard_map/pallas_call | solution.py:399
  86.4 0.0 collective-permute-done.1.other_ref
  86.4 0.9 %shard_map.125 = (f32[128,512]{1,0:T(8,128)}, f32[512,512]{1,0:T(8,128)}, f32[172,512]{1,0:T(8,128)}) custom-call(s32[1]{0:T(128)} %bitcast.core_ref, bf16[1664,128]{1,0:T(8,128)(2,1)S(1)} %collective-permute-done.1.other_ref, f32[128,512]{1,0:T(8,128)} %get-tuple-element.41.given_first, ...), custom_call_target="tpu_custom_call", output_to_operand_aliasing={{0}: (2, {}), {1}: (3, {}), {2}: (4, {})} | custom-call | tf_op jit(solution)/shard_map/pallas_call | solution.py:407
Async XLA Ops:
  0.6 43.9 %copy-start = (bf16[512,512]{1,0:T(8,128)(2,1)S(1)}, bf16[512,512]{1,0:T(8,128)(2,1)}, u32[]{:S(2)}) copy-start(bf16[512,512]{1,0:T(8,128)(2,1)} %second_ref.1) | copy-start | bytes 1572868
  0.6 43.9 %copy-start.1 = (bf16[512,172]{0,1:T(8,128)(2,1)S(1)}, bf16[512,172]{0,1:T(8,128)(2,1)}, u32[]{:S(2)}) copy-start(bf16[512,172]{0,1:T(8,128)(2,1)} %param.15) | copy-start | bytes 528388
  0.7 43.9 %copy-start.2 = (bf16[128,512]{1,0:T(8,128)(2,1)S(1)}, bf16[128,512]{1,0:T(8,128)(2,1)}, u32[]{:S(2)}) copy-start(bf16[128,512]{1,0:T(8,128)(2,1)} %first_ref.1) | copy-start | bytes 393220
  48.3 2.6 %collective-permute-start = (bf16[1664,128]{1,0:T(8,128)(2,1)S(1)}, bf16[1664,128]{1,0:T(8,128)(2,1)S(1)}, u32[]{:S(2)}, u32[]{:S(2)}) collective-permute-start(bf16[1664,128]{1,0:T(8,128)(2,1)S(1)} %get-tuple-element.38), channel_id=1, source_target_pairs={{0,1},{1,0},{2,3},{3,2},{4,5},{5,4},{6,7},{7,6},{8,9},{9,8},{10,11... | collective-permute-start | bytes 1277960 | tf_op jit(solution)/shard_map/ppermute | solution.py:389
  81.8 4.6 %collective-permute-start.1 = (bf16[1664,128]{1,0:T(8,128)(2,1)S(1)}, bf16[1664,128]{1,0:T(8,128)(2,1)S(1)}, u32[]{:S(2)}, u32[]{:S(2)}) collective-permute-start(bf16[1664,128]{1,0:T(8,128)(2,1)S(1)} %bitcast.16), channel_id=1, source_target_pairs={{0,1},{1,0},{2,3},{3,2},{4,5},{5,4},{6,7},{7,6},{8,9},{9,8},{10,11... | collective-permute-start | bytes 1277960 | tf_op jit(solution)/shard_map/ppermute | solution.py:395

commit v7 on v6

--- a/solution.py
+++ b/solution.py
@@ -68,7 +68,7 @@
     table_ref,
     codes_ref,
     weights_ref,
-    onehot_ref,
+    label_ref,
     pairs_ref,
     owner_ref,
     local_ref,
@@ -108,8 +108,8 @@
     everything = jnp.ones((groups, codes_ref.shape[1]), bf16)
     codes_ref[...] = dot(jnp.concatenate(own, axis=0), everything).astype(bf16)
     diagonal = iota((seeds, seeds), 0) == iota((seeds, seeds), 1)
-    label = jnp.sum(jnp.where(diagonal, labels_ref[...].astype(f32), 0.0), axis=1, keepdims=True).astype(i32)
-    onehot_ref[...] = jnp.where(label == iota(onehot_ref.shape, 1), 1.0, 0.0)
+    label = jnp.sum(jnp.where(diagonal, labels_ref[...].astype(f32), 0.0), axis=1, keepdims=True)
+    label_ref[...] = label.astype(i32)
     pairs.wait()
 
 
@@ -118,12 +118,31 @@
 
 
 def serve_body(
-    capacity, asked_ref, pairs_ref, rows_ref, stage_ref, wide_ref, turned_ref, index_ref, arrival
+    capacity,
+    asked_ref,
+    pairs_ref,
+    first_hbm,
+    second_hbm,
+    third_t_hbm,
+    rows_ref,
+    first_ref,
+    second_ref,
+    third_t_ref,
+    stage_ref,
+    wide_ref,
+    turned_ref,
+    index_ref,
+    arrival,
+    params,
 ):
+    layers = zip((first_hbm, second_hbm, third_t_hbm), (first_ref, second_ref, third_t_ref))
+    copies = [pltpu.make_async_copy(source, target, params.at[i]) for i, (source, target) in enumerate(layers)]
     asked = asked_ref[...]
     turned_ref[...] = asked.T[:capacity, :] >> 1
     index = pltpu.make_async_copy(turned_ref, index_ref, arrival)
     index.start()
+    for copy in copies:
+        copy.start()
     index.wait()
     odd = (asked & 1) > 0
     groups = wide_ref.shape[0]
@@ -137,7 +156,9 @@
             first = stage[pl.ds(0, size, stride=2), :]
             second = stage[pl.ds(1, size, stride=2), :]
             wide_ref[group, pl.ds(p, size, stride=capacity), :] = jnp.where(odd[span, p : p + 1], second, first)
-        rows_ref[span] = wide_ref[group].reshape(size, capacity, -1).astype(bf16)
+        rows_ref[span] = wide_ref[group, : size * capacity, :].reshape(size, capacity, -1).astype(bf16)
+    for copy in copies:
+        copy.wait()
 
 
 def step_body(
@@ -147,7 +168,7 @@
     codes_ref,
     arrived_ref,
     weights_ref,
-    onehot_ref,
+    label_ref,
     first_ref,
     second_ref,
     third_t_ref,
@@ -213,7 +234,7 @@
         logits_ref[s, :] = logits
         highest = jnp.max(logits, axis=1, keepdims=True)
         log_total = jnp.log(jnp.sum(jnp.exp(logits - highest), axis=1, keepdims=True)) + highest
-        onehot = onehot_ref[s, :]
+        onehot = jnp.where(label_ref[s, :] == iota((seed_size, classes), 1), 1.0, 0.0)
         terms.append(log_total - jnp.sum(onehot * logits, axis=1, keepdims=True))
         logit_grad = (jnp.exp(logits - log_total) - onehot) / total_seeds
         every = jnp.broadcast_to(logit_grad[:, None, :], (seed_size, neighbours, classes)).reshape(size, classes)
@@ -328,13 +349,13 @@
 
     pairs = features.reshape(-1, 2, width)
     rows = seeds * neighbours
-    table, codes, weights, onehot, pairs = call(
+    table, codes, weights, label, pairs = call(
         functools.partial(request_body, capacity),
         (
             shape((groups, LANES), i32),
             shape((rows, LANES), bf16),
             shape((rows, LANES), f32),
-            shape((seeds, classes), f32),
+            shape((seeds, 1), i32),
             pltpu.VMEM(pairs.shape, bf16),
         ),
         [SMEM] + [FAR] * 5,
@@ -351,19 +372,21 @@
         ),
     )
     asked = everywhere(table.reshape(groups, 1, LANES), NODES).reshape(groups, LANES)
-    served = call(
+    params = (w_first, w_second, w_third.T)
+    served, *params = call(
         functools.partial(serve_body, capacity),
-        shape((groups, capacity, width), bf16),
-        [VMEM, VMEM],
+        (shape((groups, capacity, width), bf16), *(pltpu.VMEM(p.shape, bf16) for p in params)),
+        [VMEM, VMEM, FAR, FAR, FAR],
         [
-            pltpu.VMEM((4, 2 * groups // 4, width), f32),
-            pltpu.VMEM((4, groups * capacity // 4, width), f32),
+            pltpu.VMEM((4, groups // 2 + 8, width), f32),
+            pltpu.VMEM((4, (groups // 4 + 1) * capacity, width), f32),
             pltpu.VMEM((capacity, groups), i32),
             pltpu.SMEM((capacity, groups), i32),
             pltpu.SemaphoreType.DMA,
+            pltpu.SemaphoreType.DMA((3,)),
         ],
         16,
-    )(asked, pairs)
+    )(asked, pairs, *(pltpu.with_memory_space_constraint(p, pltpu.HBM) for p in params))
     arrived = everywhere(served, NODES).reshape(slots, width)
 
     half = hidden // 2
@@ -385,7 +408,7 @@
         [pltpu.VMEM(grads, f32), pltpu.VMEM((seeds, classes), f32), pltpu.SemaphoreType.DMA],
         32,
         (FAR, *[VMEM] * 8),
-    )(core, codes, arrived, weights, onehot, w_first, w_second, w_third.T)
+    )(core, codes, arrived, weights, label, *params)
     near = lax.ppermute(send, CORE, swap)
     keep = call(keep_body, shape(grads, f32), [SMEM] + [VMEM] * 7, (), 16)(core, *kept)
     parts = (keep + near.astype(f32)).astype(bf16)

time: 87.6 us -> 87.5 us (level)
  no operation moved by 1% of the time
where the time goes in v7:
time: 87.5 us; the launch traced here: 87.2 us
  blocking collectives  69.2 us (79%)
  Pallas kernels  12.1 us (14%)
  starting transfers between devices  4.36 us (5%)
    all_to_all x4, blocking collectives, everywhere(): return lax.all_to_all(parts, axis, 0, 0, tiled=True)  69.2 us
    pallas_call x1, Pallas kernels, on_device(): call(functools.partial(step_body, total_seeds, 2), (pltpu.HBM((seeds, cla...  3.7 us
    ppermute x1, starting transfers between devices, on_device(): other = lax.ppermute(own, CORE, swap)  3.14 us
    pallas_call x1, Pallas kernels, on_device(): call(functools.partial(serve_body, capacity), (shape((groups, capacity, w...  2.59 us
    pallas_call x1, Pallas kernels, on_device(): call(functools.partial(request_body, capacity), (shape((groups, LANES), i...  2.3 us
  transfers between devices with their start and end apart: 2, of which 1 were waited for; matrix products, arithmetic and copies ran while one was open for 0% of the time, Pallas kernels for 2%

profile of v7, /device:TPU:1, one launch (start us, length us, event | category | flops | bytes accessed | tf_op | source)
XLA Modules:
  0.0 87.2 jit_solution(15130690333621239434)
XLA Ops:
  0.6 2.3 %shard_map.119 = (s32[128,128]{1,0:T(8,128)S(1)}, bf16[1024,128]{1,0:T(8,128)(2,1)S(1)}, f32[1024,128]{1,0:T(8,128)S(1)}, s32[32,1]{1,0:T(8,128)S(1)}, bf16[8192,2,128]{2,1,0:T(2,128)(2,1)S(1)}) custom-call(s32[1]{0:T(128)} %bitcast.core_ref, s32[32,32]{1,0:T(8,128)} %owner_hbm.1, s32[32,32]{1,0:T(8,128)} %local_hbm.1, f32[32,32]{1,0:T(8,128)} %weight_hbm.1, ...), custom_call_target="tpu_custom_call" | custom-call | tf_op jit(solution)/shard_map/pallas_call | solution.py:352
  2.9 20.7 %all_to_all.20 = s32[128,1,128]{2,1,0:T(1,128)S(1)} all-to-all(s32[128,1,128]{2,1,0:T(1,128)S(1)} %bitcast.21), channel_id=1, replica_groups=mesh['nodes_0'=4,'nodes_1'=4,'nodes_2'=4,'nodes_3'=2] {'nodes_0','nodes_..., dimensions={0} | all-to-all | bytes 131072 | tf_op jit(solution)/shard_map/all_to_all | solution.py:334
  23.6 2.6 %shard_map.120 = (bf16[128,16,128]{2,1,0:T(8,128)(2,1)S(1)}, bf16[128,512]{1,0:T(8,128)(2,1)S(1)}, bf16[512,512]{1,0:T(8,128)(2,1)S(1)}, bf16[172,512]{1,0:T(8,128)(2,1)S(1)}) custom-call(s32[128,128]{1,0:T(8,128)S(1)} %bitcast.20, bf16[8192,2,128]{2,1,0:T(2,128)(2,1)S(1)} %get-tuple-element.32.pairs_ref, bf16[128,512]{1,0:T(8,128)(2,1)} %first_hbm.1, ...), custom_call_target="tpu_custom_call" | custom-call | tf_op jit(solution)/shard_map/pallas_call | solution.py:376
  26.2 18.2 %all_to_all.21 = bf16[128,16,128]{2,1,0:T(8,128)(2,1)S(1)} all-to-all(bf16[128,16,128]{2,1,0:T(8,128)(2,1)S(1)} %get-tuple-element.33), channel_id=1, replica_groups=mesh['nodes_0'=4,'nodes_1'=4,'nodes_2'=4,'nodes_3'=2] {'nodes_0','nodes_..., dimensions={0} | all-to-all | bytes 1048576 | tf_op jit(solution)/shard_map/all_to_all | solution.py:334
  44.5 3.7 %shard_map.121 = (f32[32,172]{1,0:T(8,128)}, bf16[1664,128]{1,0:T(8,128)(2,1)S(1)}, f32[8,128]{1,0:T(8,128)S(1)}, bf16[1024,128]{1,0:T(8,128)(2,1)S(1)}, bf16[10...) custom-call(s32[1]{0:T(128)} %bitcast.core_ref, ...), custom_call_target="tpu_custom_call" | custom-call | tf_op jit(solution)/shard_map/pallas_call | solution.py:396
  48.2 1.2 %collective-permute-start = (bf16[1664,128]{1,0:T(8,128)(2,1)S(1)}, bf16[1664,128]{1,0:T(8,128)(2,1)S(1)}, u32[]{:S(2)}, u32[]{:S(2)}) collective-permute-start(bf16[1664,128]{1,0:T(8,128)(2,1)S(1)} %get-tuple-element.46), channel_id=1, source_target_pairs={{0,1},{1,0},{2,3},{3,2},{4,5},{5,4},{6,7},{7,6},{8,9},{9,8},{10,11... | collective-permute-start | bytes 1277960 | tf_op jit(solution)/shard_map/ppermute | solution.py:412
  49.4 0.7 shard_map.122
  50.1 0.7 collective-permute-done
  50.8 0.1 add_convert_fusion
  50.9 15.4 %all_to_all.22 = bf16[832,2,128]{2,1,0:T(2,128)(2,1)S(1)} all-to-all(bf16[832,2,128]{2,1,0:T(2,128)(2,1)S(1)} %bitcast.23), channel_id=1, replica_groups=mesh['nodes_0'=4,'nodes_1'=4,'nodes_2'=4,'nodes_3'=2] {'nodes_0','nodes_..., dimensions={0} | all-to-all | bytes 851968 | tf_op jit(solution)/shard_map/all_to_all | solution.py:334
  66.3 0.5 shard_map.123
  66.8 14.9 %all_to_all.23 = bf16[832,2,128]{2,1,0:T(2,128)(2,1)S(1)} all-to-all(bf16[832,2,128]{2,1,0:T(2,128)(2,1)S(1)} %bitcast.19), channel_id=1, replica_groups=mesh['nodes_0'=4,'nodes_1'=4,'nodes_2'=4,'nodes_3'=2] {'nodes_0','nodes_..., dimensions={0} | all-to-all | bytes 851968 | tf_op jit(solution)/shard_map/all_to_all | solution.py:334
  81.7 3.1 %collective-permute-start.1 = (bf16[1664,128]{1,0:T(8,128)(2,1)S(1)}, bf16[1664,128]{1,0:T(8,128)(2,1)S(1)}, u32[]{:S(2)}, u32[]{:S(2)}) collective-permute-start(bf16[1664,128]{1,0:T(8,128)(2,1)S(1)} %bitcast.16), channel_id=1, source_target_pairs={{0,1},{1,0},{2,3},{3,2},{4,5},{5,4},{6,7},{7,6},{8,9},{9,8},{10,11... | collective-permute-start | bytes 1277960 | tf_op jit(solution)/shard_map/ppermute | solution.py:418
  84.8 1.4 %shard_map.124 = (f32[128,512]{1,0:T(8,128)}, f32[512,512]{1,0:T(8,128)}, f32[172,512]{1,0:T(8,128)}, f32[1,1]{1,0:T(1,128)}) custom-call(s32[1]{0:T(128)} %bitcast.core_ref, bf16[1664,128]{1,0:T(8,128)(2,1)S(1)} %bitcast.17), custom_call_target="tpu_custom_call" | custom-call | tf_op jit(solution)/shard_map/pallas_call | solution.py:422
  86.2 0.0 collective-permute-done.1.other_ref
  86.2 0.9 %shard_map.125 = (f32[128,512]{1,0:T(8,128)}, f32[512,512]{1,0:T(8,128)}, f32[172,512]{1,0:T(8,128)}) custom-call(s32[1]{0:T(128)} %bitcast.core_ref, bf16[1664,128]{1,0:T(8,128)(2,1)S(1)} %collective-permute-done.1.other_ref, f32[128,512]{1,0:T(8,128)} %get-tuple-element.49.given_first, ...), custom_call_target="tpu_custom_call", output_to_operand_aliasing={{0}: (2, {}), {1}: (3, {}), {2}: (4, {})} | custom-call | tf_op jit(solution)/shard_map/pallas_call | solution.py:430
Async XLA Ops:
  48.2 2.6 %collective-permute-start = (bf16[1664,128]{1,0:T(8,128)(2,1)S(1)}, bf16[1664,128]{1,0:T(8,128)(2,1)S(1)}, u32[]{:S(2)}, u32[]{:S(2)}) collective-permute-start(bf16[1664,128]{1,0:T(8,128)(2,1)S(1)} %get-tuple-element.46), channel_id=1, source_target_pairs={{0,1},{1,0},{2,3},{3,2},{4,5},{5,4},{6,7},{7,6},{8,9},{9,8},{10,11... | collective-permute-start | bytes 1277960 | tf_op jit(solution)/shard_map/ppermute | solution.py:412
  81.7 4.6 %collective-permute-start.1 = (bf16[1664,128]{1,0:T(8,128)(2,1)S(1)}, bf16[1664,128]{1,0:T(8,128)(2,1)S(1)}, u32[]{:S(2)}, u32[]{:S(2)}) collective-permute-start(bf16[1664,128]{1,0:T(8,128)(2,1)S(1)} %bitcast.16), channel_id=1, source_target_pairs={{0,1},{1,0},{2,3},{3,2},{4,5},{5,4},{6,7},{7,6},{8,9},{9,8},{10,11... | collective-permute-start | bytes 1277960 | tf_op jit(solution)/shard_map/ppermute | solution.py:418

commit v8 on v7

--- a/solution.py
+++ b/solution.py
@@ -318,11 +318,14 @@
         copy.wait()
 
 
-def own_body(total_seeds, core_ref, own_ref, first_hbm, second_hbm, third_t_hbm, loss_ref, *scratch):
+def own_body(total_seeds, core_ref, own_ref, first_hbm, second_hbm, third_t_hbm, loss_hbm, loss_ref, leaving, *scratch):
     outs = (first_hbm, second_hbm, third_t_hbm)
     at = sum(out.shape[0] for out in outs)
     loss_ref[...] = jnp.sum(own_ref[at : at + 1, :].astype(f32), axis=1, keepdims=True) / total_seeds
+    copy = pltpu.make_async_copy(loss_ref, loss_hbm, leaving)
+    copy.start()
     columns(core_ref[0], own_ref, outs, scratch[:3], scratch[3])
+    copy.wait()
 
 
 def other_body(core_ref, other_ref, given_first, given_second, given_third_t, first_hbm, second_hbm, third_t_hbm, *scratch):
@@ -421,11 +424,11 @@
     sums = tuple(pltpu.HBM((n, hidden), f32) for n in sizes)
     *started, loss = call(
         functools.partial(own_body, total_seeds),
-        (*sums, shape((1, 1), f32)),
+        (*sums, pltpu.HBM((1, 1), f32)),
         [SMEM, VMEM],
-        scratch,
+        [pltpu.VMEM((1, 1), f32), pltpu.SemaphoreType.DMA, *scratch],
         8,
-        (FAR, FAR, FAR, VMEM),
+        FAR,
     )(core, own)
     grad_first, grad_second, grad_third_t = call(
         other_body, sums, [SMEM, VMEM, FAR, FAR, FAR], scratch, 8, FAR, {2: 0, 3: 1, 4: 2}

time: 87.5 us -> 87.4 us (level)
  transfers between devices with their start and end apart: 2 -> 2, of which waited for: 1 -> 2; matrix products, arithmetic and copies ran while one was open for 0% -> 0% of each run, Pallas kernels for 2% -> 2%
where the time goes in v8:
time: 87.4 us; the launch traced here: 87.1 us
  blocking collectives  69.2 us (79%)
  Pallas kernels  11.6 us (13%)
  starting transfers between devices  4.4 us (5%)
  waiting for transfers between devices  1.15 us (1%)
    all_to_all x4, blocking collectives, everywhere(): return lax.all_to_all(parts, axis, 0, 0, tiled=True)  69.2 us
    pallas_call x1, Pallas kernels, on_device(): call(functools.partial(step_body, total_seeds, 2), (pltpu.HBM((seeds, cla...  3.69 us
    ppermute x1, starting transfers between devices, on_device(): other = lax.ppermute(own, CORE, swap)  3.15 us
    pallas_call x1, Pallas kernels, on_device(): call(functools.partial(serve_body, capacity), (shape((groups, capacity, w...  2.6 us
    pallas_call x1, Pallas kernels, on_device(): call(functools.partial(request_body, capacity), (shape((groups, LANES), i...  2.3 us
  transfers between devices with their start and end apart: 2, of which 2 were waited for; matrix products, arithmetic and copies ran while one was open for 0% of the time, Pallas kernels for 2%

profile of v8, /device:TPU:1, one launch (start us, length us, event | category | flops | bytes accessed | tf_op | source)
XLA Modules:
  0.0 87.1 jit_solution(1190699460974253272)
XLA Ops:
  0.6 2.3 %shard_map.119 = (s32[128,128]{1,0:T(8,128)S(1)}, bf16[1024,128]{1,0:T(8,128)(2,1)S(1)}, f32[1024,128]{1,0:T(8,128)S(1)}, s32[32,1]{1,0:T(8,128)S(1)}, bf16[8192,2,128]{2,1,0:T(2,128)(2,1)S(1)}) custom-call(s32[1]{0:T(128)} %bitcast.core_ref, s32[32,32]{1,0:T(8,128)} %owner_hbm.1, s32[32,32]{1,0:T(8,128)} %local_hbm.1, f32[32,32]{1,0:T(8,128)} %weight_hbm.1, ...), custom_call_target="tpu_custom_call" | custom-call | tf_op jit(solution)/shard_map/pallas_call | solution.py:355
  2.9 20.7 %all_to_all.20 = s32[128,1,128]{2,1,0:T(1,128)S(1)} all-to-all(s32[128,1,128]{2,1,0:T(1,128)S(1)} %bitcast.21), channel_id=1, replica_groups=mesh['nodes_0'=4,'nodes_1'=4,'nodes_2'=4,'nodes_3'=2] {'nodes_0','nodes_..., dimensions={0} | all-to-all | bytes 131072 | tf_op jit(solution)/shard_map/all_to_all | solution.py:337
  23.6 2.6 %shard_map.120 = (bf16[128,16,128]{2,1,0:T(8,128)(2,1)S(1)}, bf16[128,512]{1,0:T(8,128)(2,1)S(1)}, bf16[512,512]{1,0:T(8,128)(2,1)S(1)}, bf16[172,512]{1,0:T(8,128)(2,1)S(1)}) custom-call(s32[128,128]{1,0:T(8,128)S(1)} %bitcast.20, bf16[8192,2,128]{2,1,0:T(2,128)(2,1)S(1)} %get-tuple-element.32.pairs_ref, bf16[128,512]{1,0:T(8,128)(2,1)} %first_hbm.1, ...), custom_call_target="tpu_custom_call" | custom-call | tf_op jit(solution)/shard_map/pallas_call | solution.py:379
  26.2 18.2 %all_to_all.21 = bf16[128,16,128]{2,1,0:T(8,128)(2,1)S(1)} all-to-all(bf16[128,16,128]{2,1,0:T(8,128)(2,1)S(1)} %get-tuple-element.33), channel_id=1, replica_groups=mesh['nodes_0'=4,'nodes_1'=4,'nodes_2'=4,'nodes_3'=2] {'nodes_0','nodes_..., dimensions={0} | all-to-all | bytes 1048576 | tf_op jit(solution)/shard_map/all_to_all | solution.py:337
  44.5 3.7 %shard_map.121 = (f32[32,172]{1,0:T(8,128)}, bf16[1664,128]{1,0:T(8,128)(2,1)S(1)}, f32[8,128]{1,0:T(8,128)S(1)}, bf16[1024,128]{1,0:T(8,128)(2,1)S(1)}, bf16[10...) custom-call(s32[1]{0:T(128)} %bitcast.core_ref, ...), custom_call_target="tpu_custom_call" | custom-call | tf_op jit(solution)/shard_map/pallas_call | solution.py:399
  48.2 1.2 %collective-permute-start = (bf16[1664,128]{1,0:T(8,128)(2,1)S(1)}, bf16[1664,128]{1,0:T(8,128)(2,1)S(1)}, u32[]{:S(2)}, u32[]{:S(2)}) collective-permute-start(bf16[1664,128]{1,0:T(8,128)(2,1)S(1)} %get-tuple-element.46), channel_id=1, source_target_pairs={{0,1},{1,0},{2,3},{3,2},{4,5},{5,4},{6,7},{7,6},{8,9},{9,8},{10,11... | collective-permute-start | bytes 1277960 | tf_op jit(solution)/shard_map/ppermute | solution.py:415
  49.4 0.7 shard_map.122
  50.1 0.7 collective-permute-done
  50.8 0.1 add_convert_fusion
  50.9 15.4 %all_to_all.22 = bf16[832,2,128]{2,1,0:T(2,128)(2,1)S(1)} all-to-all(bf16[832,2,128]{2,1,0:T(2,128)(2,1)S(1)} %bitcast.23), channel_id=1, replica_groups=mesh['nodes_0'=4,'nodes_1'=4,'nodes_2'=4,'nodes_3'=2] {'nodes_0','nodes_..., dimensions={0} | all-to-all | bytes 851968 | tf_op jit(solution)/shard_map/all_to_all | solution.py:337
  66.3 0.5 shard_map.123
  66.8 14.9 %all_to_all.23 = bf16[832,2,128]{2,1,0:T(2,128)(2,1)S(1)} all-to-all(bf16[832,2,128]{2,1,0:T(2,128)(2,1)S(1)} %bitcast.19), channel_id=1, replica_groups=mesh['nodes_0'=4,'nodes_1'=4,'nodes_2'=4,'nodes_3'=2] {'nodes_0','nodes_..., dimensions={0} | all-to-all | bytes 851968 | tf_op jit(solution)/shard_map/all_to_all | solution.py:337
  81.7 3.2 %collective-permute-start.1 = (bf16[1664,128]{1,0:T(8,128)(2,1)S(1)}, bf16[1664,128]{1,0:T(8,128)(2,1)S(1)}, u32[]{:S(2)}, u32[]{:S(2)}) collective-permute-start(bf16[1664,128]{1,0:T(8,128)(2,1)S(1)} %bitcast.16), channel_id=1, source_target_pairs={{0,1},{1,0},{2,3},{3,2},{4,5},{5,4},{6,7},{7,6},{8,9},{9,8},{10,11... | collective-permute-start | bytes 1277960 | tf_op jit(solution)/shard_map/ppermute | solution.py:421
  84.8 0.9 %shard_map.124 = (f32[128,512]{1,0:T(8,128)}, f32[512,512]{1,0:T(8,128)}, f32[172,512]{1,0:T(8,128)}, f32[1,1]{1,0:T(1,128)}) custom-call(s32[1]{0:T(128)} %bitcast.core_ref, bf16[1664,128]{1,0:T(8,128)(2,1)S(1)} %bitcast.17), custom_call_target="tpu_custom_call" | custom-call | tf_op jit(solution)/shard_map/pallas_call | solution.py:425
  85.7 0.5 collective-permute-done.1.other_ref
  86.2 0.9 %shard_map.125 = (f32[128,512]{1,0:T(8,128)}, f32[512,512]{1,0:T(8,128)}, f32[172,512]{1,0:T(8,128)}) custom-call(s32[1]{0:T(128)} %bitcast.core_ref, bf16[1664,128]{1,0:T(8,128)(2,1)S(1)} %collective-permute-done.1.other_ref, f32[128,512]{1,0:T(8,128)} %get-tuple-element.49.given_first, ...), custom_call_target="tpu_custom_call", output_to_operand_aliasing={{0}: (2, {}), {1}: (3, {}), {2}: (4, {})} | custom-call | tf_op jit(solution)/shard_map/pallas_call | solution.py:433
Async XLA Ops:
  48.2 2.6 %collective-permute-start = (bf16[1664,128]{1,0:T(8,128)(2,1)S(1)}, bf16[1664,128]{1,0:T(8,128)(2,1)S(1)}, u32[]{:S(2)}, u32[]{:S(2)}) collective-permute-start(bf16[1664,128]{1,0:T(8,128)(2,1)S(1)} %get-tuple-element.46), channel_id=1, source_target_pairs={{0,1},{1,0},{2,3},{3,2},{4,5},{5,4},{6,7},{7,6},{8,9},{9,8},{10,11... | collective-permute-start | bytes 1277960 | tf_op jit(solution)/shard_map/ppermute | solution.py:415
  81.7 4.5 %collective-permute-start.1 = (bf16[1664,128]{1,0:T(8,128)(2,1)S(1)}, bf16[1664,128]{1,0:T(8,128)(2,1)S(1)}, u32[]{:S(2)}, u32[]{:S(2)}) collective-permute-start(bf16[1664,128]{1,0:T(8,128)(2,1)S(1)} %bitcast.16), channel_id=1, source_target_pairs={{0,1},{1,0},{2,3},{3,2},{4,5},{5,4},{6,7},{7,6},{8,9},{9,8},{10,11... | collective-permute-start | bytes 1277960 | tf_op jit(solution)/shard_map/ppermute | solution.py:421

commit v9 on v8

--- a/solution.py
+++ b/solution.py
@@ -77,12 +77,12 @@
     arrivals,
 ):
     del core_ref
+    pairs = pltpu.make_async_copy(pairs_hbm, pairs_ref, arrivals.at[4])
+    pairs.start()
     small = zip((owner_hbm, local_hbm, weight_hbm, labels_hbm), (owner_ref, local_ref, weight_ref, labels_ref))
     copies = [pltpu.make_async_copy(source, target, arrivals.at[i]) for i, (source, target) in enumerate(small)]
     for copy in copies:
         copy.start()
-    pairs = pltpu.make_async_copy(pairs_hbm, pairs_ref, arrivals.at[len(copies)])
-    pairs.start()
     for copy in copies:
         copy.wait()
     groups = table_ref.shape[0]

time: 87.4 us -> 88.2 us (level)
  Pallas kernels: 11.6 us -> 12.5 us
where the time goes in v9:
time: 88.2 us; the launch traced here: 88 us
  blocking collectives  69.2 us (78%)
  Pallas kernels  12.5 us (14%)
  starting transfers between devices  4.4 us (5%)
  waiting for transfers between devices  1.15 us (1%)
    all_to_all x4, blocking collectives, everywhere(): return lax.all_to_all(parts, axis, 0, 0, tiled=True)  69.2 us
    pallas_call x1, Pallas kernels, on_device(): call(functools.partial(step_body, total_seeds, 2), (pltpu.HBM((seeds, cla...  3.69 us
    pallas_call x1, Pallas kernels, on_device(): call(functools.partial(request_body, capacity), (shape((groups, LANES), i...  3.18 us
    ppermute x1, starting transfers between devices, on_device(): other = lax.ppermute(own, CORE, swap)  3.15 us
    pallas_call x1, Pallas kernels, on_device(): call(functools.partial(serve_body, capacity), (shape((groups, capacity, w...  2.59 us
  transfers between devices with their start and end apart: 2, of which 2 were waited for; matrix products, arithmetic and copies ran while one was open for 0% of the time, Pallas kernels for 2%

profile of v9, /device:TPU:1, one launch (start us, length us, event | category | flops | bytes accessed | tf_op | source)
XLA Modules:
  0.0 88.0 jit_solution(15677347378029399395)
XLA Ops:
  0.6 3.2 %shard_map.119 = (s32[128,128]{1,0:T(8,128)S(1)}, bf16[1024,128]{1,0:T(8,128)(2,1)S(1)}, f32[1024,128]{1,0:T(8,128)S(1)}, s32[32,1]{1,0:T(8,128)S(1)}, bf16[8192,2,128]{2,1,0:T(2,128)(2,1)S(1)}) custom-call(s32[1]{0:T(128)} %bitcast.core_ref, s32[32,32]{1,0:T(8,128)} %owner_hbm.1, s32[32,32]{1,0:T(8,128)} %local_hbm.1, f32[32,32]{1,0:T(8,128)} %weight_hbm.1, ...), custom_call_target="tpu_custom_call" | custom-call | tf_op jit(solution)/shard_map/pallas_call | solution.py:355
  3.8 20.7 %all_to_all.20 = s32[128,1,128]{2,1,0:T(1,128)S(1)} all-to-all(s32[128,1,128]{2,1,0:T(1,128)S(1)} %bitcast.21), channel_id=1, replica_groups=mesh['nodes_0'=4,'nodes_1'=4,'nodes_2'=4,'nodes_3'=2] {'nodes_0','nodes_..., dimensions={0} | all-to-all | bytes 131072 | tf_op jit(solution)/shard_map/all_to_all | solution.py:337
  24.5 2.6 %shard_map.120 = (bf16[128,16,128]{2,1,0:T(8,128)(2,1)S(1)}, bf16[128,512]{1,0:T(8,128)(2,1)S(1)}, bf16[512,512]{1,0:T(8,128)(2,1)S(1)}, bf16[172,512]{1,0:T(8,128)(2,1)S(1)}) custom-call(s32[128,128]{1,0:T(8,128)S(1)} %bitcast.20, bf16[8192,2,128]{2,1,0:T(2,128)(2,1)S(1)} %get-tuple-element.32.pairs_ref, bf16[128,512]{1,0:T(8,128)(2,1)} %first_hbm.1, ...), custom_call_target="tpu_custom_call" | custom-call | tf_op jit(solution)/shard_map/pallas_call | solution.py:379
  27.1 18.3 %all_to_all.21 = bf16[128,16,128]{2,1,0:T(8,128)(2,1)S(1)} all-to-all(bf16[128,16,128]{2,1,0:T(8,128)(2,1)S(1)} %get-tuple-element.33), channel_id=1, replica_groups=mesh['nodes_0'=4,'nodes_1'=4,'nodes_2'=4,'nodes_3'=2] {'nodes_0','nodes_..., dimensions={0} | all-to-all | bytes 1048576 | tf_op jit(solution)/shard_map/all_to_all | solution.py:337
  45.4 3.7 %shard_map.121 = (f32[32,172]{1,0:T(8,128)}, bf16[1664,128]{1,0:T(8,128)(2,1)S(1)}, f32[8,128]{1,0:T(8,128)S(1)}, bf16[1024,128]{1,0:T(8,128)(2,1)S(1)}, bf16[10...) custom-call(s32[1]{0:T(128)} %bitcast.core_ref, ...), custom_call_target="tpu_custom_call" | custom-call | tf_op jit(solution)/shard_map/pallas_call | solution.py:399
  49.1 1.2 %collective-permute-start = (bf16[1664,128]{1,0:T(8,128)(2,1)S(1)}, bf16[1664,128]{1,0:T(8,128)(2,1)S(1)}, u32[]{:S(2)}, u32[]{:S(2)}) collective-permute-start(bf16[1664,128]{1,0:T(8,128)(2,1)S(1)} %get-tuple-element.46), channel_id=1, source_target_pairs={{0,1},{1,0},{2,3},{3,2},{4,5},{5,4},{6,7},{7,6},{8,9},{9,8},{10,11... | collective-permute-start | bytes 1277960 | tf_op jit(solution)/shard_map/ppermute | solution.py:415
  50.3 0.7 shard_map.122
  51.0 0.7 collective-permute-done
  51.7 0.1 add_convert_fusion
  51.8 15.4 %all_to_all.22 = bf16[832,2,128]{2,1,0:T(2,128)(2,1)S(1)} all-to-all(bf16[832,2,128]{2,1,0:T(2,128)(2,1)S(1)} %bitcast.23), channel_id=1, replica_groups=mesh['nodes_0'=4,'nodes_1'=4,'nodes_2'=4,'nodes_3'=2] {'nodes_0','nodes_..., dimensions={0} | all-to-all | bytes 851968 | tf_op jit(solution)/shard_map/all_to_all | solution.py:337
  67.2 0.5 shard_map.123
  67.7 14.9 %all_to_all.23 = bf16[832,2,128]{2,1,0:T(2,128)(2,1)S(1)} all-to-all(bf16[832,2,128]{2,1,0:T(2,128)(2,1)S(1)} %bitcast.19), channel_id=1, replica_groups=mesh['nodes_0'=4,'nodes_1'=4,'nodes_2'=4,'nodes_3'=2] {'nodes_0','nodes_..., dimensions={0} | all-to-all | bytes 851968 | tf_op jit(solution)/shard_map/all_to_all | solution.py:337
  82.5 3.2 %collective-permute-start.1 = (bf16[1664,128]{1,0:T(8,128)(2,1)S(1)}, bf16[1664,128]{1,0:T(8,128)(2,1)S(1)}, u32[]{:S(2)}, u32[]{:S(2)}) collective-permute-start(bf16[1664,128]{1,0:T(8,128)(2,1)S(1)} %bitcast.16), channel_id=1, source_target_pairs={{0,1},{1,0},{2,3},{3,2},{4,5},{5,4},{6,7},{7,6},{8,9},{9,8},{10,11... | collective-permute-start | bytes 1277960 | tf_op jit(solution)/shard_map/ppermute | solution.py:421
  85.7 0.9 %shard_map.124 = (f32[128,512]{1,0:T(8,128)}, f32[512,512]{1,0:T(8,128)}, f32[172,512]{1,0:T(8,128)}, f32[1,1]{1,0:T(1,128)}) custom-call(s32[1]{0:T(128)} %bitcast.core_ref, bf16[1664,128]{1,0:T(8,128)(2,1)S(1)} %bitcast.17), custom_call_target="tpu_custom_call" | custom-call | tf_op jit(solution)/shard_map/pallas_call | solution.py:425
  86.6 0.5 collective-permute-done.1.other_ref
  87.1 0.9 %shard_map.125 = (f32[128,512]{1,0:T(8,128)}, f32[512,512]{1,0:T(8,128)}, f32[172,512]{1,0:T(8,128)}) custom-call(s32[1]{0:T(128)} %bitcast.core_ref, bf16[1664,128]{1,0:T(8,128)(2,1)S(1)} %collective-permute-done.1.other_ref, f32[128,512]{1,0:T(8,128)} %get-tuple-element.49.given_first, ...), custom_call_target="tpu_custom_call", output_to_operand_aliasing={{0}: (2, {}), {1}: (3, {}), {2}: (4, {})} | custom-call | tf_op jit(solution)/shard_map/pallas_call | solution.py:433
Async XLA Ops:
  49.1 2.6 %collective-permute-start = (bf16[1664,128]{1,0:T(8,128)(2,1)S(1)}, bf16[1664,128]{1,0:T(8,128)(2,1)S(1)}, u32[]{:S(2)}, u32[]{:S(2)}) collective-permute-start(bf16[1664,128]{1,0:T(8,128)(2,1)S(1)} %get-tuple-element.46), channel_id=1, source_target_pairs={{0,1},{1,0},{2,3},{3,2},{4,5},{5,4},{6,7},{7,6},{8,9},{9,8},{10,11... | collective-permute-start | bytes 1277960 | tf_op jit(solution)/shard_map/ppermute | solution.py:415
  82.5 4.5 %collective-permute-start.1 = (bf16[1664,128]{1,0:T(8,128)(2,1)S(1)}, bf16[1664,128]{1,0:T(8,128)(2,1)S(1)}, u32[]{:S(2)}, u32[]{:S(2)}) collective-permute-start(bf16[1664,128]{1,0:T(8,128)(2,1)S(1)} %bitcast.16), channel_id=1, source_target_pairs={{0,1},{1,0},{2,3},{3,2},{4,5},{5,4},{6,7},{7,6},{8,9},{9,8},{10,11... | collective-permute-start | bytes 1277960 | tf_op jit(solution)/shard_map/ppermute | solution.py:421
